TPU v7x, 32 devices: a whole 2x2x4 slice. The times are simulated.
32 devices in a mesh: mom: 4 (over y, core), pair: 8 (over z, x).
Axes of the slice: x: 2, y: 2, z: 4, core: 2. Of those that a mesh axis runs over, the one named last changes fastest.
Arguments:
- blocks: bfloat16 [4, 16, 1024, 1024], P('mom', None, 'pair'), may hold values from -1.078125 to 1.078125
- left_ids: int32 [4, 24], P('mom', 'pair'), may hold values from 0 to 15
- right_ids: int32 [4, 24], P('mom', 'pair'), may hold values from 0 to 15
- slice_ids: int32 [4, 24], P('mom', 'pair'), may hold values from 0 to 1
- weight_ids: int32 [4, 24], P('mom', 'pair'), may hold values from 0 to 7
- counts: int32 [4, 8], P('mom', 'pair'), may hold values from 1 to 3, 16 in all within a row
- subduction: float32 [8], replicated, may hold values from -1 to 1
Outputs:
- operator: float32 [4, 1024, 2, 1024], P('mom', 'pair')
Inputs may be any that keep to these rules, and one draw needn't show every extreme that they name: Each row of counts sums to exactly 16.
All inputs are finite; a program needn't handle non-finite values. No bound on the sum of `counts` on one device may be relied on, other than what follows from the above.
Results may differ from a plain program's by a relative error of at most 0.0029.
Values may be sent and summed in bfloat16 or wider, within the bound.
No kernel may reach another device: no remote copies, remote signals or barrier semaphores. Data moves between devices by JAX's collectives and lax.ppermute only.
A program may use at most 128 MiB of HBM per device.

v0:
```python
import functools

import jax
import jax.numpy as jnp
from jax import lax
from jax.experimental import pallas as pl
from jax.experimental.pallas import tpu as pltpu
from jax.sharding import PartitionSpec as P

SLICES = 2
SUBLANES = 16
LANES = 128
ROW_PARTS = (6, 2)
COLUMN_PARTS = (3, 1)


def cut(length, unit, parts):
    units, total = length // unit, sum(parts)
    edges = [units * sum(parts[:part]) // total for part in range(len(parts) + 1)]
    return [(lo * unit, (hi - lo) * unit) for lo, hi in zip(edges, edges[1:]) if hi > lo]


def swap(value, axis, apart):
    size = lax.axis_size(axis)
    return lax.ppermute(value, axis, [(i, i ^ apart) for i in range(size)])


def spec(space=pltpu.VMEM):
    return pl.BlockSpec(memory_space=space)


def plan_kernel(families, metas, subduction, left_list, weight_list, offsets, cursor):
    lists, keys = metas.shape[0], SLICES * families
    per_list = (metas.shape[1] - 1) // 4
    dump = lists * per_list

    def clear(q, carry):
        cursor[q] = 0
        return carry

    lax.fori_loop(0, keys + 1, clear, 0)
    slots = []
    for i in range(lists):
        count = metas[i, 4 * per_list]
        for k in range(per_list):
            live = k < count
            key = metas[i, 2 * per_list + k] * families + metas[i, per_list + k]
            key = jnp.where(live, key, keys)
            slots.append((live, key, metas[i, k], metas[i, 3 * per_list + k]))
    for _, key, _, _ in slots:
        cursor[key] = cursor[key] + 1

    def place(q, total):
        here = cursor[q]
        offsets[q] = total
        cursor[q] = total
        return total + here

    offsets[keys] = lax.fori_loop(0, keys, place, 0)
    cursor[keys] = 0
    for live, key, left, weight in slots:
        at = cursor[key]
        cursor[key] = at + 1
        at = jnp.where(live, at, dump)
        left_list[at] = left
        weight_list[at] = subduction[weight]


def plan(metas, subduction, families):
    slots = metas.shape[0] * (metas.shape[1] - 1) // 4
    keys = SLICES * families
    return pl.pallas_call(
        functools.partial(plan_kernel, families),
        out_shape=(
            jax.ShapeDtypeStruct((slots + 1,), jnp.int32),
            jax.ShapeDtypeStruct((slots + 1,), jnp.float32),
            jax.ShapeDtypeStruct((keys + 1,), jnp.int32),
        ),
        in_specs=[spec(pltpu.SMEM)] * 2,
        out_specs=(spec(pltpu.SMEM),) * 3,
        scratch_shapes=[pltpu.SMEM((keys + 1,), jnp.int32)],
        name="plan",
    )(metas, subduction)


def pack_kernel(start, rows, width, me, own, *refs):
    outs, sems = refs[:-1], refs[-1]
    copies = []
    for group, out in enumerate(outs):
        for half in range(2):
            column = pl.multiple_of((me[0] ^ (2 * group + half)) * width, width)
            source = own.at[:, pl.ds(start, rows), pl.ds(column, width)]
            sem = sems.at[2 * group + half]
            copies.append(pltpu.make_async_copy(source, out.at[half], sem))
    for copy in copies:
        copy.start()
    for copy in copies:
        copy.wait()


def pack(own, me, start, rows, width, groups):
    families = own.shape[0]
    if width % LANES:

        def columns(offset):
            at = (0, start, (me[0] ^ offset) * width)
            return lax.dynamic_slice(own, at, (families, rows, width))

        return [
            jnp.stack([columns(2 * group), columns(2 * group + 1)]) for group in range(groups)
        ]
    piece = jax.ShapeDtypeStruct((2, families, rows, width), own.dtype)
    return pl.pallas_call(
        functools.partial(pack_kernel, start, rows, width),
        out_shape=[piece] * groups,
        in_specs=[spec(pltpu.SMEM), spec(pl.ANY)],
        out_specs=[spec()] * groups,
        scratch_shapes=[pltpu.SemaphoreType.DMA((2 * groups,))],
        cost_estimate=pl.CostEstimate(
            flops=0, transcendentals=0, bytes_accessed=4 * groups * piece.size
        ),
        name="pack",
    )(me, own)


def slab_kernel(start, own, out, sem):
    copy = pltpu.make_async_copy(own.at[:, :, pl.ds(start, out.shape[2])], out, sem)
    copy.start()
    copy.wait()


def slab(own, start, columns):
    shape = own.shape[:2] + (columns,)
    return pl.pallas_call(
        functools.partial(slab_kernel, start),
        out_shape=jax.ShapeDtypeStruct(shape, own.dtype),
        in_specs=[spec(pl.ANY)],
        out_specs=spec(),
        scratch_shapes=[pltpu.SemaphoreType.DMA],
        cost_estimate=pl.CostEstimate(
            flops=0, transcendentals=0, bytes_accessed=4 * own.size * columns // own.shape[2]
        ),
        name="slab",
    )(own)


def combine_rows(table, lefts, combined):
    left_list, weight_list, offsets = table
    _, families, rows, width = lefts[0].shape
    step = min(rows, 2 * SUBLANES)

    def combine(q, carry):
        t, b = q // families, q % families
        first, last = offsets[q], offsets[q + 1]
        for top in range(0, rows, step):
            here = min(step, rows - top)

            def add(s, sums):
                left, weight = left_list[s], weight_list[s]
                pieces = [
                    ref[half, left, top : top + here, :].astype(jnp.float32)
                    for ref in lefts
                    for half in range(2)
                ]
                return tuple(total + weight * piece for total, piece in zip(sums, pieces))

            zeros = (jnp.zeros((here, width), jnp.float32),) * (2 * len(lefts))
            sums = lax.fori_loop(first, last, add, zeros)
            for i, total in enumerate(sums):
                at = (t * len(lefts) + i // 2) * rows + top
                start = (i % 2 * families + b) * width
                if not isinstance(q, int):
                    at = pl.multiple_of(at, SUBLANES)
                    start = pl.multiple_of(start, width)
                value = total.astype(combined.dtype)
                combined[pl.ds(at, here), pl.ds(start, width)] = value
        return carry

    if width % LANES:
        for q in range(SLICES * families):
            combine(q, 0)
    else:
        lax.fori_loop(0, SLICES * families, combine, 0)


def combine_kernel(*refs):
    combine_rows(refs[:3], refs[3:-1], refs[-1])


def combined_shape(lefts):
    _, families, rows, width = lefts[0].shape
    return SLICES * len(lefts) * rows, 2 * families * width


def combine(table, lefts):
    shape = combined_shape(lefts)
    size = shape[0] * shape[1]
    return pl.pallas_call(
        combine_kernel,
        out_shape=jax.ShapeDtypeStruct(shape, jnp.bfloat16),
        in_specs=[spec(pltpu.SMEM)] * 3 + [spec()] * len(lefts),
        out_specs=spec(),
        cost_estimate=pl.CostEstimate(
            flops=4 * size, transcendentals=0, bytes_accessed=3 * size
        ),
        name="combine",
    )(*table, *lefts)


def product_kernel(groups, chunks, edges, *refs):
    combined, near = refs[: len(chunks)], refs[len(chunks)]
    far, (send, keep) = refs[len(chunks) + 1 : -2], refs[-2:]
    families, width, tile = near.shape
    depth, step = families * width, pl.program_id(0)

    def multiply(other):
        top = 0
        for chunk in combined:
            part = jnp.dot(
                chunk[:, :depth],
                near[...].reshape(depth, tile),
                preferred_element_type=jnp.float32,
            ) + jnp.dot(
                chunk[:, depth:],
                other[...].reshape(depth, tile),
                preferred_element_type=jnp.float32,
            )
            rows = chunk.shape[0] // (SLICES * groups)
            for i in range(SLICES * groups):
                t, group = divmod(i, groups)
                piece = part[i * rows : (i + 1) * rows]
                if group % 2:
                    send[group // 2, t, top : top + rows] = piece.astype(send.dtype)
                else:
                    keep[group // 2, t, top : top + rows] = piece
            top += rows

    if len(far) == 1:
        multiply(far[0])
    else:
        for other, (lo, hi) in zip(far, edges):
            pl.when((step >= lo) & (step < hi))(functools.partial(multiply, other))


def product(combined, near, far, start, groups):
    families, width, _ = near.shape
    rows = [chunk.shape[0] // (SLICES * groups) for chunk in combined]
    columns = sum(part.shape[2] for part in far)
    tile = 2 * LANES
    edges, at = [], 0
    for part in far:
        edges.append((at, at + part.shape[2] // tile))
        at = edges[-1][1]

    def place(lo, hi):
        return lambda i: (0, 0, jnp.clip(i - lo, 0, hi - lo - 1))

    shape = (groups // 2, SLICES, sum(rows), columns)
    block = pl.BlockSpec((groups // 2, SLICES, sum(rows), tile), lambda i: (0, 0, 0, i))
    return pl.pallas_call(
        functools.partial(product_kernel, groups, rows, edges),
        grid=(columns // tile,),
        out_shape=(
            jax.ShapeDtypeStruct(shape, jnp.bfloat16),
            jax.ShapeDtypeStruct(shape, jnp.float32),
        ),
        in_specs=[
            pl.BlockSpec(chunk.shape, lambda i: (0, 0), pipeline_mode=pl.Buffered(1))
            for chunk in combined
        ]
        + [pl.BlockSpec((families, width, tile), lambda i: (0, 0, start // tile + i))]
        + [pl.BlockSpec((families, width, tile), place(lo, hi)) for lo, hi in edges],
        out_specs=(block, block),
        compiler_params=pltpu.CompilerParams(vmem_limit_bytes=48 << 20),
        cost_estimate=pl.CostEstimate(
            flops=2 * sum(chunk.size for chunk in combined) * columns,
            transcendentals=0,
            bytes_accessed=sum(2 * chunk.size for chunk in combined)
            + 4 * families * width * columns,
        ),
        name="product",
    )(*combined, near, *far)


def halve_kernel(keep, came, send, kept):
    for i in range(send.shape[0]):
        kept[i] = keep[2 * i] + came[2 * i].astype(jnp.float32)
        total = keep[2 * i + 1] + came[2 * i + 1].astype(jnp.float32)
        send[i] = total.astype(send.dtype)


def halve(keep, came):
    shape = (keep.shape[0] // 2,) + keep.shape[1:]
    return pl.pallas_call(
        halve_kernel,
        out_shape=(
            jax.ShapeDtypeStruct(shape, jnp.bfloat16),
            jax.ShapeDtypeStruct(shape, jnp.float32),
        ),
        in_specs=[spec()] * 2,
        out_specs=(spec(), spec()),
        cost_estimate=pl.CostEstimate(
            flops=keep.size, transcendentals=0, bytes_accessed=9 * keep.size
        ),
        name="halve",
    )(keep, came)


def finish_kernel(row, column, keep, came, *refs):
    out, buffer, sem = refs[-3:]
    rows, _, columns = buffer.shape
    for t in range(SLICES):
        buffer[:, t, :] = keep[0, t] + came[0, t].astype(jnp.float32)
    target = out.at[pl.ds(row, rows), :, pl.ds(column, columns)]
    copy = pltpu.make_async_copy(buffer, target, sem)
    copy.start()
    copy.wait()


def finish(keep, came, row, column, rows, order, result):
    here, columns = keep.shape[2:]
    before = [] if result is None else [result]
    return pl.pallas_call(
        functools.partial(finish_kernel, row, column),
        out_shape=jax.ShapeDtypeStruct((rows, SLICES, order), jnp.float32),
        in_specs=[spec()] * 2 + [spec(pl.ANY)] * len(before),
        out_specs=spec(pl.ANY),
        scratch_shapes=[
            pltpu.VMEM((here, SLICES, columns), jnp.float32),
            pltpu.SemaphoreType.DMA,
        ],
        input_output_aliases={2: 0} if before else {},
        cost_estimate=pl.CostEstimate(
            flops=keep.size, transcendentals=0, bytes_accessed=10 * keep.size
        ),
        name="finish",
    )(keep, came, *before)


def body(blocks, left_ids, right_ids, slice_ids, weight_ids, counts, subduction):
    own = blocks[0]
    families, rows, order = own.shape
    devices = lax.axis_size("pair")
    groups, width = devices // 2, order // devices
    me = lax.axis_index("pair").reshape(1)
    meta = jnp.concatenate([left_ids, right_ids, slice_ids, weight_ids, counts], axis=1)
    metas = lax.all_to_all(
        jnp.broadcast_to(meta, (devices, meta.shape[1])), "pair", 0, 0, tiled=True
    )
    row_cuts = cut(rows, SUBLANES, ROW_PARTS)
    column_cuts = cut(order, 2 * LANES, COLUMN_PARTS)
    arrived, far = [], []
    for i in range(max(len(row_cuts), len(column_cuts))):
        if i < len(row_cuts):
            pieces = pack(own, me, *row_cuts[i], width, groups)
            moved = [swap(pieces[group], "pair", 2 * group) for group in range(groups - 1, 0, -1)]
            arrived.append([pieces[0]] + moved[::-1])
        if i < len(column_cuts):
            part = own
            if len(column_cuts) > 1:
                part = slab(own, *column_cuts[i])
            far.append(swap(part, ("mom", "pair"), devices + 1))
    near = swap(own, "mom", 1)
    table = plan(metas, subduction, families)
    last, columns = len(row_cuts) - 1, range(len(column_cuts))
    jobs = [(range(last), [j]) for j in columns] + [([last], columns)]
    combined = [combine(table, lefts) for lefts in arrived]
    result = None
    for chunks, parts in jobs:
        row, column = row_cuts[chunks[0]][0], column_cuts[parts[0]][0]
        send, keep = product(
            [combined[i] for i in chunks], near, [far[j] for j in parts], column, groups
        )
        apart = 1
        while 2 * apart < groups:
            came = swap(send, "pair", 2 * apart)
            send, keep = halve(keep, came)
            apart *= 2
        came = swap(send, "pair", 2 * apart)
        result = finish(keep, came, row, column, rows, order, result)
    return result.reshape((1,) + result.shape)


def solution(mesh):
    return jax.shard_map(
        body,
        mesh=mesh,
        in_specs=(
            P("mom", None, "pair", None),
            P("mom", "pair"),
            P("mom", "pair"),
            P("mom", "pair"),
            P("mom", "pair"),
            P("mom", "pair"),
            P(),
        ),
        out_specs=P("mom", "pair", None, None),
        check_vma=False,
    )
```

profile of v0, /device:TPU:0, one launch (start us, length us, event | category | flops | bytes accessed | tf_op | source)
XLA Modules:
  0.0 180.1 jit_solution(1765403743356005344)
XLA Ops:
  0.0 0.5 collective-permute-start.3
  0.5 3.5 %slab.2 = bf16[16,128,768]{2,1,0:T(8,128)(2,1)} custom-call(bf16[16,128,1024]{2,1,0:T(8,128)(2,1)} %bitcast.6), custom_call_target="tpu_custom_call" | custom-call | bytes 6291456 | tf_op jit(solution)/shard_map/slab/pallas_call | solution.py:134
  4.0 2.7 %collective-permute-start.4 = (bf16[16,128,768]{2,1,0:T(8,128)(2,1)}, bf16[16,128,768]{2,1,0:T(8,128)(2,1)}, u32[]{:S(2)}, u32[]{:S(2)}) collective-permute-start(bf16[16,128,768]{2,1,0:T(8,128)(2,1)} %slab.2), channel_id=1, source_target_pairs={{0,9},{1,8},{2,11},{3,10},{4,13},{5,12},{6,15},{7,14},{8,1},{9,0},... | collective-permute-start | bytes 9437192 | tf_op jit(solution)/shard_map/ppermute | solution.py:25
  6.7 3.7 %pack.3 = (bf16[2,16,96,128]{3,2,1,0:T(8,128)(2,1)}, bf16[2,16,96,128]{3,2,1,0:T(8,128)(2,1)}, bf16[2,16,96,128]{3,2,1,0:T(8,128)(2,1)}, bf16[2,16,96,128]{3,2,1,0:T(8,128)(2,1)}) custom-call(s32[1]{0:T(128)} %bitcast.2.me, bf16[16,128,1024]{2,1,0:T(8,128)(2,1)} %bitcast.7), custom_call_target="tpu_custom_call" | custom-call | bytes 6291456 | tf_op jit(solution)/shard_map/pack/pallas_call | solution.py:113
  10.4 0.0 copy-start.15
  10.4 0.0 copy-start.16
  10.4 0.0 copy-start.17
  10.4 0.0 copy-start.18
  10.4 3.7 %collective-permute-start.10 = (bf16[2,16,96,128]{3,2,1,0:T(8,128)(2,1)}, bf16[2,16,96,128]{3,2,1,0:T(8,128)(2,1)S(1)}, u32[]{:S(2)}, u32[]{:S(2)}) collective-permute-start(bf16[2,16,96,128]{3,2,1,0:T(8,128)(2,1)} %get-tuple-element.42), channel_id=1, source_target_pairs={{0,6},{1,7},{2,4},{3,5},{4,2},{5,3},{6,0},{7,1},{8,14},{9,15},{10,... | collective-permute-start | bytes 2359304 | tf_op jit(solution)/shard_map/ppermute | solution.py:25
  14.1 0.0 collective-permute-start.8
  14.1 0.8 collective-permute-start.9
  14.9 2.2 %slab.3 = bf16[16,128,256]{2,1,0:T(8,128)(2,1)} custom-call(bf16[16,128,1024]{2,1,0:T(8,128)(2,1)} %bitcast.8), custom_call_target="tpu_custom_call" | custom-call | bytes 2097152 | tf_op jit(solution)/shard_map/slab/pallas_call | solution.py:134
  17.1 15.9 %collective-permute-done.10.refs_6_ = bf16[2,16,96,128]{3,2,1,0:T(8,128)(2,1)S(1)} collective-permute-done((bf16[2,16,96,128]{3,2,1,0:T(8,128)(2,1)}, bf16[2,16,96,128]{3,2,1,0:T(8,128)(2,1)S(1)}, u32[]{:S(2)}, u32[]{:S(2)}) %collective-permute-start.10) | collective-permute-done | bytes 786464 | tf_op jit(solution)/shard_map/ppermute | solution.py:25
  33.0 0.0 collective-permute-start.5
  33.7 0.1 concatenate.5
  33.8 0.6 broadcast_in_dim.2
  34.4 18.8 %all-to-all-start = ((s32[8,1,13]{2,1,0:T(1,128)}), s32[8,1,13]{2,1,0:T(1,128)S(1)}, u32[]{:S(2)}, u32[]{:S(2)}) async-start(s32[8,1,13]{2,1,0:T(1,128)} %broadcast_in_dim.2), calls=%async_computation | async-start | bytes 8192 | tf_op jit(solution)/shard_map/all_to_all | solution.py:347
  53.2 2.4 %pack.2 = (bf16[2,16,32,128]{3,2,1,0:T(8,128)(2,1)}, bf16[2,16,32,128]{3,2,1,0:T(8,128)(2,1)}, bf16[2,16,32,128]{3,2,1,0:T(8,128)(2,1)}, bf16[2,16,32,128]{3,2,1,0:T(8,128)(2,1)}) custom-call(s32[1]{0:T(128)} %bitcast.2.me, bf16[16,128,1024]{2,1,0:T(8,128)(2,1)} %bitcast.9), custom_call_target="tpu_custom_call" | custom-call | bytes 2097152 | tf_op jit(solution)/shard_map/pack/pallas_call | solution.py:113
  55.6 42.4 %all-to-all-done = s32[8,1,13]{2,1,0:T(1,128)S(1)} async-done(((s32[8,1,13]{2,1,0:T(1,128)}), s32[8,1,13]{2,1,0:T(1,128)S(1)}, u32[]{:S(2)}, u32[]{:S(2)}) %all-to-all-start) | async-done | bytes 448 | tf_op jit(solution)/shard_map/all_to_all | solution.py:347
  98.1 0.6 copy-done.14
  98.6 1.9 %plan.1 = (s32[25]{0:T(128)}, f32[25]{0:T(128)}, s32[33]{0:T(128)}) custom-call(s32[8,13]{1,0:T(8,128)} %bitcast.10, f32[8]{0:T(128)} %subduction.1), custom_call_target="tpu_custom_call" | custom-call | tf_op jit(solution)/shard_map/plan/pallas_call | solution.py:72
  100.6 0.0 collective-permute-done.8.refs_4_
  100.6 1.8 collective-permute-start
  102.4 0.0 collective-permute-done.9.refs_5_
  102.4 2.6 %collective-permute-start.1 = (bf16[2,16,32,128]{3,2,1,0:T(8,128)(2,1)}, bf16[2,16,32,128]{3,2,1,0:T(8,128)(2,1)}, u32[]{:S(2)}, u32[]{:S(2)}) collective-permute-start(bf16[2,16,32,128]{3,2,1,0:T(8,128)(2,1)} %get-tuple-element.33), channel_id=1, source_target_pairs={{0,4},{1,5},{2,6},{3,7},{4,0},{5,1},{6,2},{7,3},{8,12},{9,13},{10,... | collective-permute-start | bytes 786440 | tf_op jit(solution)/shard_map/ppermute | solution.py:25
  105.0 8.0 %combine.3.refs_0_ = bf16[768,4096]{1,0:T(8,128)(2,1)} custom-call(s32[25]{0:T(128)} %get-tuple-element.28.refs_0_, f32[25]{0:T(128)} %get-tuple-element.29.refs_1_, s32[33]{0:T(128)} %get-tuple-element.30.refs_2_, bf16[2,16,96,128]{3,2,1,0:T(8,128)(2,1)} %get-tuple-element.39.refs_3_, bf16[2,16,96,128]{3,2,1,0:T(8,128)(2,1)} %copy-done.5, ...), custom_call_target="tpu_custom_call" | custom-call | flops 12582912 | bytes 9437184 | tf_op jit(solution)/shard_map/combine/pallas_call | solution.py:198
  113.0 0.0 collective-permute-done.4.refs_2_
  113.0 0.8 collective-permute-start.2
  113.8 0.0 collective-permute-done.3.refs_1_
  113.8 9.0 %product.5 = (bf16[2,2,96,768]{3,2,1,0:T(8,128)(2,1)S(1)}, f32[2,2,96,768]{3,2,1,0:T(8,128)S(1)}) custom-call(bf16[768,4096]{1,0:T(8,128)(2,1)} %combine.3.refs_0_, bf16[16,128,1024]{2,1,0:T(8,128)(2,1)} %collective-permute-done.3.refs_1_, bf16[16,128,768]{2,1,0:T(8,128)(2,1)} %collective-permute-done.4.refs_2_), custom_call_target="tpu_custom_call" | custom-call | flops 4831838208 | bytes 12582912 | tf_op jit(solution)/shard_map/product/pallas_call | solution.py:260
  122.8 1.0 copy-done.1
  123.9 0.7 collective-permute-start.13
  124.5 0.0 collective-permute-done.refs_4_
  124.6 0.0 collective-permute-done.1.refs_5_
  124.6 0.0 collective-permute-done.2.refs_6_
  124.6 0.7 copy-done.10
  125.2 3.9 %combine.2.refs_0_ = bf16[256,4096]{1,0:T(8,128)(2,1)} custom-call(s32[25]{0:T(128)} %get-tuple-element.28.refs_0_, f32[25]{0:T(128)} %get-tuple-element.29.refs_1_, s32[33]{0:T(128)} %get-tuple-element.30.refs_2_, bf16[2,16,32,128]{3,2,1,0:T(8,128)(2,1)} %get-tuple-element.31.refs_3_, bf16[2,16,32,128]{3,2,1,0:T(8,128)(2,1)} %collective-permute-done.refs_4_, ...), custom_call_target="tpu_custom_call" | custom-call | flops 4194304 | bytes 3145728 | tf_op jit(solution)/shard_map/combine/pallas_call | solution.py:198
  129.1 0.0 collective-permute-done.5.refs_3_.refs_2_
  129.1 1.6 copy-done
  130.7 5.4 %product.3 = (bf16[2,2,32,1024]{3,2,1,0:T(8,128)(2,1)S(1)}, f32[2,2,32,1024]{3,2,1,0:T(8,128)S(1)}) custom-call(bf16[256,4096]{1,0:T(8,128)(2,1)S(1)} %copy-done, bf16[16,128,1024]{2,1,0:T(8,128)(2,1)} %collective-permute-done.3.refs_1_, bf16[16,128,768]{2,1,0:T(8,128)(2,1)} %collective-permute-done.4.refs_2_, ...), custom_call_target="tpu_custom_call" | custom-call | flops 2147483648 | bytes 10485760 | tf_op jit(solution)/shard_map/product/pallas_call | solution.py:260
  136.2 0.8 copy-done.2
  137.0 3.7 %collective-permute-start.6 = (bf16[2,2,32,1024]{3,2,1,0:T(8,128)(2,1)S(1)}, bf16[2,2,32,1024]{3,2,1,0:T(8,128)(2,1)S(1)}, u32[]{:S(2)}, u32[]{:S(2)}) collective-permute-start(bf16[2,2,32,1024]{3,2,1,0:T(8,128)(2,1)S(1)} %get-tuple-element.36), channel_id=1, source_target_pairs={{0,2},{1,3},{2,0},{3,1},{4,6},{5,7},{6,4},{7,5},{8,10},{9,11},{10,... | collective-permute-start | bytes 786440 | tf_op jit(solution)/shard_map/ppermute | solution.py:25
  140.7 4.8 %product.4 = (bf16[2,2,96,256]{3,2,1,0:T(8,128)(2,1)S(1)}, f32[2,2,96,256]{3,2,1,0:T(8,128)S(1)}) custom-call(bf16[768,4096]{1,0:T(8,128)(2,1)} %combine.3.refs_0_, bf16[16,128,1024]{2,1,0:T(8,128)(2,1)} %collective-permute-done.3.refs_1_, bf16[16,128,256]{2,1,0:T(8,128)(2,1)S(1)} %collective-permute-done.5.refs_3_.refs_2_), custom_call_target="tpu_custom_call" | custom-call | flops 1610612736 | bytes 8388608 | tf_op jit(solution)/shard_map/product/pallas_call | solution.py:260
  145.5 0.7 copy-done.3
  146.3 0.0 collective-permute-start.11
  146.3 0.0 collective-permute-done.13.came
  146.3 0.8 copy-done.7
  147.1 2.4 %halve.5 = (bf16[1,2,96,768]{3,2,1,0:T(8,128)(2,1)}, f32[1,2,96,768]{3,2,1,0:T(8,128)}) custom-call(f32[2,2,96,768]{3,2,1,0:T(8,128)} %copy-done.1, bf16[2,2,96,768]{3,2,1,0:T(8,128)(2,1)} %copy-done.7), custom_call_target="tpu_custom_call" | custom-call | flops 294912 | bytes 2654208 | tf_op jit(solution)/shard_map/halve/pallas_call | solution.py:294
  149.5 3.0 %collective-permute-start.14 = (bf16[1,2,96,768]{3,2,1,0:T(8,128)(2,1)}, bf16[1,2,96,768]{3,2,1,0:T(8,128)(2,1)S(1)}, u32[]{:S(2)}, u32[]{:S(2)}) collective-permute-start(bf16[1,2,96,768]{3,2,1,0:T(8,128)(2,1)} %get-tuple-element.50), channel_id=1, source_target_pairs={{0,4},{1,5},{2,6},{3,7},{4,0},{5,1},{6,2},{7,3},{8,12},{9,13},{10,... | collective-permute-start | bytes 884744 | tf_op jit(solution)/shard_map/ppermute | solution.py:25
  152.5 0.0 collective-permute-done.6.came
  152.5 0.7 copy-done.9
  153.2 1.9 %halve.3 = (bf16[1,2,32,1024]{3,2,1,0:T(8,128)(2,1)}, f32[1,2,32,1024]{3,2,1,0:T(8,128)}) custom-call(f32[2,2,32,1024]{3,2,1,0:T(8,128)} %copy-done.2, bf16[2,2,32,1024]{3,2,1,0:T(8,128)(2,1)} %copy-done.9), custom_call_target="tpu_custom_call" | custom-call | flops 131072 | bytes 1179648 | tf_op jit(solution)/shard_map/halve/pallas_call | solution.py:294
  155.1 0.0 collective-permute-start.7
  155.1 0.7 copy-done.11
  155.8 1.8 %halve.4 = (bf16[1,2,96,256]{3,2,1,0:T(8,128)(2,1)}, f32[1,2,96,256]{3,2,1,0:T(8,128)}) custom-call(f32[2,2,96,256]{3,2,1,0:T(8,128)} %copy-done.3, bf16[2,2,96,256]{3,2,1,0:T(8,128)(2,1)} %copy-done.11), custom_call_target="tpu_custom_call" | custom-call | flops 98304 | bytes 884736 | tf_op jit(solution)/shard_map/halve/pallas_call | solution.py:294
  157.6 2.9 %collective-permute-start.12 = (bf16[1,2,96,256]{3,2,1,0:T(8,128)(2,1)}, bf16[1,2,96,256]{3,2,1,0:T(8,128)(2,1)S(1)}, u32[]{:S(2)}, u32[]{:S(2)}) collective-permute-start(bf16[1,2,96,256]{3,2,1,0:T(8,128)(2,1)} %get-tuple-element.46), channel_id=1, source_target_pairs={{0,4},{1,5},{2,6},{3,7},{4,0},{5,1},{6,2},{7,3},{8,12},{9,13},{10,... | collective-permute-start | bytes 294920 | tf_op jit(solution)/shard_map/ppermute | solution.py:25
  160.5 11.2 %collective-permute-done.14.came = bf16[1,2,96,768]{3,2,1,0:T(8,128)(2,1)S(1)} collective-permute-done((bf16[1,2,96,768]{3,2,1,0:T(8,128)(2,1)}, bf16[1,2,96,768]{3,2,1,0:T(8,128)(2,1)S(1)}, u32[]{:S(2)}, u32[]{:S(2)}) %collective-permute-start.14) | collective-permute-done | bytes 294944 | tf_op jit(solution)/shard_map/ppermute | solution.py:25
  171.7 0.7 copy-done.8
  172.4 2.1 %finish.3.refs_0_ = f32[128,2,1024]{2,1,0:T(2,128)} custom-call(f32[1,2,96,768]{3,2,1,0:T(8,128)} %get-tuple-element.49.keep, bf16[1,2,96,768]{3,2,1,0:T(8,128)(2,1)} %copy-done.8), custom_call_target="tpu_custom_call" | custom-call | flops 147456 | bytes 1474560 | tf_op jit(solution)/shard_map/finish/pallas_call | solution.py:323
  174.6 0.8 collective-permute-done.12.came
  175.4 0.6 copy-done.13
  176.0 1.7 finish.4.refs_0_
  177.7 0.6 copy-done.12
  178.4 1.8 finish.5
  (24 shorter events, 0.0 us)
Async XLA Ops:
  0.0 113.8 %collective-permute-start.3 = (bf16[16,128,1024]{2,1,0:T(8,128)(2,1)}, bf16[16,128,1024]{2,1,0:T(8,128)(2,1)}, u32[]{:S(2)}, u32[]{:S(2)}) collective-permute-start(bf16[16,128,1024]{2,1,0:T(8,128)(2,1)} %bitcast.5), channel_id=1, source_target_pairs={{0,8},{8,0},{16,24},{24,16},{1,9},{9,1},{17,25},{25,17},{2,10},{10... | collective-permute-start | bytes 12582920 | tf_op jit(solution)/shard_map/ppermute | solution.py:25
  4.0 109.0 %collective-permute-start.4 = (bf16[16,128,768]{2,1,0:T(8,128)(2,1)}, bf16[16,128,768]{2,1,0:T(8,128)(2,1)}, u32[]{:S(2)}, u32[]{:S(2)}) collective-permute-start(bf16[16,128,768]{2,1,0:T(8,128)(2,1)} %slab.2), channel_id=1, source_target_pairs={{0,9},{1,8},{2,11},{3,10},{4,13},{5,12},{6,15},{7,14},{8,1},{9,0},... | collective-permute-start | bytes 9437192 | tf_op jit(solution)/shard_map/ppermute | solution.py:25
  10.4 23.3 %copy-start.15 = (s32[1,3]{1,0:T(1,128)S(1)}, s32[1,3]{1,0:T(1,128)}, u32[]{:S(2)}) copy-start(s32[1,3]{1,0:T(1,128)} %param.8) | copy-start | bytes 40
  10.4 23.3 %copy-start.16 = (s32[1,3]{1,0:T(1,128)S(1)}, s32[1,3]{1,0:T(1,128)}, u32[]{:S(2)}) copy-start(s32[1,3]{1,0:T(1,128)} %param.9) | copy-start | bytes 40
  10.4 23.3 %copy-start.17 = (s32[1,3]{1,0:T(1,128)S(1)}, s32[1,3]{1,0:T(1,128)}, u32[]{:S(2)}) copy-start(s32[1,3]{1,0:T(1,128)} %param.10) | copy-start | bytes 40
  10.4 23.3 %copy-start.18 = (s32[1,3]{1,0:T(1,128)S(1)}, s32[1,3]{1,0:T(1,128)}, u32[]{:S(2)}) copy-start(s32[1,3]{1,0:T(1,128)} %param.11) | copy-start | bytes 40
  10.4 22.6 %collective-permute-start.10 = (bf16[2,16,96,128]{3,2,1,0:T(8,128)(2,1)}, bf16[2,16,96,128]{3,2,1,0:T(8,128)(2,1)S(1)}, u32[]{:S(2)}, u32[]{:S(2)}) collective-permute-start(bf16[2,16,96,128]{3,2,1,0:T(8,128)(2,1)} %get-tuple-element.42), channel_id=1, source_target_pairs={{0,6},{1,7},{2,4},{3,5},{4,2},{5,3},{6,0},{7,1},{8,14},{9,15},{10,... | collective-permute-start | bytes 2359304 | tf_op jit(solution)/shard_map/ppermute | solution.py:25
  14.1 86.5 %collective-permute-start.8 = (bf16[2,16,96,128]{3,2,1,0:T(8,128)(2,1)}, bf16[2,16,96,128]{3,2,1,0:T(8,128)(2,1)S(1)}, u32[]{:S(2)}, u32[]{:S(2)}) collective-permute-start(bf16[2,16,96,128]{3,2,1,0:T(8,128)(2,1)} %get-tuple-element.40), channel_id=1, source_target_pairs={{0,2},{1,3},{2,0},{3,1},{4,6},{5,7},{6,4},{7,5},{8,10},{9,11},{10,... | collective-permute-start | bytes 2359304 | tf_op jit(solution)/shard_map/ppermute | solution.py:25
  14.1 88.3 %collective-permute-start.9 = (bf16[2,16,96,128]{3,2,1,0:T(8,128)(2,1)}, bf16[2,16,96,128]{3,2,1,0:T(8,128)(2,1)S(1)}, u32[]{:S(2)}, u32[]{:S(2)}) collective-permute-start(bf16[2,16,96,128]{3,2,1,0:T(8,128)(2,1)} %get-tuple-element.41), channel_id=1, source_target_pairs={{0,4},{1,5},{2,6},{3,7},{4,0},{5,1},{6,2},{7,3},{8,12},{9,13},{10,... | collective-permute-start | bytes 2359304 | tf_op jit(solution)/shard_map/ppermute | solution.py:25
  33.0 72.0 %copy-start.4 = (bf16[2,16,96,128]{3,2,1,0:T(8,128)(2,1)}, bf16[2,16,96,128]{3,2,1,0:T(8,128)(2,1)S(1)}, u32[]{:S(2)}) copy-start(bf16[2,16,96,128]{3,2,1,0:T(8,128)(2,1)S(1)} %collective-permute-done.10.refs_6_) | copy-start | bytes 2359300
  33.0 96.1 %collective-permute-start.5 = (bf16[16,128,256]{2,1,0:T(8,128)(2,1)}, bf16[16,128,256]{2,1,0:T(8,128)(2,1)S(1)}, u32[]{:S(2)}, u32[]{:S(2)}) collective-permute-start(bf16[16,128,256]{2,1,0:T(8,128)(2,1)} %slab.3), channel_id=1, source_target_pairs={{0,9},{1,8},{2,11},{3,10},{4,13},{5,12},{6,15},{7,14},{8,1},{9,0},... | collective-permute-start | bytes 3145736 | tf_op jit(solution)/shard_map/ppermute | solution.py:25
  34.4 63.7 %all-to-all-start = ((s32[8,1,13]{2,1,0:T(1,128)}), s32[8,1,13]{2,1,0:T(1,128)S(1)}, u32[]{:S(2)}, u32[]{:S(2)}) async-start(s32[8,1,13]{2,1,0:T(1,128)} %broadcast_in_dim.2), calls=%async_computation | async-start | bytes 8192 | tf_op jit(solution)/shard_map/all_to_all | solution.py:347
  98.1 0.6 copy-start.14
  100.6 4.4 %copy-start.5 = (bf16[2,16,96,128]{3,2,1,0:T(8,128)(2,1)}, bf16[2,16,96,128]{3,2,1,0:T(8,128)(2,1)S(1)}, u32[]{:S(2)}) copy-start(bf16[2,16,96,128]{3,2,1,0:T(8,128)(2,1)S(1)} %collective-permute-done.8.refs_4_) | copy-start | bytes 2359300
  100.6 24.0 %collective-permute-start = (bf16[2,16,32,128]{3,2,1,0:T(8,128)(2,1)}, bf16[2,16,32,128]{3,2,1,0:T(8,128)(2,1)}, u32[]{:S(2)}, u32[]{:S(2)}) collective-permute-start(bf16[2,16,32,128]{3,2,1,0:T(8,128)(2,1)} %get-tuple-element.32), channel_id=1, source_target_pairs={{0,2},{1,3},{2,0},{3,1},{4,6},{5,7},{6,4},{7,5},{8,10},{9,11},{10,... | collective-permute-start | bytes 786440 | tf_op jit(solution)/shard_map/ppermute | solution.py:25
  102.4 2.6 %copy-start.6 = (bf16[2,16,96,128]{3,2,1,0:T(8,128)(2,1)}, bf16[2,16,96,128]{3,2,1,0:T(8,128)(2,1)S(1)}, u32[]{:S(2)}) copy-start(bf16[2,16,96,128]{3,2,1,0:T(8,128)(2,1)S(1)} %collective-permute-done.9.refs_5_) | copy-start | bytes 2359300
  102.4 22.2 %collective-permute-start.1 = (bf16[2,16,32,128]{3,2,1,0:T(8,128)(2,1)}, bf16[2,16,32,128]{3,2,1,0:T(8,128)(2,1)}, u32[]{:S(2)}, u32[]{:S(2)}) collective-permute-start(bf16[2,16,32,128]{3,2,1,0:T(8,128)(2,1)} %get-tuple-element.33), channel_id=1, source_target_pairs={{0,4},{1,5},{2,6},{3,7},{4,0},{5,1},{6,2},{7,3},{8,12},{9,13},{10,... | collective-permute-start | bytes 786440 | tf_op jit(solution)/shard_map/ppermute | solution.py:25
  113.0 11.5 %collective-permute-start.2 = (bf16[2,16,32,128]{3,2,1,0:T(8,128)(2,1)}, bf16[2,16,32,128]{3,2,1,0:T(8,128)(2,1)S(1)}, u32[]{:S(2)}, u32[]{:S(2)}) collective-permute-start(bf16[2,16,32,128]{3,2,1,0:T(8,128)(2,1)} %get-tuple-element.34), channel_id=1, source_target_pairs={{0,6},{1,7},{2,4},{3,5},{4,2},{5,3},{6,0},{7,1},{8,14},{9,15},{10,... | collective-permute-start | bytes 786440 | tf_op jit(solution)/shard_map/ppermute | solution.py:25
  122.8 1.0 copy-start.1
  123.9 22.4 %collective-permute-start.13 = (bf16[2,2,96,768]{3,2,1,0:T(8,128)(2,1)S(1)}, bf16[2,2,96,768]{3,2,1,0:T(8,128)(2,1)S(1)}, u32[]{:S(2)}, u32[]{:S(2)}) collective-permute-start(bf16[2,2,96,768]{3,2,1,0:T(8,128)(2,1)S(1)} %get-tuple-element.48), channel_id=1, source_target_pairs={{0,2},{1,3},{2,0},{3,1},{4,6},{5,7},{6,4},{7,5},{8,10},{9,11},{10,... | collective-permute-start | bytes 1769480 | tf_op jit(solution)/shard_map/ppermute | solution.py:25
  124.6 0.7 copy-start.10
  129.1 1.6 copy-start
  136.2 0.8 copy-start.2
  137.0 15.5 %collective-permute-start.6 = (bf16[2,2,32,1024]{3,2,1,0:T(8,128)(2,1)S(1)}, bf16[2,2,32,1024]{3,2,1,0:T(8,128)(2,1)S(1)}, u32[]{:S(2)}, u32[]{:S(2)}) collective-permute-start(bf16[2,2,32,1024]{3,2,1,0:T(8,128)(2,1)S(1)} %get-tuple-element.36), channel_id=1, source_target_pairs={{0,2},{1,3},{2,0},{3,1},{4,6},{5,7},{6,4},{7,5},{8,10},{9,11},{10,... | collective-permute-start | bytes 786440 | tf_op jit(solution)/shard_map/ppermute | solution.py:25
  145.5 0.7 copy-start.3
  146.3 8.9 %collective-permute-start.11 = (bf16[2,2,96,256]{3,2,1,0:T(8,128)(2,1)S(1)}, bf16[2,2,96,256]{3,2,1,0:T(8,128)(2,1)S(1)}, u32[]{:S(2)}, u32[]{:S(2)}) collective-permute-start(bf16[2,2,96,256]{3,2,1,0:T(8,128)(2,1)S(1)} %get-tuple-element.44), channel_id=1, source_target_pairs={{0,2},{1,3},{2,0},{3,1},{4,6},{5,7},{6,4},{7,5},{8,10},{9,11},{10,... | collective-permute-start | bytes 589832 | tf_op jit(solution)/shard_map/ppermute | solution.py:25
  146.3 0.8 copy-start.7
  149.5 22.2 %collective-permute-start.14 = (bf16[1,2,96,768]{3,2,1,0:T(8,128)(2,1)}, bf16[1,2,96,768]{3,2,1,0:T(8,128)(2,1)S(1)}, u32[]{:S(2)}, u32[]{:S(2)}) collective-permute-start(bf16[1,2,96,768]{3,2,1,0:T(8,128)(2,1)} %get-tuple-element.50), channel_id=1, source_target_pairs={{0,4},{1,5},{2,6},{3,7},{4,0},{5,1},{6,2},{7,3},{8,12},{9,13},{10,... | collective-permute-start | bytes 884744 | tf_op jit(solution)/shard_map/ppermute | solution.py:25
  152.5 0.7 copy-start.9
  155.1 22.6 %collective-permute-start.7 = (bf16[1,2,32,1024]{3,2,1,0:T(8,128)(2,1)}, bf16[1,2,32,1024]{3,2,1,0:T(8,128)(2,1)S(1)}, u32[]{:S(2)}, u32[]{:S(2)}) collective-permute-start(bf16[1,2,32,1024]{3,2,1,0:T(8,128)(2,1)} %get-tuple-element.38), channel_id=1, source_target_pairs={{0,4},{1,5},{2,6},{3,7},{4,0},{5,1},{6,2},{7,3},{8,12},{9,13},{10,... | collective-permute-start | bytes 393224 | tf_op jit(solution)/shard_map/ppermute | solution.py:25
  155.1 0.7 copy-start.11
  157.6 17.8 %collective-permute-start.12 = (bf16[1,2,96,256]{3,2,1,0:T(8,128)(2,1)}, bf16[1,2,96,256]{3,2,1,0:T(8,128)(2,1)S(1)}, u32[]{:S(2)}, u32[]{:S(2)}) collective-permute-start(bf16[1,2,96,256]{3,2,1,0:T(8,128)(2,1)} %get-tuple-element.46), channel_id=1, source_target_pairs={{0,4},{1,5},{2,6},{3,7},{4,0},{5,1},{6,2},{7,3},{8,12},{9,13},{10,... | collective-permute-start | bytes 294920 | tf_op jit(solution)/shard_map/ppermute | solution.py:25
  171.7 0.7 copy-start.8
  175.4 0.6 copy-start.13
  177.7 0.7 copy-start.12
where the time goes:
time: 181 us; the launch traced here: 180 us
  waiting for transfers between devices  70.3 us (39%)
  Pallas kernels  56.7 us (31%)
  starting transfers between devices  41.9 us (23%)
  local copies, waits for them, and re-layouts  10.3 us (6%)
    all_to_all x1, waiting for transfers between devices, body(): lax.all_to_all(jnp.broadcast_to(meta, (devices, meta.shape[1])), 'pair',...  42.4 us
    ppermute x15, waiting for transfers between devices, swap(): return lax.ppermute(value, axis, [(i, i ^ apart) for i in range(size)])  27.9 us
    ppermute x15, starting transfers between devices, swap(): return lax.ppermute(value, axis, [(i, i ^ apart) for i in range(size)])  23.1 us
    pallas_call x3, Pallas kernels, product(): pl.pallas_call(functools.partial(product_kernel, groups, rows, edges), gr...  19.3 us
    all_to_all x1, starting transfers between devices, body(): lax.all_to_all(jnp.broadcast_to(meta, (devices, meta.shape[1])), 'pair',...  18.8 us
    pallas_call x2, Pallas kernels, combine(): pl.pallas_call(combine_kernel, out_shape=jax.ShapeDtypeStruct(shape, jnp....  11.9 us
    unnamed x38, local copies, waits for them, and re-layouts  9.62 us
    pallas_call x2, Pallas kernels, pack(): pl.pallas_call(functools.partial(pack_kernel, start, rows, width), out_sh...  6.11 us
  transfers between devices with their start and end apart: 16, of which 4 were waited for; matrix products, arithmetic and copies ran while one was open for 0% of the time, Pallas kernels for 30%

commit v1 on v0

v1 whole, which is shorter than its diff:
```python
import functools

import jax
import jax.numpy as jnp
from jax import lax
from jax.experimental import pallas as pl
from jax.experimental.pallas import tpu as pltpu
from jax.sharding import PartitionSpec as P

SLICES = 2
SUBLANES = 16
LANES = 128
ROW_PARTS = (6, 2)
COLUMN_PARTS = (3, 1)


def cut(length, unit, parts):
    units, total = length // unit, sum(parts)
    edges = [units * sum(parts[:part]) // total for part in range(len(parts) + 1)]
    return [(lo * unit, (hi - lo) * unit) for lo, hi in zip(edges, edges[1:]) if hi > lo]


def swap(value, axis, apart):
    size = lax.axis_size(axis)
    return lax.ppermute(value, axis, [(i, i ^ apart) for i in range(size)])


def spec(space=pltpu.VMEM):
    return pl.BlockSpec(memory_space=space)


def base_count(families):
    return families - families // 4


def slot_fields(metas):
    per_list = (metas.shape[1] - 1) // 4
    for i in range(metas.shape[0]):
        count = metas[i, 4 * per_list]
        for k in range(per_list):
            yield (k < count,) + tuple(metas[i, field * per_list + k] for field in range(4))


def order_kernel(families, metas, left_order, left_rank, right_order, right_rank, more, used):
    def clear(a, carry):
        used[a] = 0
        used[families + 1 + a] = 0
        left_order[a] = 0
        right_order[a] = 0
        return carry

    lax.fori_loop(0, families + 1, clear, 0)
    for live, left, right, _, _ in slot_fields(metas):
        used[jnp.where(live, left, families)] = 1
        used[families + 1 + jnp.where(live, right, families)] = 1

    def place(a, found):
        lefts, rights = found
        left_rank[a] = lefts
        right_rank[a] = rights
        has_left, has_right = used[a], used[families + 1 + a]
        left_order[jnp.where(has_left > 0, lefts, families)] = a
        right_order[jnp.where(has_right > 0, rights, families)] = a
        return lefts + has_left, rights + has_right

    zero = jnp.int32(0)
    lefts, rights = lax.fori_loop(0, families, place, (zero, zero))
    more[0] = (jnp.maximum(lefts, rights) > base_count(families)).astype(jnp.int32)


def order_blocks(metas, families):
    ids = jax.ShapeDtypeStruct((families + 1,), jnp.int32)
    return pl.pallas_call(
        functools.partial(order_kernel, families),
        out_shape=(ids, ids, ids, ids, jax.ShapeDtypeStruct((1,), jnp.int32)),
        in_specs=[spec(pltpu.SMEM)],
        out_specs=(spec(pltpu.SMEM),) * 5,
        scratch_shapes=[pltpu.SMEM((2 * families + 2,), jnp.int32)],
        name="order",
    )(metas)


def plan_kernel(
    families, metas, left_rank, right_rank, subduction, left_list, weight_list, offsets, cursor
):
    base, keys = base_count(families), 2 * SLICES * families
    dump = left_list.shape[0] - 1

    def clear(q, carry):
        cursor[q] = 0
        return carry

    lax.fori_loop(0, keys + 1, clear, 0)
    slots = []
    for live, left, right, piece, weight in slot_fields(metas):
        rank = left_rank[left]
        late = (rank >= base).astype(jnp.int32)
        key = 2 * (piece * families + right_rank[right]) + late
        slots.append((live, jnp.where(live, key, keys), rank - base * late, weight))
    for _, key, _, _ in slots:
        cursor[key] = cursor[key] + 1

    def place(q, total):
        here = cursor[q]
        offsets[q] = total
        cursor[q] = total
        return total + here

    offsets[keys] = lax.fori_loop(0, keys, place, 0)
    cursor[keys] = 0
    for live, key, rank, weight in slots:
        at = cursor[key]
        cursor[key] = at + 1
        at = jnp.where(live, at, dump)
        left_list[at] = rank
        weight_list[at] = subduction[weight]


def plan(metas, left_rank, right_rank, subduction, families):
    slots = metas.shape[0] * (metas.shape[1] - 1) // 4
    keys = 2 * SLICES * families
    return pl.pallas_call(
        functools.partial(plan_kernel, families),
        out_shape=(
            jax.ShapeDtypeStruct((slots + 1,), jnp.int32),
            jax.ShapeDtypeStruct((slots + 1,), jnp.float32),
            jax.ShapeDtypeStruct((keys + 1,), jnp.int32),
        ),
        in_specs=[spec(pltpu.SMEM)] * 4,
        out_specs=(spec(pltpu.SMEM),) * 3,
        scratch_shapes=[pltpu.SMEM((keys + 1,), jnp.int32)],
        name="plan",
    )(metas, left_rank, right_rank, subduction)


def pack_kernel(first, start, rows, width, order, me, own, *refs):
    outs, sem = refs[:-1], refs[-1]
    copies = []
    for group, out in enumerate(outs):
        for half in range(2):
            column = pl.multiple_of((me[0] ^ (2 * group + half)) * width, width)
            for i in range(out.shape[1]):
                source = own.at[order[first + i], pl.ds(start, rows), pl.ds(column, width)]
                at = (2 * group + half) * out.shape[1] + i
                copies.append(pltpu.make_async_copy(source, out.at[half, i], sem.at[at]))
    for copy in copies:
        copy.start()
    for copy in copies:
        copy.wait()


def pack(own, order, me, first, number, start, rows, width, groups):
    if width % LANES:
        blocks = jnp.take(own, order[first : first + number], axis=0)

        def columns(offset):
            at = (0, start, (me[0] ^ offset) * width)
            return lax.dynamic_slice(blocks, at, (number, rows, width))

        return [
            jnp.stack([columns(2 * group), columns(2 * group + 1)]) for group in range(groups)
        ]
    piece = jax.ShapeDtypeStruct((2, number, rows, width), own.dtype)
    return pl.pallas_call(
        functools.partial(pack_kernel, first, start, rows, width),
        out_shape=[piece] * groups,
        in_specs=[spec(pltpu.SMEM)] * 2 + [spec(pl.ANY)],
        out_specs=[spec()] * groups,
        scratch_shapes=[pltpu.SemaphoreType.DMA((2 * groups * number,))],
        cost_estimate=pl.CostEstimate(
            flops=0, transcendentals=0, bytes_accessed=4 * groups * piece.size
        ),
        compiler_params=pltpu.CompilerParams(vmem_limit_bytes=8 << 20),
        name="pack",
    )(order, me, own)


def slab_kernel(first, start, order, own, out, sem):
    copies = []
    for i in range(out.shape[0]):
        source = own.at[order[first + i], :, pl.ds(start, out.shape[2])]
        copies.append(pltpu.make_async_copy(source, out.at[i], sem.at[i]))
    for copy in copies:
        copy.start()
    for copy in copies:
        copy.wait()


def slab(own, order, first, number, start, columns):
    shape = (number, own.shape[1], columns)
    return pl.pallas_call(
        functools.partial(slab_kernel, first, start),
        out_shape=jax.ShapeDtypeStruct(shape, own.dtype),
        in_specs=[spec(pltpu.SMEM), spec(pl.ANY)],
        out_specs=spec(),
        scratch_shapes=[pltpu.SemaphoreType.DMA((number,))],
        cost_estimate=pl.CostEstimate(
            flops=0, transcendentals=0, bytes_accessed=4 * number * own.shape[1] * columns
        ),
        compiler_params=pltpu.CompilerParams(vmem_limit_bytes=8 << 20),
        name="slab",
    )(order, own)


def unset(shapes):
    return pl.pallas_call(
        lambda *refs: None,
        out_shape=shapes,
        out_specs=[spec(pl.ANY)] * len(shapes),
        name="unset",
    )()


def late_blocks(own, left_order, right_order, me, more, width, groups):
    families, rows, order = own.shape
    devices, first = 2 * groups, base_count(families)
    number = families - first
    piece = jax.ShapeDtypeStruct((2, number, rows, width), own.dtype)
    part = jax.ShapeDtypeStruct((number, rows, order), own.dtype)

    def exchange():
        pieces = pack(own, left_order, me, first, number, 0, rows, width, groups)
        moved = [swap(pieces[group], "pair", 2 * group) for group in range(1, groups)]
        mine = slab(own, right_order, first, number, 0, order)
        near = swap(mine, "mom", 1)
        far = swap(mine, ("mom", "pair"), devices + 1)
        return [pieces[0], *moved, near, far]

    def skip():
        return list(unset([piece] * groups + [part] * 2))

    arrays = lax.cond(more, exchange, skip)
    return arrays[:groups], arrays[groups], arrays[groups + 1]


def combine_rows(table, more, lefts, lates, combined):
    left_list, weight_list, offsets = table
    _, base, rows, width = lefts[0].shape
    families = base + lates[0].shape[1]
    step = min(rows, 2 * SUBLANES)

    def combine(t, b):
        q = 2 * (t * families + b)
        for top in range(0, rows, step):
            here = min(step, rows - top)

            def add_from(refs, low):
                def add(s, sums):
                    left, weight = left_list[s], weight_list[s]
                    pieces = [
                        ref[half, left, low : low + here, :].astype(jnp.float32)
                        for ref in refs
                        for half in range(2)
                    ]
                    return tuple(total + weight * piece for total, piece in zip(sums, pieces))

                return add

            sums = (jnp.zeros((here, width), jnp.float32),) * (2 * len(lefts))
            sums = lax.fori_loop(offsets[q], offsets[q + 1], add_from(lefts, top), sums)
            sums = lax.fori_loop(
                offsets[q + 1], offsets[q + 2], add_from(lates, top), sums
            )
            for i, total in enumerate(sums):
                group, half = divmod(i, 2)
                at = (t * len(lefts) + group) * rows + top
                column = jnp.where(
                    b < base,
                    half * base + b,
                    2 * base + half * (families - base) + b - base,
                )
                if isinstance(b, int):
                    column = half * base + b
                    if b >= base:
                        column = 2 * base + half * (families - base) + b - base
                    column *= width
                else:
                    at = pl.multiple_of(at, SUBLANES)
                    column = pl.multiple_of(column * width, width)
                value = total.astype(combined.dtype)
                combined[pl.ds(at, here), pl.ds(column, width)] = value

    if width % LANES:
        for t in range(SLICES):
            for b in range(families):
                combine(t, b)
        return
    count = jnp.where(more[0] > 0, families, base)

    def both(b, carry):
        for t in range(SLICES):
            combine(t, b)
        return carry

    lax.fori_loop(0, count, both, 0)


def fetch_if(wanted, sources, targets, sems):
    @pl.when(wanted)
    def fetch():
        copies = [
            pltpu.make_async_copy(source, target, sems.at[i])
            for i, (source, target) in enumerate(zip(sources, targets))
        ]
        for copy in copies:
            copy.start()
        for copy in copies:
            copy.wait()


def combine_kernel(start, groups, *refs):
    table, more, refs = refs[:3], refs[3], refs[4:]
    lefts, lates, combined = refs[:groups], refs[groups : 2 * groups], refs[2 * groups]
    held, sems = refs[2 * groups + 1 : -1], refs[-1]
    rows = lefts[0].shape[2]
    sources = [late.at[:, :, pl.ds(start, rows)] for late in lates]
    fetch_if(more[0] > 0, sources, held, sems)
    combine_rows(table, more, lefts, held, combined)


def combine(table, more, lefts, lates, start):
    _, base, rows, width = lefts[0].shape
    families = base + lates[0].shape[1]
    shape = SLICES * len(lefts) * rows, 2 * families * width
    size = shape[0] * shape[1]
    return pl.pallas_call(
        functools.partial(combine_kernel, start, len(lefts)),
        out_shape=jax.ShapeDtypeStruct(shape, jnp.bfloat16),
        in_specs=[spec(pltpu.SMEM)] * 4
        + [spec()] * len(lefts)
        + [spec(pl.ANY)] * len(lates),
        out_specs=spec(),
        scratch_shapes=[pltpu.VMEM((2, families - base, rows, width), jnp.bfloat16)] * len(lates)
        + [pltpu.SemaphoreType.DMA((len(lates),))],
        compiler_params=pltpu.CompilerParams(vmem_limit_bytes=20 << 20),
        cost_estimate=pl.CostEstimate(
            flops=4 * size, transcendentals=0, bytes_accessed=3 * size
        ),
        name="combine",
    )(*table, more, *lefts, *lates)


def product_kernel(groups, chunks, edges, start, more, *refs):
    combined, refs = refs[: len(chunks)], refs[len(chunks) :]
    nears, fars, refs = refs[: len(edges)], refs[len(edges) : 2 * len(edges)], refs[-7:]
    lates, (send, keep), held, sems = refs[:2], refs[2:4], refs[4:6], refs[6]
    _, width, tile = nears[0].shape
    step = pl.program_id(0)
    columns = pl.ds(pl.multiple_of(start + step * tile, tile), tile)
    fetch_if(more[0] > 0, [late.at[:, :, columns] for late in lates], held, sems)

    def multiply(parts):
        top = 0
        for chunk in combined:
            total, at = None, 0
            for part in parts:
                depth = part.shape[0] * width
                term = jnp.dot(
                    chunk[:, at : at + depth],
                    part[...].reshape(depth, tile),
                    preferred_element_type=jnp.float32,
                )
                total = term if total is None else total + term
                at += depth
            rows = chunk.shape[0] // (SLICES * groups)
            for i in range(SLICES * groups):
                t, group = divmod(i, groups)
                piece = total[i * rows : (i + 1) * rows]
                if group % 2:
                    send[group // 2, t, top : top + rows] = piece.astype(send.dtype)
                else:
                    keep[group // 2, t, top : top + rows] = piece
            top += rows

    for near, far, (lo, hi) in zip(nears, fars, edges):
        here = (step >= lo) & (step < hi)
        usual = functools.partial(multiply, (near, far))
        full = functools.partial(multiply, (near, far, *held))
        pl.when(here & (more[0] == 0))(usual)
        pl.when(here & (more[0] > 0))(full)


def product(more, combined, nears, fars, lates, start, groups):
    base, width, _ = nears[0].shape
    late = lates[0].shape[0]
    rows = [chunk.shape[0] // (SLICES * groups) for chunk in combined]
    columns = sum(part.shape[2] for part in fars)
    tile = 2 * LANES
    edges, at = [], 0
    for part in fars:
        edges.append((at, at + part.shape[2] // tile))
        at = edges[-1][1]

    def place(lo, hi):
        return lambda i: (0, 0, jnp.clip(i - lo, 0, hi - lo - 1))

    shape = (groups // 2, SLICES, sum(rows), columns)
    block = pl.BlockSpec((groups // 2, SLICES, sum(rows), tile), lambda i: (0, 0, 0, i))
    return pl.pallas_call(
        functools.partial(product_kernel, groups, rows, edges, start),
        grid=(columns // tile,),
        out_shape=(
            jax.ShapeDtypeStruct(shape, jnp.bfloat16),
            jax.ShapeDtypeStruct(shape, jnp.float32),
        ),
        in_specs=[spec(pltpu.SMEM)]
        + [
            pl.BlockSpec(chunk.shape, lambda i: (0, 0), pipeline_mode=pl.Buffered(1))
            for chunk in combined
        ]
        + [pl.BlockSpec((base, width, tile), place(lo, hi)) for lo, hi in edges] * 2
        + [spec(pl.ANY)] * 2,
        out_specs=(block, block),
        scratch_shapes=[pltpu.VMEM((late, width, tile), jnp.bfloat16)] * 2
        + [pltpu.SemaphoreType.DMA((2,))],
        compiler_params=pltpu.CompilerParams(vmem_limit_bytes=24 << 20),
        cost_estimate=pl.CostEstimate(
            flops=2 * sum(chunk.size for chunk in combined) * columns,
            transcendentals=0,
            bytes_accessed=sum(2 * chunk.size for chunk in combined)
            + 4 * (base + late) * width * columns,
        ),
        name="product",
    )(more, *combined, *nears, *fars, *lates)


def halve_kernel(keep, came, send, kept):
    for i in range(send.shape[0]):
        kept[i] = keep[2 * i] + came[2 * i].astype(jnp.float32)
        total = keep[2 * i + 1] + came[2 * i + 1].astype(jnp.float32)
        send[i] = total.astype(send.dtype)


def halve(keep, came):
    shape = (keep.shape[0] // 2,) + keep.shape[1:]
    return pl.pallas_call(
        halve_kernel,
        out_shape=(
            jax.ShapeDtypeStruct(shape, jnp.bfloat16),
            jax.ShapeDtypeStruct(shape, jnp.float32),
        ),
        in_specs=[spec()] * 2,
        out_specs=(spec(), spec()),
        cost_estimate=pl.CostEstimate(
            flops=keep.size, transcendentals=0, bytes_accessed=9 * keep.size
        ),
        compiler_params=pltpu.CompilerParams(vmem_limit_bytes=8 << 20),
        name="halve",
    )(keep, came)


def finish_kernel(row, column, keep, came, *refs):
    out, buffer, sem = refs[-3:]
    rows, _, columns = buffer.shape
    for t in range(SLICES):
        buffer[:, t, :] = keep[0, t] + came[0, t].astype(jnp.float32)
    target = out.at[pl.ds(row, rows), :, pl.ds(column, columns)]
    copy = pltpu.make_async_copy(buffer, target, sem)
    copy.start()
    copy.wait()


def finish(keep, came, row, column, rows, order, result):
    here, columns = keep.shape[2:]
    before = [] if result is None else [result]
    return pl.pallas_call(
        functools.partial(finish_kernel, row, column),
        out_shape=jax.ShapeDtypeStruct((rows, SLICES, order), jnp.float32),
        in_specs=[spec()] * 2 + [spec(pl.ANY)] * len(before),
        out_specs=spec(pl.ANY),
        scratch_shapes=[
            pltpu.VMEM((here, SLICES, columns), jnp.float32),
            pltpu.SemaphoreType.DMA,
        ],
        input_output_aliases={2: 0} if before else {},
        cost_estimate=pl.CostEstimate(
            flops=keep.size, transcendentals=0, bytes_accessed=10 * keep.size
        ),
        compiler_params=pltpu.CompilerParams(vmem_limit_bytes=8 << 20),
        name="finish",
    )(keep, came, *before)


def body(blocks, left_ids, right_ids, slice_ids, weight_ids, counts, subduction):
    own = blocks[0]
    families, rows, order = own.shape
    devices = lax.axis_size("pair")
    groups, width = devices // 2, order // devices
    me = lax.axis_index("pair").reshape(1)
    meta = jnp.concatenate([left_ids, right_ids, slice_ids, weight_ids, counts], axis=1)
    metas = lax.all_to_all(
        jnp.broadcast_to(meta, (devices, meta.shape[1])), "pair", 0, 0, tiled=True
    )
    partner = swap(metas, "mom", 1)
    left_order, left_rank, _, right_rank, more = order_blocks(metas, families)
    right_order = order_blocks(partner, families)[2]
    base = base_count(families)
    row_cuts = cut(rows, SUBLANES, ROW_PARTS)
    column_cuts = cut(order, 2 * LANES, COLUMN_PARTS)
    arrived, nears, fars = [], [], []
    for start, here in row_cuts:
        pieces = pack(
            own, left_order, me, 0, base, start, here, width, groups
        )
        moved = [swap(pieces[group], "pair", 2 * group) for group in range(groups - 1, 0, -1)]
        arrived.append([pieces[0]] + moved[::-1])
    for start, columns in column_cuts:
        mine = slab(own, right_order, 0, base, start, columns)
        fars.append(swap(mine, ("mom", "pair"), devices + 1))
        nears.append(swap(mine, "mom", 1))
    anywhere = more
    for bit in range(lax.axis_size("mom").bit_length() - 1):
        anywhere = jnp.maximum(anywhere, swap(anywhere, "mom", 1 << bit))
    late_lefts, late_near, late_far = late_blocks(
        own, left_order, right_order, me, anywhere[0] > 0, width, groups
    )
    table = plan(metas, left_rank, right_rank, subduction, families)
    last, columns = len(row_cuts) - 1, range(len(column_cuts))
    jobs = [(range(last), [j]) for j in columns] + [([last], columns)]
    combined = [
        combine(table, more, lefts, late_lefts, row_cuts[i][0])
        for i, lefts in enumerate(arrived)
    ]
    result = None
    for chunks, parts in jobs:
        row, column = row_cuts[chunks[0]][0], column_cuts[parts[0]][0]
        send, keep = product(
            more,
            [combined[i] for i in chunks],
            [nears[j] for j in parts],
            [fars[j] for j in parts],
            [late_near, late_far],
            column,
            groups,
        )
        apart = 1
        while 2 * apart < groups:
            came = swap(send, "pair", 2 * apart)
            send, keep = halve(keep, came)
            apart *= 2
        came = swap(send, "pair", 2 * apart)
        result = finish(keep, came, row, column, rows, order, result)
    return result.reshape((1,) + result.shape)


def solution(mesh):
    return jax.shard_map(
        body,
        mesh=mesh,
        in_specs=(
            P("mom", None, "pair", None),
            P("mom", "pair"),
            P("mom", "pair"),
            P("mom", "pair"),
            P("mom", "pair"),
            P("mom", "pair"),
            P(),
        ),
        out_specs=P("mom", "pair", None, None),
        check_vma=False,
    )
```

time: 181 us -> 166 us (0.917)
  Pallas kernels: 56.7 us -> 39.9 us
  waiting for transfers between devices: 70.3 us -> 84.7 us
  starting transfers between devices: 41.9 us -> 28.7 us
  between operations: 0.9 us -> 2.88 us
    ppermute x15 -> x19, waiting for transfers between devices: 27.9 us -> 78.3 us  [swap(): return lax.ppermute(value, axis, [(i, i ^ apart) for i in range(size)])]
    all_to_all x1, waiting for transfers between devices: 42.4 us -> 6.42 us  [body(): lax.all_to_all(jnp.broadcast_to(meta, (devices, meta.shape[1])), 'pair',...]
    all_to_all x1, starting transfers between devices: 18.8 us -> 7.28 us  [body(): lax.all_to_all(jnp.broadcast_to(meta, (devices, meta.shape[1])), 'pair',...]
    pallas_call x9 -> x12, Pallas kernels: 43 us -> 34.8 us  [the longest x3 13.9 us: product(): pl.pallas_call(functools.partial(product_kernel, groups, rows, edges, sta...]
    pallas_call x3, Pallas kernels: 6.1 us -> 0.18 us  [halve(): pl.pallas_call(halve_kernel, out_shape=(jax.ShapeDtypeStruct(shape, jnp.b...]
    pallas_call x3, Pallas kernels: 5.61 us -> 2.5 us  [finish(): pl.pallas_call(functools.partial(finish_kernel, row, column), out_shape=j...]
    unnamed x38, local copies, waits for them, and re-layouts: 9.62 us -> 7.68 us
    ppermute x15 -> x19, starting transfers between devices: 23.1 us -> 21.4 us  [swap(): return lax.ppermute(value, axis, [(i, i ^ apart) for i in range(size)])]
  transfers between devices with their start and end apart: 16 -> 20, of which waited for: 4 -> 11; matrix products, arithmetic and copies ran while one was open for 0% -> 0% of each run, Pallas kernels for 30% -> 19%
where the time goes in v1:
time: 166 us; the launch traced here: 165 us
  waiting for transfers between devices  84.7 us (51%)
  Pallas kernels  39.9 us (24%)
  starting transfers between devices  28.7 us (17%)
  local copies, waits for them, and re-layouts  9.07 us (5%)
  between operations  2.88 us (2%)
    ppermute x19, waiting for transfers between devices, swap(): return lax.ppermute(value, axis, [(i, i ^ apart) for i in range(size)])  78.3 us
    ppermute x19, starting transfers between devices, swap(): return lax.ppermute(value, axis, [(i, i ^ apart) for i in range(size)])  21.4 us
    pallas_call x3, Pallas kernels, product(): pl.pallas_call(functools.partial(product_kernel, groups, rows, edges, sta...  13.9 us
    unnamed x38, local copies, waits for them, and re-layouts  7.68 us
    all_to_all x1, starting transfers between devices, body(): lax.all_to_all(jnp.broadcast_to(meta, (devices, meta.shape[1])), 'pair',...  7.28 us
    pallas_call x2, Pallas kernels, combine(): pl.pallas_call(functools.partial(combine_kernel, start, len(lefts)), out_...  7 us
    all_to_all x1, waiting for transfers between devices, body(): lax.all_to_all(jnp.broadcast_to(meta, (devices, meta.shape[1])), 'pair',...  6.42 us
    pallas_call x2, Pallas kernels, pack(): pl.pallas_call(functools.partial(pack_kernel, first, start, rows, width),...  5.94 us
  transfers between devices with their start and end apart: 20, of which 11 were waited for; matrix products, arithmetic and copies ran while one was open for 0% of the time, Pallas kernels for 19%

profile of v1, /device:TPU:0, one launch (start us, length us, event | category | flops | bytes accessed | tf_op | source)
XLA Modules:
  0.0 165.3 jit_solution(56575755014958445)
XLA Ops:
  0.7 0.8 concatenate.5
  1.4 0.6 broadcast_in_dim.2
  2.0 7.3 %all-to-all-start = ((s32[8,1,13]{2,1,0:T(1,128)}), s32[8,1,13]{2,1,0:T(1,128)S(1)}, u32[]{:S(2)}, u32[]{:S(2)}) async-start(s32[8,1,13]{2,1,0:T(1,128)} %broadcast_in_dim.2), calls=%async_computation | async-start | bytes 8192 | tf_op jit(solution)/shard_map/all_to_all | solution.py:491
  9.3 6.4 %all-to-all-done = s32[8,1,13]{2,1,0:T(1,128)S(1)} async-done(((s32[8,1,13]{2,1,0:T(1,128)}), s32[8,1,13]{2,1,0:T(1,128)S(1)}, u32[]{:S(2)}, u32[]{:S(2)}) %all-to-all-start) | async-done | bytes 448 | tf_op jit(solution)/shard_map/all_to_all | solution.py:491
  15.7 0.6 copy-done.18
  16.3 1.7 %order.2 = (s32[17]{0:T(128)S(1)}, s32[17]{0:T(128)}, s32[17]{0:T(128)}, s32[17]{0:T(128)}, s32[1]{0:T(128)}) custom-call(s32[8,13]{1,0:T(8,128)} %bitcast.11), custom_call_target="tpu_custom_call" | custom-call | tf_op jit(solution)/shard_map/order/pallas_call | solution.py:73
  18.1 0.1 collective-permute-start.10
  18.2 0.5 collective-permute-start.8
  18.6 1.0 collective-permute-done.8
  20.9 2.9 %collective-permute-start.9 = (s32[1]{0:T(128)}, s32[1]{0:T(128)}, u32[]{:S(2)}, u32[]{:S(2)}) collective-permute-start(s32[1]{0:T(128)} %max.6), channel_id=1, source_target_pairs={{0,16},{8,24},{16,0},{24,8},{1,17},{9,25},{17,1},{25,9},{2,18},{10... | collective-permute-start | bytes 20 | tf_op jit(solution)/shard_map/ppermute | solution.py:25
  23.8 0.9 collective-permute-done.9
  25.3 0.0 collective-permute-done.10.metas
  25.3 0.0 copy-start.19
  25.3 0.6 copy-done.19
  25.9 1.7 %order.3 = (s32[17]{0:T(128)}, s32[17]{0:T(128)}, s32[17]{0:T(128)S(1)}, s32[17]{0:T(128)}, s32[1]{0:T(128)}) custom-call(s32[8,13]{1,0:T(8,128)} %copy-done.19), custom_call_target="tpu_custom_call" | custom-call | tf_op jit(solution)/shard_map/order/pallas_call | solution.py:73
  27.6 3.7 %slab.4 = bf16[12,128,768]{2,1,0:T(8,128)(2,1)} custom-call(s32[17]{0:T(128)S(1)} %get-tuple-element.66.order, bf16[16,128,1024]{2,1,0:T(8,128)(2,1)} %bitcast.6), custom_call_target="tpu_custom_call" | custom-call | bytes 4718592 | tf_op jit(solution)/shard_map/slab/pallas_call | solution.py:191
  31.4 0.0 copy-start.15
  31.4 0.1 collective-permute-start.11
  31.5 0.7 collective-permute-start.13
  32.1 4.0 %pack.5 = (bf16[2,12,96,128]{3,2,1,0:T(8,128)(2,1)S(1)}, bf16[2,12,96,128]{3,2,1,0:T(8,128)(2,1)S(1)}, bf16[2,12,96,128]{3,2,1,0:T(8,128)(2,1)S(1)}, bf16[2,12,96,128]{3,2,1,0:T(8,128)(2,1)}) custom-call(s32[17]{0:T(128)S(1)} %get-tuple-element.61.order, s32[1]{0:T(128)} %bitcast.2.me, bf16[16,128,1024]{2,1,0:T(8,128)(2,1)} %bitcast.8), custom_call_target="tpu_custom_call" | custom-call | bytes 4718592 | tf_op jit(solution)/shard_map/pack/pallas_call | solution.py:164
  36.1 0.6 collective-permute-start.17
  36.7 0.6 collective-permute-start.18
  37.3 3.2 %collective-permute-start.19 = (bf16[2,12,96,128]{3,2,1,0:T(8,128)(2,1)}, bf16[2,12,96,128]{3,2,1,0:T(8,128)(2,1)}, u32[]{:S(2)}, u32[]{:S(2)}) collective-permute-start(bf16[2,12,96,128]{3,2,1,0:T(8,128)(2,1)} %get-tuple-element.80), channel_id=1, source_target_pairs={{0,6},{1,7},{2,4},{3,5},{4,2},{5,3},{6,0},{7,1},{8,14},{9,15},{10,... | collective-permute-start | bytes 1769480 | tf_op jit(solution)/shard_map/ppermute | solution.py:25
  40.5 0.8 slab.5
  41.3 21.6 %collective-permute-done.17.refs_5_ = bf16[2,12,96,128]{3,2,1,0:T(8,128)(2,1)S(1)} collective-permute-done((bf16[2,12,96,128]{3,2,1,0:T(8,128)(2,1)S(1)}, bf16[2,12,96,128]{3,2,1,0:T(8,128)(2,1)S(1)}, u32[]{:S(2)}, u32[]{:S(2)}) %collective-permute-start.17) | collective-permute-done | bytes 589856 | tf_op jit(solution)/shard_map/ppermute | solution.py:25
  63.0 0.0 collective-permute-start.12
  63.0 16.2 %collective-permute-done.18.refs_6_ = bf16[2,12,96,128]{3,2,1,0:T(8,128)(2,1)S(1)} collective-permute-done((bf16[2,12,96,128]{3,2,1,0:T(8,128)(2,1)S(1)}, bf16[2,12,96,128]{3,2,1,0:T(8,128)(2,1)S(1)}, u32[]{:S(2)}, u32[]{:S(2)}) %collective-permute-start.18) | collective-permute-done | bytes 589856 | tf_op jit(solution)/shard_map/ppermute | solution.py:25
  79.1 0.8 copy-done
  79.9 0.0 collective-permute-start.14
  79.9 2.0 %pack.4 = (bf16[2,12,32,128]{3,2,1,0:T(8,128)(2,1)S(1)}, bf16[2,12,32,128]{3,2,1,0:T(8,128)(2,1)S(1)}, bf16[2,12,32,128]{3,2,1,0:T(8,128)(2,1)S(1)}, bf16[2,12,32,128]{3,2,1,0:T(8,128)(2,1)S(1)}) custom-call(s32[17]{0:T(128)S(1)} %get-tuple-element.61.order, s32[1]{0:T(128)} %bitcast.2.me, bf16[16,128,1024]{2,1,0:T(8,128)(2,1)S(1)} %bitcast.10), custom_call_target="tpu_custom_call" | custom-call | bytes 1572864 | tf_op jit(solution)/shard_map/pack/pallas_call | solution.py:164
  81.9 0.7 copy-done.2
  82.6 0.7 copy-done.10
  83.3 0.7 copy-done.12
  84.0 0.7 copy-done.14
  84.7 2.4 %plan.1 = (s32[25]{0:T(128)}, f32[25]{0:T(128)}, s32[65]{0:T(128)}) custom-call(s32[8,13]{1,0:T(8,128)} %bitcast.13, s32[17]{0:T(128)} %get-tuple-element.56.left_rank, s32[17]{0:T(128)} %get-tuple-element.57.right_rank, f32[8]{0:T(128)} %subduction.1), custom_call_target="tpu_custom_call" | custom-call | tf_op jit(solution)/shard_map/plan/pallas_call | solution.py:122
  87.1 4.2 %collective-permute-start.5 = (bf16[2,12,32,128]{3,2,1,0:T(8,128)(2,1)}, bf16[2,12,32,128]{3,2,1,0:T(8,128)(2,1)S(1)}, u32[]{:S(2)}, u32[]{:S(2)}) collective-permute-start(bf16[2,12,32,128]{3,2,1,0:T(8,128)(2,1)} %copy-done.14), channel_id=1, source_target_pairs={{0,2},{1,3},{2,0},{3,1},{4,6},{5,7},{6,4},{7,5},{8,10},{9,11},{10,... | collective-permute-start | bytes 589832 | tf_op jit(solution)/shard_map/ppermute | solution.py:25
  91.3 1.1 copy-done.1
  92.4 0.6 copy-done.4
  93.0 0.6 copy-done.6
  93.6 0.6 copy-done.8
  94.2 4.7 %combine.3.refs_0_ = bf16[768,4096]{1,0:T(8,128)(2,1)S(1)} custom-call(s32[25]{0:T(128)S(1)} %copy-done.4, f32[25]{0:T(128)S(1)} %copy-done.6, s32[65]{0:T(128)S(1)} %copy-done.8, s32[1]{0:T(128)} %get-tuple-element.55.refs_3_.more, bf16[2,12,96,128]{3,2,1,0:T(8,128)(2,1)S(1)} %get-tuple-element.77.refs_4_, ...), custom_call_target="tpu_custom_call" | custom-call | flops 12582912 | bytes 9437184 | tf_op jit(solution)/shard_map/combine/pallas_call | solution.py:326
  99.0 0.0 collective-permute-done.11.refs_1_
  99.0 6.5 %product.5 = (bf16[2,2,96,768]{3,2,1,0:T(8,128)(2,1)S(1)}, f32[2,2,96,768]{3,2,1,0:T(8,128)S(1)}) custom-call(s32[1]{0:T(128)} %get-tuple-element.55.refs_3_.more, bf16[768,4096]{1,0:T(8,128)(2,1)S(1)} %combine.3.refs_0_, bf16[12,128,768]{2,1,0:T(8,128)(2,1)} %collective-permute-done.11.refs_1_, ...), custom_call_target="tpu_custom_call" | custom-call | flops 4831838208 | bytes 12582912 | tf_op jit(solution)/shard_map/product/pallas_call | solution.py:399
  105.6 0.1 collective-permute-start.22
  105.7 2.0 %collective-permute-start.6 = (bf16[2,12,32,128]{3,2,1,0:T(8,128)(2,1)S(1)}, bf16[2,12,32,128]{3,2,1,0:T(8,128)(2,1)S(1)}, u32[]{:S(2)}, u32[]{:S(2)}) collective-permute-start(bf16[2,12,32,128]{3,2,1,0:T(8,128)(2,1)S(1)} %copy-done.13), channel_id=1, source_target_pairs={{0,4},{1,5},{2,6},{3,7},{4,0},{5,1},{6,2},{7,3},{8,12},{9,13},{10,... | collective-permute-start | bytes 589832 | tf_op jit(solution)/shard_map/ppermute | solution.py:25
  107.7 2.4 %collective-permute-start.7 = (bf16[2,12,32,128]{3,2,1,0:T(8,128)(2,1)S(1)}, bf16[2,12,32,128]{3,2,1,0:T(8,128)(2,1)S(1)}, u32[]{:S(2)}, u32[]{:S(2)}) collective-permute-start(bf16[2,12,32,128]{3,2,1,0:T(8,128)(2,1)S(1)} %copy-done.11), channel_id=1, source_target_pairs={{0,6},{1,7},{2,4},{3,5},{4,2},{5,3},{6,0},{7,1},{8,14},{9,15},{10,... | collective-permute-start | bytes 589832 | tf_op jit(solution)/shard_map/ppermute | solution.py:25
  110.0 13.5 %collective-permute-done.6.refs_6_ = bf16[2,12,32,128]{3,2,1,0:T(8,128)(2,1)S(1)} collective-permute-done((bf16[2,12,32,128]{3,2,1,0:T(8,128)(2,1)S(1)}, bf16[2,12,32,128]{3,2,1,0:T(8,128)(2,1)S(1)}, u32[]{:S(2)}, u32[]{:S(2)}) %collective-permute-start.6) | collective-permute-done | bytes 196640 | tf_op jit(solution)/shard_map/ppermute | solution.py:25
  123.6 4.4 %collective-permute-done.7.refs_7_ = bf16[2,12,32,128]{3,2,1,0:T(8,128)(2,1)S(1)} collective-permute-done((bf16[2,12,32,128]{3,2,1,0:T(8,128)(2,1)S(1)}, bf16[2,12,32,128]{3,2,1,0:T(8,128)(2,1)S(1)}, u32[]{:S(2)}, u32[]{:S(2)}) %collective-permute-start.7) | collective-permute-done | bytes 196640 | tf_op jit(solution)/shard_map/ppermute | solution.py:25
  128.0 2.3 %combine.2.refs_0_ = bf16[256,4096]{1,0:T(8,128)(2,1)S(1)} custom-call(s32[25]{0:T(128)S(1)} %copy-done.5, f32[25]{0:T(128)S(1)} %copy-done.7, s32[65]{0:T(128)S(1)} %copy-done.9, s32[1]{0:T(128)} %get-tuple-element.55.refs_3_.more, bf16[2,12,32,128]{3,2,1,0:T(8,128)(2,1)S(1)} %copy-done.3, bf16[2,12,32,128]{3,2,1,0:T(8,128)(2,1)S(1)} %collective-permute-done.5.refs_5_, ...), custom_call_target="tpu_custom_call" | custom-call | flops 4194304 | bytes 3145728 | tf_op jit(solution)/shard_map/combine/pallas_call | solution.py:326
  130.3 5.4 %product.3 = (bf16[2,2,32,1024]{3,2,1,0:T(8,128)(2,1)S(1)}, f32[2,2,32,1024]{3,2,1,0:T(8,128)S(1)}) custom-call(s32[1]{0:T(128)} %get-tuple-element.55.refs_3_.more, bf16[256,4096]{1,0:T(8,128)(2,1)S(1)} %combine.2.refs_0_, bf16[12,128,768]{2,1,0:T(8,128)(2,1)} %collective-permute-done.11.refs_1_, ...), custom_call_target="tpu_custom_call" | custom-call | flops 2147483648 | bytes 10485760 | tf_op jit(solution)/shard_map/product/pallas_call | solution.py:399
  135.7 0.1 collective-permute-start.15
  135.8 2.0 %product.4 = (bf16[2,2,96,256]{3,2,1,0:T(8,128)(2,1)S(1)}, f32[2,2,96,256]{3,2,1,0:T(8,128)S(1)}) custom-call(s32[1]{0:T(128)} %get-tuple-element.55.refs_3_.more, bf16[768,4096]{1,0:T(8,128)(2,1)S(1)} %combine.3.refs_0_, bf16[12,128,256]{2,1,0:T(8,128)(2,1)S(1)} %collective-permute-done.12.refs_2_.refs_1_, ...), custom_call_target="tpu_custom_call" | custom-call | flops 1610612736 | bytes 8388608 | tf_op jit(solution)/shard_map/product/pallas_call | solution.py:399
  137.8 2.1 %collective-permute-start.20 = (bf16[2,2,96,256]{3,2,1,0:T(8,128)(2,1)S(1)}, bf16[2,2,96,256]{3,2,1,0:T(8,128)(2,1)S(1)}, u32[]{:S(2)}, u32[]{:S(2)}) collective-permute-start(bf16[2,2,96,256]{3,2,1,0:T(8,128)(2,1)S(1)} %get-tuple-element.82), channel_id=1, source_target_pairs={{0,2},{1,3},{2,0},{3,1},{4,6},{5,7},{6,4},{7,5},{8,10},{9,11},{10,... | collective-permute-start | bytes 589832 | tf_op jit(solution)/shard_map/ppermute | solution.py:25
  139.9 0.1 halve.5
  140.0 0.9 collective-permute-start.23
  140.9 9.3 %collective-permute-done.15.came = bf16[2,2,32,1024]{3,2,1,0:T(8,128)(2,1)S(1)} collective-permute-done((bf16[2,2,32,1024]{3,2,1,0:T(8,128)(2,1)S(1)}, bf16[2,2,32,1024]{3,2,1,0:T(8,128)(2,1)S(1)}, u32[]{:S(2)}, u32[]{:S(2)}) %collective-permute-start.15) | collective-permute-done | bytes 262176 | tf_op jit(solution)/shard_map/ppermute | solution.py:25
  150.2 0.1 collective-permute-start.16
  150.3 2.0 %collective-permute-done.20.came = bf16[2,2,96,256]{3,2,1,0:T(8,128)(2,1)S(1)} collective-permute-done((bf16[2,2,96,256]{3,2,1,0:T(8,128)(2,1)S(1)}, bf16[2,2,96,256]{3,2,1,0:T(8,128)(2,1)S(1)}, u32[]{:S(2)}, u32[]{:S(2)}) %collective-permute-start.20) | collective-permute-done | bytes 196640 | tf_op jit(solution)/shard_map/ppermute | solution.py:25
  152.3 1.0 collective-permute-start.21
  153.3 8.0 %collective-permute-done.23.came = bf16[1,2,96,768]{3,2,1,0:T(8,128)(2,1)S(1)} collective-permute-done((bf16[1,2,96,768]{3,2,1,0:T(8,128)(2,1)S(1)}, bf16[1,2,96,768]{3,2,1,0:T(8,128)(2,1)S(1)}, u32[]{:S(2)}, u32[]{:S(2)}) %collective-permute-start.23) | collective-permute-done | bytes 294944 | tf_op jit(solution)/shard_map/ppermute | solution.py:25
  161.3 1.0 finish.3.refs_0_
  162.3 1.5 collective-permute-done.21.came
  163.7 0.8 finish.4.refs_0_
  164.5 0.8 finish.5
  (36 shorter events, 0.2 us)
Async XLA Ops:
  2.0 13.7 %all-to-all-start = ((s32[8,1,13]{2,1,0:T(1,128)}), s32[8,1,13]{2,1,0:T(1,128)S(1)}, u32[]{:S(2)}, u32[]{:S(2)}) async-start(s32[8,1,13]{2,1,0:T(1,128)} %broadcast_in_dim.2), calls=%async_computation | async-start | bytes 8192 | tf_op jit(solution)/shard_map/all_to_all | solution.py:491
  15.7 0.6 copy-start.18
  18.1 7.2 %collective-permute-start.10 = (s32[8,13]{1,0:T(8,128)}, s32[8,13]{1,0:T(8,128)S(1)}, u32[]{:S(2)}, u32[]{:S(2)}) collective-permute-start(s32[8,13]{1,0:T(8,128)} %bitcast.12), channel_id=1, source_target_pairs={{0,8},{8,0},{16,24},{24,16},{1,9},{9,1},{17,25},{25,17},{2,10},{10... | collective-permute-start | bytes 1256 | tf_op jit(solution)/shard_map/ppermute | solution.py:25
  18.2 1.5 collective-permute-start.8
  20.9 3.7 %collective-permute-start.9 = (s32[1]{0:T(128)}, s32[1]{0:T(128)}, u32[]{:S(2)}, u32[]{:S(2)}) collective-permute-start(s32[1]{0:T(128)} %max.6), channel_id=1, source_target_pairs={{0,16},{8,24},{16,0},{24,8},{1,17},{9,25},{17,1},{25,9},{2,18},{10... | collective-permute-start | bytes 20 | tf_op jit(solution)/shard_map/ppermute | solution.py:25
  25.3 0.6 copy-start.19
  31.4 9.2 %copy-start.15 = (bf16[1,16,128,1024]{3,2,1,0:T(8,128)(2,1)S(1)}, bf16[1,16,128,1024]{3,2,1,0:T(8,128)(2,1)}, u32[]{:S(2)}) copy-start(bf16[1,16,128,1024]{3,2,1,0:T(8,128)(2,1)} %param.9) | copy-start | bytes 12582916
  31.4 67.6 %collective-permute-start.11 = (bf16[12,128,768]{2,1,0:T(8,128)(2,1)}, bf16[12,128,768]{2,1,0:T(8,128)(2,1)}, u32[]{:S(2)}, u32[]{:S(2)}) collective-permute-start(bf16[12,128,768]{2,1,0:T(8,128)(2,1)} %slab.4), channel_id=1, source_target_pairs={{0,8},{8,0},{16,24},{24,16},{1,9},{9,1},{17,25},{25,17},{2,10},{10... | collective-permute-start | bytes 7077896 | tf_op jit(solution)/shard_map/ppermute | solution.py:25
  31.5 67.5 %collective-permute-start.13 = (bf16[12,128,768]{2,1,0:T(8,128)(2,1)}, bf16[12,128,768]{2,1,0:T(8,128)(2,1)}, u32[]{:S(2)}, u32[]{:S(2)}) collective-permute-start(bf16[12,128,768]{2,1,0:T(8,128)(2,1)} %slab.4), channel_id=1, source_target_pairs={{0,9},{1,8},{2,11},{3,10},{4,13},{5,12},{6,15},{7,14},{8,1},{9,0},... | collective-permute-start | bytes 7077896 | tf_op jit(solution)/shard_map/ppermute | solution.py:25
  36.1 26.9 %collective-permute-start.17 = (bf16[2,12,96,128]{3,2,1,0:T(8,128)(2,1)S(1)}, bf16[2,12,96,128]{3,2,1,0:T(8,128)(2,1)S(1)}, u32[]{:S(2)}, u32[]{:S(2)}) collective-permute-start(bf16[2,12,96,128]{3,2,1,0:T(8,128)(2,1)S(1)} %get-tuple-element.78), channel_id=1, source_target_pairs={{0,2},{1,3},{2,0},{3,1},{4,6},{5,7},{6,4},{7,5},{8,10},{9,11},{10,... | collective-permute-start | bytes 1769480 | tf_op jit(solution)/shard_map/ppermute | solution.py:25
  36.7 42.4 %collective-permute-start.18 = (bf16[2,12,96,128]{3,2,1,0:T(8,128)(2,1)S(1)}, bf16[2,12,96,128]{3,2,1,0:T(8,128)(2,1)S(1)}, u32[]{:S(2)}, u32[]{:S(2)}) collective-permute-start(bf16[2,12,96,128]{3,2,1,0:T(8,128)(2,1)S(1)} %get-tuple-element.79), channel_id=1, source_target_pairs={{0,4},{1,5},{2,6},{3,7},{4,0},{5,1},{6,2},{7,3},{8,12},{9,13},{10,... | collective-permute-start | bytes 1769480 | tf_op jit(solution)/shard_map/ppermute | solution.py:25
  37.3 49.8 %collective-permute-start.19 = (bf16[2,12,96,128]{3,2,1,0:T(8,128)(2,1)}, bf16[2,12,96,128]{3,2,1,0:T(8,128)(2,1)}, u32[]{:S(2)}, u32[]{:S(2)}) collective-permute-start(bf16[2,12,96,128]{3,2,1,0:T(8,128)(2,1)} %get-tuple-element.80), channel_id=1, source_target_pairs={{0,6},{1,7},{2,4},{3,5},{4,2},{5,3},{6,0},{7,1},{8,14},{9,15},{10,... | collective-permute-start | bytes 1769480 | tf_op jit(solution)/shard_map/ppermute | solution.py:25
  63.0 67.4 %collective-permute-start.12 = (bf16[12,128,256]{2,1,0:T(8,128)(2,1)S(1)}, bf16[12,128,256]{2,1,0:T(8,128)(2,1)S(1)}, u32[]{:S(2)}, u32[]{:S(2)}) collective-permute-start(bf16[12,128,256]{2,1,0:T(8,128)(2,1)S(1)} %slab.5), channel_id=1, source_target_pairs={{0,8},{8,0},{16,24},{24,16},{1,9},{9,1},{17,25},{25,17},{2,10},{10... | collective-permute-start | bytes 2359304 | tf_op jit(solution)/shard_map/ppermute | solution.py:25
  79.1 0.8 copy-start
  79.9 50.4 %collective-permute-start.14 = (bf16[12,128,256]{2,1,0:T(8,128)(2,1)S(1)}, bf16[12,128,256]{2,1,0:T(8,128)(2,1)S(1)}, u32[]{:S(2)}, u32[]{:S(2)}) collective-permute-start(bf16[12,128,256]{2,1,0:T(8,128)(2,1)S(1)} %slab.5), channel_id=1, source_target_pairs={{0,9},{1,8},{2,11},{3,10},{4,13},{5,12},{6,15},{7,14},{8,1},{9,0},... | collective-permute-start | bytes 2359304 | tf_op jit(solution)/shard_map/ppermute | solution.py:25
  81.9 0.7 copy-start.2
  82.6 0.7 copy-start.10
  83.3 0.7 copy-start.12
  84.0 0.7 copy-start.14
  87.1 20.6 %collective-permute-start.5 = (bf16[2,12,32,128]{3,2,1,0:T(8,128)(2,1)}, bf16[2,12,32,128]{3,2,1,0:T(8,128)(2,1)S(1)}, u32[]{:S(2)}, u32[]{:S(2)}) collective-permute-start(bf16[2,12,32,128]{3,2,1,0:T(8,128)(2,1)} %copy-done.14), channel_id=1, source_target_pairs={{0,2},{1,3},{2,0},{3,1},{4,6},{5,7},{6,4},{7,5},{8,10},{9,11},{10,... | collective-permute-start | bytes 589832 | tf_op jit(solution)/shard_map/ppermute | solution.py:25
  91.3 1.1 copy-start.1
  92.4 0.6 copy-start.4
  93.0 0.6 copy-start.6
  93.6 0.6 copy-start.8
  99.0 6.7 %copy-start.13 = (bf16[2,12,32,128]{3,2,1,0:T(8,128)(2,1)S(1)}, bf16[2,12,32,128]{3,2,1,0:T(8,128)(2,1)}, u32[]{:S(2)}) copy-start(bf16[2,12,32,128]{3,2,1,0:T(8,128)(2,1)} %copy-done.12) | copy-start | bytes 589828
  99.0 8.7 %copy-start.11 = (bf16[2,12,32,128]{3,2,1,0:T(8,128)(2,1)S(1)}, bf16[2,12,32,128]{3,2,1,0:T(8,128)(2,1)}, u32[]{:S(2)}) copy-start(bf16[2,12,32,128]{3,2,1,0:T(8,128)(2,1)} %copy-done.10) | copy-start | bytes 589828
  99.0 29.0 %copy-start.3 = (bf16[2,12,32,128]{3,2,1,0:T(8,128)(2,1)S(1)}, bf16[2,12,32,128]{3,2,1,0:T(8,128)(2,1)}, u32[]{:S(2)}) copy-start(bf16[2,12,32,128]{3,2,1,0:T(8,128)(2,1)} %copy-done.2) | copy-start | bytes 589828
  99.0 29.0 %copy-start.5 = (s32[25]{0:T(128)S(1)}, s32[25]{0:T(128)}, u32[]{:S(2)}) copy-start(s32[25]{0:T(128)} %get-tuple-element.58.refs_0_) | copy-start | bytes 304
  99.0 29.0 %copy-start.7 = (f32[25]{0:T(128)S(1)}, f32[25]{0:T(128)}, u32[]{:S(2)}) copy-start(f32[25]{0:T(128)} %get-tuple-element.59.refs_1_) | copy-start | bytes 304
  99.0 29.0 %copy-start.9 = (s32[65]{0:T(128)S(1)}, s32[65]{0:T(128)}, u32[]{:S(2)}) copy-start(s32[65]{0:T(128)} %get-tuple-element.60.refs_2_) | copy-start | bytes 784
  99.0 29.0 %copy-start.17 = (bf16[2,4,128,128]{3,2,1,0:T(8,128)(2,1)S(1)}, bf16[2,4,128,128]{3,2,1,0:T(8,128)(2,1)}, u32[]{:S(2)}) copy-start(bf16[2,4,128,128]{3,2,1,0:T(8,128)(2,1)} %get-tuple-element.67.refs_8_) | copy-start | bytes 786436
  105.6 34.3 %collective-permute-start.22 = (bf16[2,2,96,768]{3,2,1,0:T(8,128)(2,1)S(1)}, bf16[2,2,96,768]{3,2,1,0:T(8,128)(2,1)S(1)}, u32[]{:S(2)}, u32[]{:S(2)}) collective-permute-start(bf16[2,2,96,768]{3,2,1,0:T(8,128)(2,1)S(1)} %get-tuple-element.86), channel_id=1, source_target_pairs={{0,2},{1,3},{2,0},{3,1},{4,6},{5,7},{6,4},{7,5},{8,10},{9,11},{10,... | collective-permute-start | bytes 1769480 | tf_op jit(solution)/shard_map/ppermute | solution.py:25
  105.7 17.9 %collective-permute-start.6 = (bf16[2,12,32,128]{3,2,1,0:T(8,128)(2,1)S(1)}, bf16[2,12,32,128]{3,2,1,0:T(8,128)(2,1)S(1)}, u32[]{:S(2)}, u32[]{:S(2)}) collective-permute-start(bf16[2,12,32,128]{3,2,1,0:T(8,128)(2,1)S(1)} %copy-done.13), channel_id=1, source_target_pairs={{0,4},{1,5},{2,6},{3,7},{4,0},{5,1},{6,2},{7,3},{8,12},{9,13},{10,... | collective-permute-start | bytes 589832 | tf_op jit(solution)/shard_map/ppermute | solution.py:25
  107.7 20.3 %collective-permute-start.7 = (bf16[2,12,32,128]{3,2,1,0:T(8,128)(2,1)S(1)}, bf16[2,12,32,128]{3,2,1,0:T(8,128)(2,1)S(1)}, u32[]{:S(2)}, u32[]{:S(2)}) collective-permute-start(bf16[2,12,32,128]{3,2,1,0:T(8,128)(2,1)S(1)} %copy-done.11), channel_id=1, source_target_pairs={{0,6},{1,7},{2,4},{3,5},{4,2},{5,3},{6,0},{7,1},{8,14},{9,15},{10,... | collective-permute-start | bytes 589832 | tf_op jit(solution)/shard_map/ppermute | solution.py:25
  135.7 14.4 %collective-permute-start.15 = (bf16[2,2,32,1024]{3,2,1,0:T(8,128)(2,1)S(1)}, bf16[2,2,32,1024]{3,2,1,0:T(8,128)(2,1)S(1)}, u32[]{:S(2)}, u32[]{:S(2)}) collective-permute-start(bf16[2,2,32,1024]{3,2,1,0:T(8,128)(2,1)S(1)} %get-tuple-element.74), channel_id=1, source_target_pairs={{0,2},{1,3},{2,0},{3,1},{4,6},{5,7},{6,4},{7,5},{8,10},{9,11},{10,... | collective-permute-start | bytes 786440 | tf_op jit(solution)/shard_map/ppermute | solution.py:25
  137.8 14.4 %collective-permute-start.20 = (bf16[2,2,96,256]{3,2,1,0:T(8,128)(2,1)S(1)}, bf16[2,2,96,256]{3,2,1,0:T(8,128)(2,1)S(1)}, u32[]{:S(2)}, u32[]{:S(2)}) collective-permute-start(bf16[2,2,96,256]{3,2,1,0:T(8,128)(2,1)S(1)} %get-tuple-element.82), channel_id=1, source_target_pairs={{0,2},{1,3},{2,0},{3,1},{4,6},{5,7},{6,4},{7,5},{8,10},{9,11},{10,... | collective-permute-start | bytes 589832 | tf_op jit(solution)/shard_map/ppermute | solution.py:25
  140.0 21.3 %collective-permute-start.23 = (bf16[1,2,96,768]{3,2,1,0:T(8,128)(2,1)S(1)}, bf16[1,2,96,768]{3,2,1,0:T(8,128)(2,1)S(1)}, u32[]{:S(2)}, u32[]{:S(2)}) collective-permute-start(bf16[1,2,96,768]{3,2,1,0:T(8,128)(2,1)S(1)} %get-tuple-element.88), channel_id=1, source_target_pairs={{0,4},{1,5},{2,6},{3,7},{4,0},{5,1},{6,2},{7,3},{8,12},{9,13},{10,... | collective-permute-start | bytes 884744 | tf_op jit(solution)/shard_map/ppermute | solution.py:25
  150.2 14.3 %collective-permute-start.16 = (bf16[1,2,32,1024]{3,2,1,0:T(8,128)(2,1)S(1)}, bf16[1,2,32,1024]{3,2,1,0:T(8,128)(2,1)S(1)}, u32[]{:S(2)}, u32[]{:S(2)}) collective-permute-start(bf16[1,2,32,1024]{3,2,1,0:T(8,128)(2,1)S(1)} %get-tuple-element.76), channel_id=1, source_target_pairs={{0,4},{1,5},{2,6},{3,7},{4,0},{5,1},{6,2},{7,3},{8,12},{9,13},{10,... | collective-permute-start | bytes 393224 | tf_op jit(solution)/shard_map/ppermute | solution.py:25
  152.3 11.5 %collective-permute-start.21 = (bf16[1,2,96,256]{3,2,1,0:T(8,128)(2,1)S(1)}, bf16[1,2,96,256]{3,2,1,0:T(8,128)(2,1)S(1)}, u32[]{:S(2)}, u32[]{:S(2)}) collective-permute-start(bf16[1,2,96,256]{3,2,1,0:T(8,128)(2,1)S(1)} %get-tuple-element.84), channel_id=1, source_target_pairs={{0,4},{1,5},{2,6},{3,7},{4,0},{5,1},{6,2},{7,3},{8,12},{9,13},{10,... | collective-permute-start | bytes 294920 | tf_op jit(solution)/shard_map/ppermute | solution.py:25

commit v2 on v1

--- a/solution.py
+++ b/solution.py
@@ -10,8 +10,9 @@
 SLICES = 2
 SUBLANES = 16
 LANES = 128
-ROW_PARTS = (6, 2)
-COLUMN_PARTS = (3, 1)
+ROW_PARTS = (1, 5, 2)
+COLUMN_PARTS = (1, 2, 1)
+HALVES = (True, True, False)
 
 
 def cut(length, unit, parts):
@@ -30,7 +31,7 @@
 
 
 def base_count(families):
-    return families - families // 4
+    return families - 3 * families // 16
 
 
 def slot_fields(metas):
@@ -133,12 +134,18 @@
     )(metas, left_rank, right_rank, subduction)
 
 
-def pack_kernel(first, start, rows, width, order, me, own, *refs):
-    outs, sem = refs[:-1], refs[-1]
+def pack_kernel(first, start, rows, width, *refs):
+    order, refs = (None, refs) if first is None else (refs[0], refs[1:])
+    me, own, outs, sem = refs[0], refs[1], refs[2:-1], refs[-1]
     copies = []
     for group, out in enumerate(outs):
         for half in range(2):
             column = pl.multiple_of((me[0] ^ (2 * group + half)) * width, width)
+            if order is None:
+                source = own.at[:, pl.ds(start, rows), pl.ds(column, width)]
+                at = sem.at[2 * group + half]
+                copies.append(pltpu.make_async_copy(source, out.at[half], at))
+                continue
             for i in range(out.shape[1]):
                 source = own.at[order[first + i], pl.ds(start, rows), pl.ds(column, width)]
                 at = (2 * group + half) * out.shape[1] + i
@@ -151,7 +158,9 @@
 
 def pack(own, order, me, first, number, start, rows, width, groups):
     if width % LANES:
-        blocks = jnp.take(own, order[first : first + number], axis=0)
+        blocks = own
+        if order is not None:
+            blocks = jnp.take(own, order[first : first + number], axis=0)
 
         def columns(offset):
             at = (0, start, (me[0] ^ offset) * width)
@@ -161,10 +170,11 @@
             jnp.stack([columns(2 * group), columns(2 * group + 1)]) for group in range(groups)
         ]
     piece = jax.ShapeDtypeStruct((2, number, rows, width), own.dtype)
-    return pl.pallas_call(
-        functools.partial(pack_kernel, first, start, rows, width),
+    orders = [] if order is None else [order]
+    return pl.pallas_call(
+        functools.partial(pack_kernel, first if orders else None, start, rows, width),
         out_shape=[piece] * groups,
-        in_specs=[spec(pltpu.SMEM)] * 2 + [spec(pl.ANY)],
+        in_specs=[spec(pltpu.SMEM)] * (1 + len(orders)) + [spec(pl.ANY)],
         out_specs=[spec()] * groups,
         scratch_shapes=[pltpu.SemaphoreType.DMA((2 * groups * number,))],
         cost_estimate=pl.CostEstimate(
@@ -172,11 +182,18 @@
         ),
         compiler_params=pltpu.CompilerParams(vmem_limit_bytes=8 << 20),
         name="pack",
-    )(order, me, own)
-
-
-def slab_kernel(first, start, order, own, out, sem):
-    copies = []
+    )(*orders, me, own)
+
+
+def slab_kernel(first, start, *refs):
+    own, out, sem = refs[-3:]
+    if first is None:
+        whole = own.at[:, :, pl.ds(start, out.shape[2])]
+        copy = pltpu.make_async_copy(whole, out, sem.at[0])
+        copy.start()
+        copy.wait()
+        return
+    order, copies = refs[0], []
     for i in range(out.shape[0]):
         source = own.at[order[first + i], :, pl.ds(start, out.shape[2])]
         copies.append(pltpu.make_async_copy(source, out.at[i], sem.at[i]))
@@ -188,10 +205,11 @@
 
 def slab(own, order, first, number, start, columns):
     shape = (number, own.shape[1], columns)
-    return pl.pallas_call(
-        functools.partial(slab_kernel, first, start),
+    orders = [] if order is None else [order]
+    return pl.pallas_call(
+        functools.partial(slab_kernel, first if orders else None, start),
         out_shape=jax.ShapeDtypeStruct(shape, own.dtype),
-        in_specs=[spec(pltpu.SMEM), spec(pl.ANY)],
+        in_specs=[spec(pltpu.SMEM)] * len(orders) + [spec(pl.ANY)],
         out_specs=spec(),
         scratch_shapes=[pltpu.SemaphoreType.DMA((number,))],
         cost_estimate=pl.CostEstimate(
@@ -199,7 +217,43 @@
         ),
         compiler_params=pltpu.CompilerParams(vmem_limit_bytes=8 << 20),
         name="slab",
-    )(order, own)
+    )(*orders, own)
+
+
+def pick_kernel(order, *refs):
+    count = len(refs) // 2
+    whole, outs, sem = refs[:count], refs[count:-1], refs[-1]
+    number = outs[0].shape[1]
+    copies = []
+    for j, (source, out) in enumerate(zip(whole, outs)):
+        for i in range(number):
+            piece = source.at[:, pl.ds(order[i], 1)]
+            copies.append(
+                pltpu.make_async_copy(piece, out.at[:, pl.ds(i, 1)], sem.at[j * number + i])
+            )
+    for copy in copies:
+        copy.start()
+    for copy in copies:
+        copy.wait()
+
+
+def pick(order, number, *whole):
+    shapes = [
+        jax.ShapeDtypeStruct((piece.shape[0], number) + piece.shape[2:], piece.dtype)
+        for piece in whole
+    ]
+    return pl.pallas_call(
+        pick_kernel,
+        out_shape=shapes,
+        in_specs=[spec(pltpu.SMEM)] + [spec(pl.ANY)] * len(whole),
+        out_specs=[spec()] * len(whole),
+        scratch_shapes=[pltpu.SemaphoreType.DMA((number * len(whole),))],
+        compiler_params=pltpu.CompilerParams(vmem_limit_bytes=8 << 20),
+        cost_estimate=pl.CostEstimate(
+            flops=0, transcendentals=0, bytes_accessed=4 * sum(piece.size for piece in whole)
+        ),
+        name="pick",
+    )(order, *whole)
 
 
 def unset(shapes):
@@ -340,10 +394,10 @@
     )(*table, more, *lefts, *lates)
 
 
-def product_kernel(groups, chunks, edges, start, more, *refs):
+def product_kernel(groups, chunks, edges, start, halves, more, *refs):
     combined, refs = refs[: len(chunks)], refs[len(chunks) :]
-    nears, fars, refs = refs[: len(edges)], refs[len(edges) : 2 * len(edges)], refs[-7:]
-    lates, (send, keep), held, sems = refs[:2], refs[2:4], refs[4:6], refs[6]
+    nears, fars, refs = refs[: len(edges)], refs[len(edges) : 2 * len(edges)], refs[2 * len(edges) :]
+    lates, outs, held, sems = refs[:2], refs[2:-3], refs[-3:-1], refs[-1]
     _, width, tile = nears[0].shape
     step = pl.program_id(0)
     columns = pl.ds(pl.multiple_of(start + step * tile, tile), tile)
@@ -366,10 +420,11 @@
             for i in range(SLICES * groups):
                 t, group = divmod(i, groups)
                 piece = total[i * rows : (i + 1) * rows]
-                if group % 2:
-                    send[group // 2, t, top : top + rows] = piece.astype(send.dtype)
+                if halves:
+                    out, at = outs[1 - group % 2], group // 2
                 else:
-                    keep[group // 2, t, top : top + rows] = piece
+                    out, at = outs[group - 1], 0
+                out[at, t, top : top + rows] = piece.astype(out.dtype)
             top += rows
 
     for near, far, (lo, hi) in zip(nears, fars, edges):
@@ -380,7 +435,7 @@
         pl.when(here & (more[0] > 0))(full)
 
 
-def product(more, combined, nears, fars, lates, start, groups):
+def product(halves, more, combined, nears, fars, lates, start, groups):
     base, width, _ = nears[0].shape
     late = lates[0].shape[0]
     rows = [chunk.shape[0] // (SLICES * groups) for chunk in combined]
@@ -394,15 +449,14 @@
     def place(lo, hi):
         return lambda i: (0, 0, jnp.clip(i - lo, 0, hi - lo - 1))
 
-    shape = (groups // 2, SLICES, sum(rows), columns)
-    block = pl.BlockSpec((groups // 2, SLICES, sum(rows), tile), lambda i: (0, 0, 0, i))
-    return pl.pallas_call(
-        functools.partial(product_kernel, groups, rows, edges, start),
+    kept, sends = (groups // 2, 1) if halves else (1, groups - 1)
+    shape = (kept, SLICES, sum(rows), columns)
+    block = pl.BlockSpec((kept, SLICES, sum(rows), tile), lambda i: (0, 0, 0, i))
+    return pl.pallas_call(
+        functools.partial(product_kernel, groups, rows, edges, start, halves),
         grid=(columns // tile,),
-        out_shape=(
-            jax.ShapeDtypeStruct(shape, jnp.bfloat16),
-            jax.ShapeDtypeStruct(shape, jnp.float32),
-        ),
+        out_shape=[jax.ShapeDtypeStruct(shape, jnp.bfloat16)] * sends
+        + [jax.ShapeDtypeStruct(shape, jnp.float32)],
         in_specs=[spec(pltpu.SMEM)]
         + [
             pl.BlockSpec(chunk.shape, lambda i: (0, 0), pipeline_mode=pl.Buffered(1))
@@ -410,7 +464,7 @@
         ]
         + [pl.BlockSpec((base, width, tile), place(lo, hi)) for lo, hi in edges] * 2
         + [spec(pl.ANY)] * 2,
-        out_specs=(block, block),
+        out_specs=[block] * (sends + 1),
         scratch_shapes=[pltpu.VMEM((late, width, tile), jnp.bfloat16)] * 2
         + [pltpu.SemaphoreType.DMA((2,))],
         compiler_params=pltpu.CompilerParams(vmem_limit_bytes=24 << 20),
@@ -449,36 +503,39 @@
     )(keep, came)
 
 
-def finish_kernel(row, column, keep, came, *refs):
-    out, buffer, sem = refs[-3:]
+def finish_kernel(row, column, count, keep, *refs):
+    cames, (out, buffer, sem) = refs[:count], refs[-3:]
     rows, _, columns = buffer.shape
     for t in range(SLICES):
-        buffer[:, t, :] = keep[0, t] + came[0, t].astype(jnp.float32)
+        total = keep[0, t]
+        for came in cames:
+            total = total + came[0, t].astype(jnp.float32)
+        buffer[:, t, :] = total
     target = out.at[pl.ds(row, rows), :, pl.ds(column, columns)]
     copy = pltpu.make_async_copy(buffer, target, sem)
     copy.start()
     copy.wait()
 
 
-def finish(keep, came, row, column, rows, order, result):
+def finish(keep, cames, row, column, rows, order, result):
     here, columns = keep.shape[2:]
     before = [] if result is None else [result]
     return pl.pallas_call(
-        functools.partial(finish_kernel, row, column),
+        functools.partial(finish_kernel, row, column, len(cames)),
         out_shape=jax.ShapeDtypeStruct((rows, SLICES, order), jnp.float32),
-        in_specs=[spec()] * 2 + [spec(pl.ANY)] * len(before),
+        in_specs=[spec()] * (1 + len(cames)) + [spec(pl.ANY)] * len(before),
         out_specs=spec(pl.ANY),
         scratch_shapes=[
             pltpu.VMEM((here, SLICES, columns), jnp.float32),
             pltpu.SemaphoreType.DMA,
         ],
-        input_output_aliases={2: 0} if before else {},
+        input_output_aliases={1 + len(cames): 0} if before else {},
         cost_estimate=pl.CostEstimate(
             flops=keep.size, transcendentals=0, bytes_accessed=10 * keep.size
         ),
         compiler_params=pltpu.CompilerParams(vmem_limit_bytes=8 << 20),
         name="finish",
-    )(keep, came, *before)
+    )(keep, *cames, *before)
 
 
 def body(blocks, left_ids, right_ids, slice_ids, weight_ids, counts, subduction):
@@ -492,22 +549,32 @@
         jnp.broadcast_to(meta, (devices, meta.shape[1])), "pair", 0, 0, tiled=True
     )
     partner = swap(metas, "mom", 1)
-    left_order, left_rank, _, right_rank, more = order_blocks(metas, families)
+    left_order, left_rank, needed, right_rank, more = order_blocks(metas, families)
     right_order = order_blocks(partner, families)[2]
     base = base_count(families)
     row_cuts = cut(rows, SUBLANES, ROW_PARTS)
     column_cuts = cut(order, 2 * LANES, COLUMN_PARTS)
     arrived, nears, fars = [], [], []
-    for start, here in row_cuts:
+    for i, (start, here) in enumerate(row_cuts):
+        chosen, number = (left_order, base) if i else (None, families)
         pieces = pack(
-            own, left_order, me, 0, base, start, here, width, groups
+            own, chosen, me, 0, number, start, here, width, groups
         )
         moved = [swap(pieces[group], "pair", 2 * group) for group in range(groups - 1, 0, -1)]
-        arrived.append([pieces[0]] + moved[::-1])
-    for start, columns in column_cuts:
-        mine = slab(own, right_order, 0, base, start, columns)
-        fars.append(swap(mine, ("mom", "pair"), devices + 1))
-        nears.append(swap(mine, "mom", 1))
+        pieces = [pieces[0]] + moved[::-1]
+        if not i:
+            pieces = list(pick(left_order, base, *pieces))
+        arrived.append(pieces)
+    for i, (start, columns) in enumerate(column_cuts):
+        chosen, number = (right_order, base) if i else (None, families)
+        mine = slab(own, chosen, 0, number, start, columns)
+        far = swap(mine, ("mom", "pair"), devices + 1)
+        near = swap(mine, "mom", 1)
+        if not i:
+            near, far = pick(needed, base, near[None], far[None])
+            near, far = near[0], far[0]
+        fars.append(far)
+        nears.append(near)
     anywhere = more
     for bit in range(lax.axis_size("mom").bit_length() - 1):
         anywhere = jnp.maximum(anywhere, swap(anywhere, "mom", 1 << bit))
@@ -516,15 +583,16 @@
     )
     table = plan(metas, left_rank, right_rank, subduction, families)
     last, columns = len(row_cuts) - 1, range(len(column_cuts))
-    jobs = [(range(last), [j]) for j in columns] + [([last], columns)]
+    jobs = [(range(last), columns[:-1]), (range(last), columns[-1:]), ([last], columns)]
     combined = [
         combine(table, more, lefts, late_lefts, row_cuts[i][0])
         for i, lefts in enumerate(arrived)
     ]
     result = None
-    for chunks, parts in jobs:
+    for k, (chunks, parts) in enumerate(jobs):
         row, column = row_cuts[chunks[0]][0], column_cuts[parts[0]][0]
-        send, keep = product(
+        halves = HALVES[k]
+        *sends, keep = functools.partial(product, halves)(
             more,
             [combined[i] for i in chunks],
             [nears[j] for j in parts],
@@ -533,13 +601,19 @@
             column,
             groups,
         )
-        apart = 1
-        while 2 * apart < groups:
-            came = swap(send, "pair", 2 * apart)
-            send, keep = halve(keep, came)
+        apart, steps = 1, [0] * (groups.bit_length() - 2) if halves else []
+        for _ in steps:
+            came = swap(sends[0], "pair", 2 * apart)
+            *sends, keep = halve(keep, came)
             apart *= 2
-        came = swap(send, "pair", 2 * apart)
-        result = finish(keep, came, row, column, rows, order, result)
+        if halves:
+            cames = [swap(sends[0], "pair", 2 * apart)]
+        else:
+            cames = [
+                swap(sends[group - 1], "pair", 2 * group)
+                for group in range(groups - 1, 0, -1)
+            ]
+        result = finish(keep, cames, row, column, rows, order, result)
     return result.reshape((1,) + result.shape)
 
 

time: 166 us -> 199 us (1.20)
  starting transfers between devices: 28.7 us -> 43.2 us
  waiting for transfers between devices: 84.7 us -> 97.4 us
  Pallas kernels: 39.9 us -> 47.9 us
  local copies, waits for them, and re-layouts: 9.07 us -> 7.01 us
    ppermute x19 -> x25, starting transfers between devices: 21.4 us -> 35.9 us  [swap(): return lax.ppermute(value, axis, [(i, i ^ apart) for i in range(size)])]
    ppermute x19 -> x25, waiting for transfers between devices: 78.3 us -> 91 us  [swap(): return lax.ppermute(value, axis, [(i, i ^ apart) for i in range(size)])]
    pallas_call x7 -> x11, Pallas kernels: 13 us -> 20.4 us  [the longest x3 7.33 us: pack(): pl.pallas_call(functools.partial(pack_kernel, first if orders else None,...]
    unnamed x38 -> x42, local copies, waits for them, and re-layouts: 7.68 us -> 5.62 us
    pallas_call x2 -> x3, Pallas kernels: 7 us -> 8.97 us  [combine(): pl.pallas_call(functools.partial(combine_kernel, start, len(lefts)), out_...]
  transfers between devices with their start and end apart: 20 -> 26, of which waited for: 11 -> 11; matrix products, arithmetic and copies ran while one was open for 0% -> 0% of each run, Pallas kernels for 19% -> 20%
where the time goes in v2:
time: 199 us
  waiting for transfers between devices  97.4 us (49%)
  Pallas kernels  47.9 us (24%)
  starting transfers between devices  43.2 us (22%)
  local copies, waits for them, and re-layouts  7.01 us (4%)
  between operations  3.22 us (2%)
    ppermute x25, waiting for transfers between devices, swap(): return lax.ppermute(value, axis, [(i, i ^ apart) for i in range(size)])  91 us
    ppermute x25, starting transfers between devices, swap(): return lax.ppermute(value, axis, [(i, i ^ apart) for i in range(size)])  35.9 us
    pallas_call x3, Pallas kernels, product(): pl.pallas_call(functools.partial(product_kernel, groups, rows, edges, sta...  12.5 us
    pallas_call x3, Pallas kernels, combine(): pl.pallas_call(functools.partial(combine_kernel, start, len(lefts)), out_...  8.97 us
    pallas_call x3, Pallas kernels, pack(): pl.pallas_call(functools.partial(pack_kernel, first if orders else None,...  7.33 us
    all_to_all x1, starting transfers between devices, body(): lax.all_to_all(jnp.broadcast_to(meta, (devices, meta.shape[1])), 'pair',...  7.28 us
    pallas_call x3, Pallas kernels, slab(): pl.pallas_call(functools.partial(slab_kernel, first if orders else None,...  6.83 us
    all_to_all x1, waiting for transfers between devices, body(): lax.all_to_all(jnp.broadcast_to(meta, (devices, meta.shape[1])), 'pair',...  6.42 us
  transfers between devices with their start and end apart: 26, of which 11 were waited for; matrix products, arithmetic and copies ran while one was open for 0% of the time, Pallas kernels for 20%

profile of v2, /device:TPU:0, one launch (start us, length us, event | category | flops | bytes accessed | tf_op | source)
XLA Modules:
  0.0 198.8 jit_solution(7698291103144367443)
XLA Ops:
  0.7 0.8 concatenate.5
  1.4 0.6 broadcast_in_dim.11
  2.0 7.3 %all-to-all-start = ((s32[8,1,13]{2,1,0:T(1,128)}), s32[8,1,13]{2,1,0:T(1,128)S(1)}, u32[]{:S(2)}, u32[]{:S(2)}) async-start(s32[8,1,13]{2,1,0:T(1,128)} %broadcast_in_dim.11), calls=%async_computation | async-start | bytes 8192 | tf_op jit(solution)/shard_map/all_to_all | solution.py:548
  9.3 6.4 %all-to-all-done = s32[8,1,13]{2,1,0:T(1,128)S(1)} async-done(((s32[8,1,13]{2,1,0:T(1,128)}), s32[8,1,13]{2,1,0:T(1,128)S(1)}, u32[]{:S(2)}, u32[]{:S(2)}) %all-to-all-start) | async-done | bytes 448 | tf_op jit(solution)/shard_map/all_to_all | solution.py:548
  15.7 0.6 copy-done.20
  16.3 1.7 order.2
  18.1 0.5 collective-permute-start.8
  18.6 1.0 collective-permute-done.8
  20.9 2.9 %collective-permute-start.9 = (s32[1]{0:T(128)}, s32[1]{0:T(128)}, u32[]{:S(2)}, u32[]{:S(2)}) collective-permute-start(s32[1]{0:T(128)} %max.6), channel_id=1, source_target_pairs={{0,16},{8,24},{16,0},{24,8},{1,17},{9,25},{17,1},{25,9},{2,18},{10... | collective-permute-start | bytes 20 | tf_op jit(solution)/shard_map/ppermute | solution.py:26
  23.8 0.9 collective-permute-done.9
  25.3 0.6 copy-done.21
  25.9 1.7 order.3
  27.6 3.4 %slab.6 = bf16[13,128,512]{2,1,0:T(8,128)(2,1)} custom-call(s32[17]{0:T(128)S(1)} %get-tuple-element.77.refs_0_, bf16[16,128,1024]{2,1,0:T(8,128)(2,1)} %bitcast.14), custom_call_target="tpu_custom_call" | custom-call | bytes 3407872 | tf_op jit(solution)/shard_map/slab/pallas_call | solution.py:209
  31.1 0.7 collective-permute-start.15
  31.8 3.9 %pack.7 = (bf16[2,13,80,128]{3,2,1,0:T(8,128)(2,1)S(1)}, bf16[2,13,80,128]{3,2,1,0:T(8,128)(2,1)S(1)}, bf16[2,13,80,128]{3,2,1,0:T(8,128)(2,1)S(1)}, bf16[2,13,80,128]{3,2,1,0:T(8,128)(2,1)}) custom-call(s32[17]{0:T(128)S(1)} %get-tuple-element.72.refs_0_.order, s32[1]{0:T(128)} %bitcast.2.refs_1_.refs_0_, bf16[16,128,1024]{2,1,0:T(8,128)(2,1)} %bitcast.16), custom_call_target="tpu_custom_call" | custom-call | bytes 4259840 | tf_op jit(solution)/shard_map/pack/pallas_call | solution.py:174
  35.7 0.8 copy-done
  36.5 0.6 collective-permute-start.23
  37.1 1.3 pack.6
  38.4 1.5 collective-permute-start.20
  39.9 0.6 collective-permute-start.21
  40.5 15.7 %collective-permute-done.20.refs_1_ = bf16[2,16,16,128]{3,2,1,0:T(8,128)(2,1)S(1)} collective-permute-done((bf16[2,16,16,128]{3,2,1,0:T(8,128)(2,1)S(1)}, bf16[2,16,16,128]{3,2,1,0:T(8,128)(2,1)S(1)}, u32[]{:S(2)}, u32[]{:S(2)}) %collective-permute-start.20) | collective-permute-done | bytes 131104 | tf_op jit(solution)/shard_map/ppermute | solution.py:26
  56.2 0.6 copy-done.6
  56.9 0.6 collective-permute-start.22
  57.5 0.7 copy-done.8
  58.1 0.4 collective-permute-start.24
  58.5 1.3 slab.5
  59.8 5.3 %collective-permute-done.22.refs_3_ = bf16[2,16,16,128]{3,2,1,0:T(8,128)(2,1)S(1)} collective-permute-done((bf16[2,16,16,128]{3,2,1,0:T(8,128)(2,1)S(1)}, bf16[2,16,16,128]{3,2,1,0:T(8,128)(2,1)S(1)}, u32[]{:S(2)}, u32[]{:S(2)}) %collective-permute-start.22) | collective-permute-done | bytes 131104 | tf_op jit(solution)/shard_map/ppermute | solution.py:26
  65.1 0.7 copy-done.10
  65.8 0.8 copy-done.2
  66.6 1.6 collective-permute-start.12
  68.1 18.3 %collective-permute-done.24.refs_6_ = bf16[2,13,80,128]{3,2,1,0:T(8,128)(2,1)S(1)} collective-permute-done((bf16[2,13,80,128]{3,2,1,0:T(8,128)(2,1)S(1)}, bf16[2,13,80,128]{3,2,1,0:T(8,128)(2,1)S(1)}, u32[]{:S(2)}, u32[]{:S(2)}) %collective-permute-start.24) | collective-permute-done | bytes 532512 | tf_op jit(solution)/shard_map/ppermute | solution.py:26
  86.4 0.8 copy-done.4
  87.3 0.9 collective-permute-start.25
  88.2 2.4 %plan.1 = (s32[25]{0:T(128)}, f32[25]{0:T(128)}, s32[65]{0:T(128)}) custom-call(s32[8,13]{1,0:T(8,128)} %bitcast.23, s32[17]{0:T(128)} %get-tuple-element.67.left_rank, s32[17]{0:T(128)} %get-tuple-element.68.right_rank, f32[8]{0:T(128)} %subduction.1), custom_call_target="tpu_custom_call" | custom-call | tf_op jit(solution)/shard_map/plan/pallas_call | solution.py:123
  90.7 2.2 %slab.7 = bf16[13,128,256]{2,1,0:T(8,128)(2,1)S(1)} custom-call(s32[17]{0:T(128)S(1)} %get-tuple-element.77.refs_0_, bf16[16,128,1024]{2,1,0:T(8,128)(2,1)} %bitcast.17), custom_call_target="tpu_custom_call" | custom-call | bytes 1703936 | tf_op jit(solution)/shard_map/slab/pallas_call | solution.py:209
  92.9 1.5 pick.3
  94.5 2.0 %combine.4.refs_0_ = bf16[128,4096]{1,0:T(8,128)(2,1)S(1)} custom-call(s32[25]{0:T(128)S(1)} %copy-done.12, f32[25]{0:T(128)S(1)} %copy-done.13, s32[65]{0:T(128)S(1)} %copy-done.14, s32[1]{0:T(128)} %get-tuple-element.66.refs_3_.more, bf16[2,13,16,128]{3,2,1,0:T(8,128)(2,1)S(1)} %get-tuple-element.95.refs_4_, ...), custom_call_target="tpu_custom_call" | custom-call | flops 2097152 | bytes 1572864 | tf_op jit(solution)/shard_map/combine/pallas_call | solution.py:380
  96.5 6.9 %collective-permute-done.25.refs_7_ = bf16[2,13,80,128]{3,2,1,0:T(8,128)(2,1)} collective-permute-done((bf16[2,13,80,128]{3,2,1,0:T(8,128)(2,1)}, bf16[2,13,80,128]{3,2,1,0:T(8,128)(2,1)}, u32[]{:S(2)}, u32[]{:S(2)}) %collective-permute-start.25) | collective-permute-done | bytes 532512 | tf_op jit(solution)/shard_map/ppermute | solution.py:26
  103.4 4.6 %combine.5.refs_1_ = bf16[640,4096]{1,0:T(8,128)(2,1)S(1)} custom-call(s32[25]{0:T(128)S(1)} %copy-done.12, f32[25]{0:T(128)S(1)} %copy-done.13, s32[65]{0:T(128)S(1)} %copy-done.14, s32[1]{0:T(128)} %get-tuple-element.66.refs_3_.more, bf16[2,13,80,128]{3,2,1,0:T(8,128)(2,1)S(1)} %copy-done.1, bf16[2,13,80,128]{3,2,1,0:T(8,128)(2,1)S(1)} %copy-done.3, ...), custom_call_target="tpu_custom_call" | custom-call | flops 10485760 | bytes 7864320 | tf_op jit(solution)/shard_map/combine/pallas_call | solution.py:380
  108.0 1.6 collective-permute-start.16
  109.7 2.2 %pick.2 = (bf16[1,13,128,256]{3,2,1,0:T(8,128)(2,1)S(1)}, bf16[1,13,128,256]{3,2,1,0:T(8,128)(2,1)S(1)}) custom-call(s32[17]{0:T(128)S(1)} %copy-done.15, bf16[1,16,128,256]{3,2,1,0:T(8,128)(2,1)} %bitcast.5.refs_0_, bf16[1,16,128,256]{3,2,1,0:T(8,128)(2,1)} %bitcast.6.refs_1_), custom_call_target="tpu_custom_call" | custom-call | bytes 4194304 | tf_op jit(solution)/shard_map/pick/pallas_call | solution.py:245
  111.9 6.2 %product.5 = (bf16[2,2,96,768]{3,2,1,0:T(8,128)(2,1)S(1)}, f32[2,2,96,768]{3,2,1,0:T(8,128)S(1)}) custom-call(s32[1]{0:T(128)} %get-tuple-element.66.refs_3_.more, bf16[128,4096]{1,0:T(8,128)(2,1)S(1)} %combine.4.refs_0_, bf16[640,4096]{1,0:T(8,128)(2,1)S(1)} %combine.5.refs_1_, bf16[13,128,256]{2,1,0:T(8,128)(2,1)S(1)} %bitcast.10, ...), custom_call_target="tpu_custom_call" | custom-call | flops 4831838208 | bytes 12582912 | tf_op jit(solution)/shard_map/product/pallas_call | solution.py:455
  118.1 7.9 %collective-permute-start.28 = (bf16[2,2,96,768]{3,2,1,0:T(8,128)(2,1)S(1)}, bf16[2,2,96,768]{3,2,1,0:T(8,128)(2,1)S(1)}, u32[]{:S(2)}, u32[]{:S(2)}) collective-permute-start(bf16[2,2,96,768]{3,2,1,0:T(8,128)(2,1)S(1)} %get-tuple-element.108), channel_id=1, source_target_pairs={{0,2},{1,3},{2,0},{3,1},{4,6},{5,7},{6,4},{7,5},{8,10},{9,11},{10,... | collective-permute-start | bytes 1769480 | tf_op jit(solution)/shard_map/ppermute | solution.py:26
  126.1 2.1 %pack.5 = (bf16[2,13,32,128]{3,2,1,0:T(8,128)(2,1)S(1)}, bf16[2,13,32,128]{3,2,1,0:T(8,128)(2,1)S(1)}, bf16[2,13,32,128]{3,2,1,0:T(8,128)(2,1)S(1)}, bf16[2,13,32,128]{3,2,1,0:T(8,128)(2,1)S(1)}) custom-call(s32[17]{0:T(128)S(1)} %get-tuple-element.72.refs_0_.order, s32[1]{0:T(128)} %bitcast.2.refs_1_.refs_0_, bf16[16,128,1024]{2,1,0:T(8,128)(2,1)S(1)} %bitcast.20), custom_call_target="tpu_custom_call" | custom-call | bytes 1703936 | tf_op jit(solution)/shard_map/pack/pallas_call | solution.py:174
  128.2 0.1 collective-permute-start.5
  128.3 3.2 %collective-permute-start.6 = (bf16[2,13,32,128]{3,2,1,0:T(8,128)(2,1)S(1)}, bf16[2,13,32,128]{3,2,1,0:T(8,128)(2,1)S(1)}, u32[]{:S(2)}, u32[]{:S(2)}) collective-permute-start(bf16[2,13,32,128]{3,2,1,0:T(8,128)(2,1)S(1)} %get-tuple-element.75), channel_id=1, source_target_pairs={{0,4},{1,5},{2,6},{3,7},{4,0},{5,1},{6,2},{7,3},{8,12},{9,13},{10,... | collective-permute-start | bytes 638984 | tf_op jit(solution)/shard_map/ppermute | solution.py:26
  131.4 17.3 %collective-permute-done.5.refs_5_ = bf16[2,13,32,128]{3,2,1,0:T(8,128)(2,1)S(1)} collective-permute-done((bf16[2,13,32,128]{3,2,1,0:T(8,128)(2,1)S(1)}, bf16[2,13,32,128]{3,2,1,0:T(8,128)(2,1)S(1)}, u32[]{:S(2)}, u32[]{:S(2)}) %collective-permute-start.5) | collective-permute-done | bytes 213024 | tf_op jit(solution)/shard_map/ppermute | solution.py:26
  148.7 2.6 %collective-permute-start.7 = (bf16[2,13,32,128]{3,2,1,0:T(8,128)(2,1)S(1)}, bf16[2,13,32,128]{3,2,1,0:T(8,128)(2,1)S(1)}, u32[]{:S(2)}, u32[]{:S(2)}) collective-permute-start(bf16[2,13,32,128]{3,2,1,0:T(8,128)(2,1)S(1)} %get-tuple-element.76), channel_id=1, source_target_pairs={{0,6},{1,7},{2,4},{3,5},{4,2},{5,3},{6,0},{7,1},{8,14},{9,15},{10,... | collective-permute-start | bytes 638984 | tf_op jit(solution)/shard_map/ppermute | solution.py:26
  151.4 5.9 %collective-permute-done.7.refs_7_ = bf16[2,13,32,128]{3,2,1,0:T(8,128)(2,1)S(1)} collective-permute-done((bf16[2,13,32,128]{3,2,1,0:T(8,128)(2,1)S(1)}, bf16[2,13,32,128]{3,2,1,0:T(8,128)(2,1)S(1)}, u32[]{:S(2)}, u32[]{:S(2)}) %collective-permute-start.7) | collective-permute-done | bytes 213024 | tf_op jit(solution)/shard_map/ppermute | solution.py:26
  157.3 2.3 %combine.3.refs_0_ = bf16[256,4096]{1,0:T(8,128)(2,1)S(1)} custom-call(s32[25]{0:T(128)S(1)} %copy-done.12, f32[25]{0:T(128)S(1)} %copy-done.13, s32[65]{0:T(128)S(1)} %copy-done.14, s32[1]{0:T(128)} %get-tuple-element.66.refs_3_.more, bf16[2,13,32,128]{3,2,1,0:T(8,128)(2,1)S(1)} %get-tuple-element.73.refs_4_, ...), custom_call_target="tpu_custom_call" | custom-call | flops 4194304 | bytes 3145728 | tf_op jit(solution)/shard_map/combine/pallas_call | solution.py:380
  159.7 2.5 %product.4 = (bf16[2,2,96,256]{3,2,1,0:T(8,128)(2,1)S(1)}, f32[2,2,96,256]{3,2,1,0:T(8,128)S(1)}) custom-call(s32[1]{0:T(128)} %get-tuple-element.66.refs_3_.more, bf16[128,4096]{1,0:T(8,128)(2,1)S(1)} %combine.4.refs_0_, bf16[640,4096]{1,0:T(8,128)(2,1)S(1)} %combine.5.refs_1_, bf16[13,128,256]{2,1,0:T(8,128)(2,1)S(1)} %collective-permute-done.14.refs_3_.refs_2_, ...), custom_call_target="tpu_custom_call" | custom-call | flops 1610612736 | bytes 8388608 | tf_op jit(solution)/shard_map/product/pallas_call | solution.py:455
  162.1 3.6 %collective-permute-start.26 = (bf16[2,2,96,256]{3,2,1,0:T(8,128)(2,1)S(1)}, bf16[2,2,96,256]{3,2,1,0:T(8,128)(2,1)S(1)}, u32[]{:S(2)}, u32[]{:S(2)}) collective-permute-start(bf16[2,2,96,256]{3,2,1,0:T(8,128)(2,1)S(1)} %get-tuple-element.104), channel_id=1, source_target_pairs={{0,2},{1,3},{2,0},{3,1},{4,6},{5,7},{6,4},{7,5},{8,10},{9,11},{10,... | collective-permute-start | bytes 589832 | tf_op jit(solution)/shard_map/ppermute | solution.py:26
  165.7 0.1 halve.3
  165.8 0.1 collective-permute-start.29
  165.9 3.9 %product.3 = (bf16[1,2,32,1024]{3,2,1,0:T(8,128)(2,1)S(1)}, bf16[1,2,32,1024]{3,2,1,0:T(8,128)(2,1)S(1)}, bf16[1,2,32,1024]{3,2,1,0:T(8,128)(2,1)S(1)}, f32[1,2,32,1024]{3,2,1,0:T(8,128)S(1)}) custom-call(s32[1]{0:T(128)} %get-tuple-element.66.refs_3_.more, bf16[256,4096]{1,0:T(8,128)(2,1)S(1)} %combine.3.refs_0_, bf16[13,128,256]{2,1,0:T(8,128)(2,1)S(1)} %bitcast.11, ...), custom_call_target="tpu_custom_call" | custom-call | flops 2147483648 | bytes 10485760 | tf_op jit(solution)/shard_map/product/pallas_call | solution.py:455
  169.8 2.4 %collective-permute-start.17 = (bf16[1,2,32,1024]{3,2,1,0:T(8,128)(2,1)S(1)}, bf16[1,2,32,1024]{3,2,1,0:T(8,128)(2,1)S(1)}, u32[]{:S(2)}, u32[]{:S(2)}) collective-permute-start(bf16[1,2,32,1024]{3,2,1,0:T(8,128)(2,1)S(1)} %get-tuple-element.88), channel_id=1, source_target_pairs={{0,6},{1,7},{2,4},{3,5},{4,2},{5,3},{6,0},{7,1},{8,14},{9,15},{10,... | collective-permute-start | bytes 393224 | tf_op jit(solution)/shard_map/ppermute | solution.py:26
  172.2 1.0 collective-permute-start.18
  173.2 1.0 collective-permute-start.19
  174.3 2.1 %collective-permute-start.27 = (bf16[1,2,96,256]{3,2,1,0:T(8,128)(2,1)S(1)}, bf16[1,2,96,256]{3,2,1,0:T(8,128)(2,1)S(1)}, u32[]{:S(2)}, u32[]{:S(2)}) collective-permute-start(bf16[1,2,96,256]{3,2,1,0:T(8,128)(2,1)S(1)} %get-tuple-element.106), channel_id=1, source_target_pairs={{0,4},{1,5},{2,6},{3,7},{4,0},{5,1},{6,2},{7,3},{8,12},{9,13},{10,... | collective-permute-start | bytes 294920 | tf_op jit(solution)/shard_map/ppermute | solution.py:26
  176.3 13.6 %collective-permute-done.29.refs_0_ = bf16[1,2,96,768]{3,2,1,0:T(8,128)(2,1)S(1)} collective-permute-done((bf16[1,2,96,768]{3,2,1,0:T(8,128)(2,1)S(1)}, bf16[1,2,96,768]{3,2,1,0:T(8,128)(2,1)S(1)}, u32[]{:S(2)}, u32[]{:S(2)}) %collective-permute-start.29) | collective-permute-done | bytes 294944 | tf_op jit(solution)/shard_map/ppermute | solution.py:26
  190.0 1.0 finish.3.refs_1_
  190.9 6.1 %collective-permute-done.27.refs_0_ = bf16[1,2,96,256]{3,2,1,0:T(8,128)(2,1)S(1)} collective-permute-done((bf16[1,2,96,256]{3,2,1,0:T(8,128)(2,1)S(1)}, bf16[1,2,96,256]{3,2,1,0:T(8,128)(2,1)S(1)}, u32[]{:S(2)}, u32[]{:S(2)}) %collective-permute-start.27) | collective-permute-done | bytes 98336 | tf_op jit(solution)/shard_map/ppermute | solution.py:26
  197.0 0.8 finish.4.refs_3_
  197.8 0.8 finish.5
  (56 shorter events, 0.3 us)
Async XLA Ops:
  2.0 13.7 %all-to-all-start = ((s32[8,1,13]{2,1,0:T(1,128)}), s32[8,1,13]{2,1,0:T(1,128)S(1)}, u32[]{:S(2)}, u32[]{:S(2)}) async-start(s32[8,1,13]{2,1,0:T(1,128)} %broadcast_in_dim.11), calls=%async_computation | async-start | bytes 8192 | tf_op jit(solution)/shard_map/all_to_all | solution.py:548
  15.7 0.6 copy-start.20
  18.1 7.2 %collective-permute-start.10 = (s32[8,13]{1,0:T(8,128)}, s32[8,13]{1,0:T(8,128)S(1)}, u32[]{:S(2)}, u32[]{:S(2)}) collective-permute-start(s32[8,13]{1,0:T(8,128)} %bitcast.22), channel_id=1, source_target_pairs={{0,8},{8,0},{16,24},{24,16},{1,9},{9,1},{17,25},{25,17},{2,10},{10... | collective-permute-start | bytes 1256 | tf_op jit(solution)/shard_map/ppermute | solution.py:26
  18.1 1.5 collective-permute-start.8
  20.9 3.7 %collective-permute-start.9 = (s32[1]{0:T(128)}, s32[1]{0:T(128)}, u32[]{:S(2)}, u32[]{:S(2)}) collective-permute-start(s32[1]{0:T(128)} %max.6), channel_id=1, source_target_pairs={{0,16},{8,24},{16,0},{24,8},{1,17},{9,25},{17,1},{25,9},{2,18},{10... | collective-permute-start | bytes 20 | tf_op jit(solution)/shard_map/ppermute | solution.py:26
  25.3 0.6 copy-start.21
  31.0 6.0 %copy-start.16 = (bf16[1,16,128,1024]{3,2,1,0:T(8,128)(2,1)S(1)}, bf16[1,16,128,1024]{3,2,1,0:T(8,128)(2,1)}, u32[]{:S(2)}) copy-start(bf16[1,16,128,1024]{3,2,1,0:T(8,128)(2,1)} %param.9) | copy-start | bytes 12582916
  31.1 80.8 %collective-permute-start.13 = (bf16[13,128,512]{2,1,0:T(8,128)(2,1)}, bf16[13,128,512]{2,1,0:T(8,128)(2,1)S(1)}, u32[]{:S(2)}, u32[]{:S(2)}) collective-permute-start(bf16[13,128,512]{2,1,0:T(8,128)(2,1)} %slab.6), channel_id=1, source_target_pairs={{0,8},{8,0},{16,24},{24,16},{1,9},{9,1},{17,25},{25,17},{2,10},{10... | collective-permute-start | bytes 5111816 | tf_op jit(solution)/shard_map/ppermute | solution.py:26
  31.1 80.7 %collective-permute-start.15 = (bf16[13,128,512]{2,1,0:T(8,128)(2,1)}, bf16[13,128,512]{2,1,0:T(8,128)(2,1)S(1)}, u32[]{:S(2)}, u32[]{:S(2)}) collective-permute-start(bf16[13,128,512]{2,1,0:T(8,128)(2,1)} %slab.6), channel_id=1, source_target_pairs={{0,9},{1,8},{2,11},{3,10},{4,13},{5,12},{6,15},{7,14},{8,1},{9,0},... | collective-permute-start | bytes 5111816 | tf_op jit(solution)/shard_map/ppermute | solution.py:26
  35.7 0.8 copy-start
  36.5 29.2 %collective-permute-start.23 = (bf16[2,13,80,128]{3,2,1,0:T(8,128)(2,1)S(1)}, bf16[2,13,80,128]{3,2,1,0:T(8,128)(2,1)S(1)}, u32[]{:S(2)}, u32[]{:S(2)}) collective-permute-start(bf16[2,13,80,128]{3,2,1,0:T(8,128)(2,1)S(1)} %get-tuple-element.100), channel_id=1, source_target_pairs={{0,2},{1,3},{2,0},{3,1},{4,6},{5,7},{6,4},{7,5},{8,10},{9,11},{10,... | collective-permute-start | bytes 1597448 | tf_op jit(solution)/shard_map/ppermute | solution.py:26
  38.4 17.8 %collective-permute-start.20 = (bf16[2,16,16,128]{3,2,1,0:T(8,128)(2,1)S(1)}, bf16[2,16,16,128]{3,2,1,0:T(8,128)(2,1)S(1)}, u32[]{:S(2)}, u32[]{:S(2)}) collective-permute-start(bf16[2,16,16,128]{3,2,1,0:T(8,128)(2,1)S(1)} %get-tuple-element.92), channel_id=1, source_target_pairs={{0,2},{1,3},{2,0},{3,1},{4,6},{5,7},{6,4},{7,5},{8,10},{9,11},{10,... | collective-permute-start | bytes 393224 | tf_op jit(solution)/shard_map/ppermute | solution.py:26
  39.9 17.5 %collective-permute-start.21 = (bf16[2,16,16,128]{3,2,1,0:T(8,128)(2,1)S(1)}, bf16[2,16,16,128]{3,2,1,0:T(8,128)(2,1)S(1)}, u32[]{:S(2)}, u32[]{:S(2)}) collective-permute-start(bf16[2,16,16,128]{3,2,1,0:T(8,128)(2,1)S(1)} %get-tuple-element.93), channel_id=1, source_target_pairs={{0,4},{1,5},{2,6},{3,7},{4,0},{5,1},{6,2},{7,3},{8,12},{9,13},{10,... | collective-permute-start | bytes 393224 | tf_op jit(solution)/shard_map/ppermute | solution.py:26
  56.2 0.7 copy-start.6
  56.9 8.2 %collective-permute-start.22 = (bf16[2,16,16,128]{3,2,1,0:T(8,128)(2,1)S(1)}, bf16[2,16,16,128]{3,2,1,0:T(8,128)(2,1)S(1)}, u32[]{:S(2)}, u32[]{:S(2)}) collective-permute-start(bf16[2,16,16,128]{3,2,1,0:T(8,128)(2,1)S(1)} %get-tuple-element.94), channel_id=1, source_target_pairs={{0,6},{1,7},{2,4},{3,5},{4,2},{5,3},{6,0},{7,1},{8,14},{9,15},{10,... | collective-permute-start | bytes 393224 | tf_op jit(solution)/shard_map/ppermute | solution.py:26
  57.5 0.7 copy-start.8
  58.1 28.3 %collective-permute-start.24 = (bf16[2,13,80,128]{3,2,1,0:T(8,128)(2,1)S(1)}, bf16[2,13,80,128]{3,2,1,0:T(8,128)(2,1)S(1)}, u32[]{:S(2)}, u32[]{:S(2)}) collective-permute-start(bf16[2,13,80,128]{3,2,1,0:T(8,128)(2,1)S(1)} %get-tuple-element.101), channel_id=1, source_target_pairs={{0,4},{1,5},{2,6},{3,7},{4,0},{5,1},{6,2},{7,3},{8,12},{9,13},{10,... | collective-permute-start | bytes 1597448 | tf_op jit(solution)/shard_map/ppermute | solution.py:26
  65.1 0.7 copy-start.10
  65.7 42.3 %collective-permute-start.11 = (bf16[16,128,256]{2,1,0:T(8,128)(2,1)}, bf16[16,128,256]{2,1,0:T(8,128)(2,1)}, u32[]{:S(2)}, u32[]{:S(2)}) collective-permute-start(bf16[16,128,256]{2,1,0:T(8,128)(2,1)} %slab.5), channel_id=1, source_target_pairs={{0,8},{8,0},{16,24},{24,16},{1,9},{9,1},{17,25},{25,17},{2,10},{10... | collective-permute-start | bytes 3145736 | tf_op jit(solution)/shard_map/ppermute | solution.py:26
  65.7 0.8 copy-start.2
  66.6 43.1 %collective-permute-start.12 = (bf16[16,128,256]{2,1,0:T(8,128)(2,1)}, bf16[16,128,256]{2,1,0:T(8,128)(2,1)}, u32[]{:S(2)}, u32[]{:S(2)}) collective-permute-start(bf16[16,128,256]{2,1,0:T(8,128)(2,1)} %slab.5), channel_id=1, source_target_pairs={{0,9},{1,8},{2,11},{3,10},{4,13},{5,12},{6,15},{7,14},{8,1},{9,0},... | collective-permute-start | bytes 3145736 | tf_op jit(solution)/shard_map/ppermute | solution.py:26
  86.4 0.8 copy-start.4
  87.3 16.1 %collective-permute-start.25 = (bf16[2,13,80,128]{3,2,1,0:T(8,128)(2,1)}, bf16[2,13,80,128]{3,2,1,0:T(8,128)(2,1)}, u32[]{:S(2)}, u32[]{:S(2)}) collective-permute-start(bf16[2,13,80,128]{3,2,1,0:T(8,128)(2,1)} %get-tuple-element.102), channel_id=1, source_target_pairs={{0,6},{1,7},{2,4},{3,5},{4,2},{5,3},{6,0},{7,1},{8,14},{9,15},{10,... | collective-permute-start | bytes 1597448 | tf_op jit(solution)/shard_map/ppermute | solution.py:26
  90.6 2.3 %copy-start.7 = (bf16[2,16,16,128]{3,2,1,0:T(8,128)(2,1)S(1)}, bf16[2,16,16,128]{3,2,1,0:T(8,128)(2,1)}, u32[]{:S(2)}) copy-start(bf16[2,16,16,128]{3,2,1,0:T(8,128)(2,1)} %copy-done.6) | copy-start | bytes 393220
  90.6 2.3 %copy-start.9 = (bf16[2,16,16,128]{3,2,1,0:T(8,128)(2,1)S(1)}, bf16[2,16,16,128]{3,2,1,0:T(8,128)(2,1)}, u32[]{:S(2)}) copy-start(bf16[2,16,16,128]{3,2,1,0:T(8,128)(2,1)} %copy-done.8) | copy-start | bytes 393220
  90.6 2.3 %copy-start.11 = (bf16[2,16,16,128]{3,2,1,0:T(8,128)(2,1)S(1)}, bf16[2,16,16,128]{3,2,1,0:T(8,128)(2,1)}, u32[]{:S(2)}) copy-start(bf16[2,16,16,128]{3,2,1,0:T(8,128)(2,1)} %copy-done.10) | copy-start | bytes 393220
  90.6 3.8 %copy-start.12 = (s32[25]{0:T(128)S(1)}, s32[25]{0:T(128)}, u32[]{:S(2)}) copy-start(s32[25]{0:T(128)} %get-tuple-element.69.refs_0_) | copy-start | bytes 304
  90.6 3.8 %copy-start.13 = (f32[25]{0:T(128)S(1)}, f32[25]{0:T(128)}, u32[]{:S(2)}) copy-start(f32[25]{0:T(128)} %get-tuple-element.70.refs_1_) | copy-start | bytes 304
  90.7 3.8 %copy-start.14 = (s32[65]{0:T(128)S(1)}, s32[65]{0:T(128)}, u32[]{:S(2)}) copy-start(s32[65]{0:T(128)} %get-tuple-element.71.refs_2_) | copy-start | bytes 784
  90.7 3.8 %copy-start.19 = (bf16[2,3,128,128]{3,2,1,0:T(8,128)(2,1)S(1)}, bf16[2,3,128,128]{3,2,1,0:T(8,128)(2,1)}, u32[]{:S(2)}) copy-start(bf16[2,3,128,128]{3,2,1,0:T(8,128)(2,1)} %get-tuple-element.78.refs_8_) | copy-start | bytes 589828
  92.9 10.5 %copy-start.1 = (bf16[2,13,80,128]{3,2,1,0:T(8,128)(2,1)S(1)}, bf16[2,13,80,128]{3,2,1,0:T(8,128)(2,1)}, u32[]{:S(2)}) copy-start(bf16[2,13,80,128]{3,2,1,0:T(8,128)(2,1)} %copy-done) | copy-start | bytes 1597444
  92.9 10.5 %copy-start.3 = (bf16[2,13,80,128]{3,2,1,0:T(8,128)(2,1)S(1)}, bf16[2,13,80,128]{3,2,1,0:T(8,128)(2,1)}, u32[]{:S(2)}) copy-start(bf16[2,13,80,128]{3,2,1,0:T(8,128)(2,1)} %copy-done.2) | copy-start | bytes 1597444
  92.9 10.5 %copy-start.5 = (bf16[2,13,80,128]{3,2,1,0:T(8,128)(2,1)S(1)}, bf16[2,13,80,128]{3,2,1,0:T(8,128)(2,1)}, u32[]{:S(2)}) copy-start(bf16[2,13,80,128]{3,2,1,0:T(8,128)(2,1)} %copy-done.4) | copy-start | bytes 1597444
  103.3 56.3 %collective-permute-start.14 = (bf16[13,128,256]{2,1,0:T(8,128)(2,1)S(1)}, bf16[13,128,256]{2,1,0:T(8,128)(2,1)S(1)}, u32[]{:S(2)}, u32[]{:S(2)}) collective-permute-start(bf16[13,128,256]{2,1,0:T(8,128)(2,1)S(1)} %slab.7), channel_id=1, source_target_pairs={{0,8},{8,0},{16,24},{24,16},{1,9},{9,1},{17,25},{25,17},{2,10},{10... | collective-permute-start | bytes 2555912 | tf_op jit(solution)/shard_map/ppermute | solution.py:26
  103.4 6.3 %copy-start.15 = (s32[17]{0:T(128)S(1)}, s32[17]{0:T(128)}, u32[]{:S(2)}) copy-start(s32[17]{0:T(128)} %get-tuple-element.82.order) | copy-start | bytes 208
  108.0 51.6 %collective-permute-start.16 = (bf16[13,128,256]{2,1,0:T(8,128)(2,1)S(1)}, bf16[13,128,256]{2,1,0:T(8,128)(2,1)S(1)}, u32[]{:S(2)}, u32[]{:S(2)}) collective-permute-start(bf16[13,128,256]{2,1,0:T(8,128)(2,1)S(1)} %slab.7), channel_id=1, source_target_pairs={{0,9},{1,8},{2,11},{3,10},{4,13},{5,12},{6,15},{7,14},{8,1},{9,0},... | collective-permute-start | bytes 2555912 | tf_op jit(solution)/shard_map/ppermute | solution.py:26
  111.9 14.2 %copy-start.17 = (bf16[1,16,128,1024]{3,2,1,0:T(8,128)(2,1)S(1)}, bf16[1,16,128,1024]{3,2,1,0:T(8,128)(2,1)}, u32[]{:S(2)}) copy-start(bf16[1,16,128,1024]{3,2,1,0:T(8,128)(2,1)} %param.9) | copy-start | bytes 12582916
  118.1 47.6 %collective-permute-start.28 = (bf16[2,2,96,768]{3,2,1,0:T(8,128)(2,1)S(1)}, bf16[2,2,96,768]{3,2,1,0:T(8,128)(2,1)S(1)}, u32[]{:S(2)}, u32[]{:S(2)}) collective-permute-start(bf16[2,2,96,768]{3,2,1,0:T(8,128)(2,1)S(1)} %get-tuple-element.108), channel_id=1, source_target_pairs={{0,2},{1,3},{2,0},{3,1},{4,6},{5,7},{6,4},{7,5},{8,10},{9,11},{10,... | collective-permute-start | bytes 1769480 | tf_op jit(solution)/shard_map/ppermute | solution.py:26
  128.2 20.6 %collective-permute-start.5 = (bf16[2,13,32,128]{3,2,1,0:T(8,128)(2,1)S(1)}, bf16[2,13,32,128]{3,2,1,0:T(8,128)(2,1)S(1)}, u32[]{:S(2)}, u32[]{:S(2)}) collective-permute-start(bf16[2,13,32,128]{3,2,1,0:T(8,128)(2,1)S(1)} %get-tuple-element.74), channel_id=1, source_target_pairs={{0,2},{1,3},{2,0},{3,1},{4,6},{5,7},{6,4},{7,5},{8,10},{9,11},{10,... | collective-permute-start | bytes 638984 | tf_op jit(solution)/shard_map/ppermute | solution.py:26
  128.3 23.1 %collective-permute-start.6 = (bf16[2,13,32,128]{3,2,1,0:T(8,128)(2,1)S(1)}, bf16[2,13,32,128]{3,2,1,0:T(8,128)(2,1)S(1)}, u32[]{:S(2)}, u32[]{:S(2)}) collective-permute-start(bf16[2,13,32,128]{3,2,1,0:T(8,128)(2,1)S(1)} %get-tuple-element.75), channel_id=1, source_target_pairs={{0,4},{1,5},{2,6},{3,7},{4,0},{5,1},{6,2},{7,3},{8,12},{9,13},{10,... | collective-permute-start | bytes 638984 | tf_op jit(solution)/shard_map/ppermute | solution.py:26
  148.7 8.6 %collective-permute-start.7 = (bf16[2,13,32,128]{3,2,1,0:T(8,128)(2,1)S(1)}, bf16[2,13,32,128]{3,2,1,0:T(8,128)(2,1)S(1)}, u32[]{:S(2)}, u32[]{:S(2)}) collective-permute-start(bf16[2,13,32,128]{3,2,1,0:T(8,128)(2,1)S(1)} %get-tuple-element.76), channel_id=1, source_target_pairs={{0,6},{1,7},{2,4},{3,5},{4,2},{5,3},{6,0},{7,1},{8,14},{9,15},{10,... | collective-permute-start | bytes 638984 | tf_op jit(solution)/shard_map/ppermute | solution.py:26
  162.1 12.1 %collective-permute-start.26 = (bf16[2,2,96,256]{3,2,1,0:T(8,128)(2,1)S(1)}, bf16[2,2,96,256]{3,2,1,0:T(8,128)(2,1)S(1)}, u32[]{:S(2)}, u32[]{:S(2)}) collective-permute-start(bf16[2,2,96,256]{3,2,1,0:T(8,128)(2,1)S(1)} %get-tuple-element.104), channel_id=1, source_target_pairs={{0,2},{1,3},{2,0},{3,1},{4,6},{5,7},{6,4},{7,5},{8,10},{9,11},{10,... | collective-permute-start | bytes 589832 | tf_op jit(solution)/shard_map/ppermute | solution.py:26
  165.8 24.2 %collective-permute-start.29 = (bf16[1,2,96,768]{3,2,1,0:T(8,128)(2,1)S(1)}, bf16[1,2,96,768]{3,2,1,0:T(8,128)(2,1)S(1)}, u32[]{:S(2)}, u32[]{:S(2)}) collective-permute-start(bf16[1,2,96,768]{3,2,1,0:T(8,128)(2,1)S(1)} %get-tuple-element.110), channel_id=1, source_target_pairs={{0,4},{1,5},{2,6},{3,7},{4,0},{5,1},{6,2},{7,3},{8,12},{9,13},{10,... | collective-permute-start | bytes 884744 | tf_op jit(solution)/shard_map/ppermute | solution.py:26
  169.8 28.0 %collective-permute-start.17 = (bf16[1,2,32,1024]{3,2,1,0:T(8,128)(2,1)S(1)}, bf16[1,2,32,1024]{3,2,1,0:T(8,128)(2,1)S(1)}, u32[]{:S(2)}, u32[]{:S(2)}) collective-permute-start(bf16[1,2,32,1024]{3,2,1,0:T(8,128)(2,1)S(1)} %get-tuple-element.88), channel_id=1, source_target_pairs={{0,6},{1,7},{2,4},{3,5},{4,2},{5,3},{6,0},{7,1},{8,14},{9,15},{10,... | collective-permute-start | bytes 393224 | tf_op jit(solution)/shard_map/ppermute | solution.py:26
  172.2 25.6 %collective-permute-start.18 = (bf16[1,2,32,1024]{3,2,1,0:T(8,128)(2,1)S(1)}, bf16[1,2,32,1024]{3,2,1,0:T(8,128)(2,1)S(1)}, u32[]{:S(2)}, u32[]{:S(2)}) collective-permute-start(bf16[1,2,32,1024]{3,2,1,0:T(8,128)(2,1)S(1)} %get-tuple-element.89), channel_id=1, source_target_pairs={{0,4},{1,5},{2,6},{3,7},{4,0},{5,1},{6,2},{7,3},{8,12},{9,13},{10,... | collective-permute-start | bytes 393224 | tf_op jit(solution)/shard_map/ppermute | solution.py:26
  173.2 24.6 %collective-permute-start.19 = (bf16[1,2,32,1024]{3,2,1,0:T(8,128)(2,1)S(1)}, bf16[1,2,32,1024]{3,2,1,0:T(8,128)(2,1)S(1)}, u32[]{:S(2)}, u32[]{:S(2)}) collective-permute-start(bf16[1,2,32,1024]{3,2,1,0:T(8,128)(2,1)S(1)} %get-tuple-element.90), channel_id=1, source_target_pairs={{0,2},{1,3},{2,0},{3,1},{4,6},{5,7},{6,4},{7,5},{8,10},{9,11},{10,... | collective-permute-start | bytes 393224 | tf_op jit(solution)/shard_map/ppermute | solution.py:26
  174.3 22.8 %collective-permute-start.27 = (bf16[1,2,96,256]{3,2,1,0:T(8,128)(2,1)S(1)}, bf16[1,2,96,256]{3,2,1,0:T(8,128)(2,1)S(1)}, u32[]{:S(2)}, u32[]{:S(2)}) collective-permute-start(bf16[1,2,96,256]{3,2,1,0:T(8,128)(2,1)S(1)} %get-tuple-element.106), channel_id=1, source_target_pairs={{0,4},{1,5},{2,6},{3,7},{4,0},{5,1},{6,2},{7,3},{8,12},{9,13},{10,... | collective-permute-start | bytes 294920 | tf_op jit(solution)/shard_map/ppermute | solution.py:26

commit v3 on v2

--- a/solution.py
+++ b/solution.py
@@ -180,7 +180,7 @@
         cost_estimate=pl.CostEstimate(
             flops=0, transcendentals=0, bytes_accessed=4 * groups * piece.size
         ),
-        compiler_params=pltpu.CompilerParams(vmem_limit_bytes=8 << 20),
+        compiler_params=pltpu.CompilerParams(vmem_limit_bytes=6 << 20),
         name="pack",
     )(*orders, me, own)
 
@@ -215,7 +215,7 @@
         cost_estimate=pl.CostEstimate(
             flops=0, transcendentals=0, bytes_accessed=4 * number * own.shape[1] * columns
         ),
-        compiler_params=pltpu.CompilerParams(vmem_limit_bytes=8 << 20),
+        compiler_params=pltpu.CompilerParams(vmem_limit_bytes=6 << 20),
         name="slab",
     )(*orders, own)
 
@@ -248,7 +248,7 @@
         in_specs=[spec(pltpu.SMEM)] + [spec(pl.ANY)] * len(whole),
         out_specs=[spec()] * len(whole),
         scratch_shapes=[pltpu.SemaphoreType.DMA((number * len(whole),))],
-        compiler_params=pltpu.CompilerParams(vmem_limit_bytes=8 << 20),
+        compiler_params=pltpu.CompilerParams(vmem_limit_bytes=6 << 20),
         cost_estimate=pl.CostEstimate(
             flops=0, transcendentals=0, bytes_accessed=4 * sum(piece.size for piece in whole)
         ),
@@ -386,7 +386,7 @@
         out_specs=spec(),
         scratch_shapes=[pltpu.VMEM((2, families - base, rows, width), jnp.bfloat16)] * len(lates)
         + [pltpu.SemaphoreType.DMA((len(lates),))],
-        compiler_params=pltpu.CompilerParams(vmem_limit_bytes=20 << 20),
+        compiler_params=pltpu.CompilerParams(vmem_limit_bytes=14 << 20),
         cost_estimate=pl.CostEstimate(
             flops=4 * size, transcendentals=0, bytes_accessed=3 * size
         ),
@@ -467,7 +467,7 @@
         out_specs=[block] * (sends + 1),
         scratch_shapes=[pltpu.VMEM((late, width, tile), jnp.bfloat16)] * 2
         + [pltpu.SemaphoreType.DMA((2,))],
-        compiler_params=pltpu.CompilerParams(vmem_limit_bytes=24 << 20),
+        compiler_params=pltpu.CompilerParams(vmem_limit_bytes=18 << 20),
         cost_estimate=pl.CostEstimate(
             flops=2 * sum(chunk.size for chunk in combined) * columns,
             transcendentals=0,
@@ -498,7 +498,7 @@
         cost_estimate=pl.CostEstimate(
             flops=keep.size, transcendentals=0, bytes_accessed=9 * keep.size
         ),
-        compiler_params=pltpu.CompilerParams(vmem_limit_bytes=8 << 20),
+        compiler_params=pltpu.CompilerParams(vmem_limit_bytes=6 << 20),
         name="halve",
     )(keep, came)
 
@@ -533,7 +533,7 @@
         cost_estimate=pl.CostEstimate(
             flops=keep.size, transcendentals=0, bytes_accessed=10 * keep.size
         ),
-        compiler_params=pltpu.CompilerParams(vmem_limit_bytes=8 << 20),
+        compiler_params=pltpu.CompilerParams(vmem_limit_bytes=6 << 20),
         name="finish",
     )(keep, *cames, *before)
 

time: 199 us -> 199 us (level)
  no operation moved by 1% of the time
where the time goes in v3:
time: 199 us
  waiting for transfers between devices  97.4 us (49%)
  Pallas kernels  47.9 us (24%)
  starting transfers between devices  43.2 us (22%)
  local copies, waits for them, and re-layouts  7.01 us (4%)
  between operations  3.22 us (2%)
    ppermute x25, waiting for transfers between devices, swap(): return lax.ppermute(value, axis, [(i, i ^ apart) for i in range(size)])  91 us
    ppermute x25, starting transfers between devices, swap(): return lax.ppermute(value, axis, [(i, i ^ apart) for i in range(size)])  35.9 us
    pallas_call x3, Pallas kernels, product(): pl.pallas_call(functools.partial(product_kernel, groups, rows, edges, sta...  12.5 us
    pallas_call x3, Pallas kernels, combine(): pl.pallas_call(functools.partial(combine_kernel, start, len(lefts)), out_...  8.97 us
    pallas_call x3, Pallas kernels, pack(): pl.pallas_call(functools.partial(pack_kernel, first if orders else None,...  7.33 us
    all_to_all x1, starting transfers between devices, body(): lax.all_to_all(jnp.broadcast_to(meta, (devices, meta.shape[1])), 'pair',...  7.28 us
    pallas_call x3, Pallas kernels, slab(): pl.pallas_call(functools.partial(slab_kernel, first if orders else None,...  6.83 us
    all_to_all x1, waiting for transfers between devices, body(): lax.all_to_all(jnp.broadcast_to(meta, (devices, meta.shape[1])), 'pair',...  6.42 us
  transfers between devices with their start and end apart: 26, of which 11 were waited for; matrix products, arithmetic and copies ran while one was open for 0% of the time, Pallas kernels for 20%

profile of v3, /device:TPU:0, one launch (start us, length us, event | category | flops | bytes accessed | tf_op | source)
XLA Modules:
  0.0 198.8 jit_solution(12470349918195036273)
XLA Ops:
  0.7 0.8 concatenate.5
  1.4 0.6 broadcast_in_dim.11
  2.0 7.3 %all-to-all-start = ((s32[8,1,13]{2,1,0:T(1,128)}), s32[8,1,13]{2,1,0:T(1,128)S(1)}, u32[]{:S(2)}, u32[]{:S(2)}) async-start(s32[8,1,13]{2,1,0:T(1,128)} %broadcast_in_dim.11), calls=%async_computation | async-start | bytes 8192 | tf_op jit(solution)/shard_map/all_to_all | solution.py:548
  9.3 6.4 %all-to-all-done = s32[8,1,13]{2,1,0:T(1,128)S(1)} async-done(((s32[8,1,13]{2,1,0:T(1,128)}), s32[8,1,13]{2,1,0:T(1,128)S(1)}, u32[]{:S(2)}, u32[]{:S(2)}) %all-to-all-start) | async-done | bytes 448 | tf_op jit(solution)/shard_map/all_to_all | solution.py:548
  15.7 0.6 copy-done.20
  16.3 1.7 order.2
  18.1 0.5 collective-permute-start.8
  18.6 1.0 collective-permute-done.8
  20.9 2.9 %collective-permute-start.9 = (s32[1]{0:T(128)}, s32[1]{0:T(128)}, u32[]{:S(2)}, u32[]{:S(2)}) collective-permute-start(s32[1]{0:T(128)} %max.6), channel_id=1, source_target_pairs={{0,16},{8,24},{16,0},{24,8},{1,17},{9,25},{17,1},{25,9},{2,18},{10... | collective-permute-start | bytes 20 | tf_op jit(solution)/shard_map/ppermute | solution.py:26
  23.8 0.9 collective-permute-done.9
  25.3 0.6 copy-done.21
  25.9 1.7 order.3
  27.6 3.4 %slab.6 = bf16[13,128,512]{2,1,0:T(8,128)(2,1)} custom-call(s32[17]{0:T(128)S(1)} %get-tuple-element.77.refs_0_, bf16[16,128,1024]{2,1,0:T(8,128)(2,1)} %bitcast.14), custom_call_target="tpu_custom_call" | custom-call | bytes 3407872 | tf_op jit(solution)/shard_map/slab/pallas_call | solution.py:209
  31.1 0.7 collective-permute-start.15
  31.8 3.9 %pack.7 = (bf16[2,13,80,128]{3,2,1,0:T(8,128)(2,1)S(1)}, bf16[2,13,80,128]{3,2,1,0:T(8,128)(2,1)S(1)}, bf16[2,13,80,128]{3,2,1,0:T(8,128)(2,1)S(1)}, bf16[2,13,80,128]{3,2,1,0:T(8,128)(2,1)}) custom-call(s32[17]{0:T(128)S(1)} %get-tuple-element.72.refs_0_.order, s32[1]{0:T(128)} %bitcast.2.refs_1_.refs_0_, bf16[16,128,1024]{2,1,0:T(8,128)(2,1)} %bitcast.16), custom_call_target="tpu_custom_call" | custom-call | bytes 4259840 | tf_op jit(solution)/shard_map/pack/pallas_call | solution.py:174
  35.7 0.8 copy-done
  36.5 0.6 collective-permute-start.23
  37.1 1.3 pack.6
  38.4 1.5 collective-permute-start.20
  39.9 0.6 collective-permute-start.21
  40.5 15.7 %collective-permute-done.20.refs_1_ = bf16[2,16,16,128]{3,2,1,0:T(8,128)(2,1)S(1)} collective-permute-done((bf16[2,16,16,128]{3,2,1,0:T(8,128)(2,1)S(1)}, bf16[2,16,16,128]{3,2,1,0:T(8,128)(2,1)S(1)}, u32[]{:S(2)}, u32[]{:S(2)}) %collective-permute-start.20) | collective-permute-done | bytes 131104 | tf_op jit(solution)/shard_map/ppermute | solution.py:26
  56.2 0.6 copy-done.6
  56.9 0.6 collective-permute-start.22
  57.5 0.7 copy-done.8
  58.1 0.4 collective-permute-start.24
  58.5 1.3 slab.5
  59.8 5.3 %collective-permute-done.22.refs_3_ = bf16[2,16,16,128]{3,2,1,0:T(8,128)(2,1)S(1)} collective-permute-done((bf16[2,16,16,128]{3,2,1,0:T(8,128)(2,1)S(1)}, bf16[2,16,16,128]{3,2,1,0:T(8,128)(2,1)S(1)}, u32[]{:S(2)}, u32[]{:S(2)}) %collective-permute-start.22) | collective-permute-done | bytes 131104 | tf_op jit(solution)/shard_map/ppermute | solution.py:26
  65.1 0.7 copy-done.10
  65.8 0.8 copy-done.2
  66.6 1.6 collective-permute-start.12
  68.1 18.3 %collective-permute-done.24.refs_6_ = bf16[2,13,80,128]{3,2,1,0:T(8,128)(2,1)S(1)} collective-permute-done((bf16[2,13,80,128]{3,2,1,0:T(8,128)(2,1)S(1)}, bf16[2,13,80,128]{3,2,1,0:T(8,128)(2,1)S(1)}, u32[]{:S(2)}, u32[]{:S(2)}) %collective-permute-start.24) | collective-permute-done | bytes 532512 | tf_op jit(solution)/shard_map/ppermute | solution.py:26
  86.4 0.8 copy-done.4
  87.3 0.9 collective-permute-start.25
  88.2 2.4 %plan.1 = (s32[25]{0:T(128)}, f32[25]{0:T(128)}, s32[65]{0:T(128)}) custom-call(s32[8,13]{1,0:T(8,128)} %bitcast.23, s32[17]{0:T(128)} %get-tuple-element.67.left_rank, s32[17]{0:T(128)} %get-tuple-element.68.right_rank, f32[8]{0:T(128)} %subduction.1), custom_call_target="tpu_custom_call" | custom-call | tf_op jit(solution)/shard_map/plan/pallas_call | solution.py:123
  90.7 2.2 %slab.7 = bf16[13,128,256]{2,1,0:T(8,128)(2,1)S(1)} custom-call(s32[17]{0:T(128)S(1)} %get-tuple-element.77.refs_0_, bf16[16,128,1024]{2,1,0:T(8,128)(2,1)} %bitcast.17), custom_call_target="tpu_custom_call" | custom-call | bytes 1703936 | tf_op jit(solution)/shard_map/slab/pallas_call | solution.py:209
  92.9 1.5 pick.3
  94.5 2.0 %combine.4.refs_0_ = bf16[128,4096]{1,0:T(8,128)(2,1)S(1)} custom-call(s32[25]{0:T(128)S(1)} %copy-done.12, f32[25]{0:T(128)S(1)} %copy-done.13, s32[65]{0:T(128)S(1)} %copy-done.14, s32[1]{0:T(128)} %get-tuple-element.66.refs_3_.more, bf16[2,13,16,128]{3,2,1,0:T(8,128)(2,1)S(1)} %get-tuple-element.95.refs_4_, ...), custom_call_target="tpu_custom_call" | custom-call | flops 2097152 | bytes 1572864 | tf_op jit(solution)/shard_map/combine/pallas_call | solution.py:380
  96.5 6.9 %collective-permute-done.25.refs_7_ = bf16[2,13,80,128]{3,2,1,0:T(8,128)(2,1)} collective-permute-done((bf16[2,13,80,128]{3,2,1,0:T(8,128)(2,1)}, bf16[2,13,80,128]{3,2,1,0:T(8,128)(2,1)}, u32[]{:S(2)}, u32[]{:S(2)}) %collective-permute-start.25) | collective-permute-done | bytes 532512 | tf_op jit(solution)/shard_map/ppermute | solution.py:26
  103.4 4.6 %combine.5.refs_1_ = bf16[640,4096]{1,0:T(8,128)(2,1)S(1)} custom-call(s32[25]{0:T(128)S(1)} %copy-done.12, f32[25]{0:T(128)S(1)} %copy-done.13, s32[65]{0:T(128)S(1)} %copy-done.14, s32[1]{0:T(128)} %get-tuple-element.66.refs_3_.more, bf16[2,13,80,128]{3,2,1,0:T(8,128)(2,1)S(1)} %copy-done.1, bf16[2,13,80,128]{3,2,1,0:T(8,128)(2,1)S(1)} %copy-done.3, ...), custom_call_target="tpu_custom_call" | custom-call | flops 10485760 | bytes 7864320 | tf_op jit(solution)/shard_map/combine/pallas_call | solution.py:380
  108.0 1.6 collective-permute-start.16
  109.7 2.2 %pick.2 = (bf16[1,13,128,256]{3,2,1,0:T(8,128)(2,1)S(1)}, bf16[1,13,128,256]{3,2,1,0:T(8,128)(2,1)S(1)}) custom-call(s32[17]{0:T(128)S(1)} %copy-done.15, bf16[1,16,128,256]{3,2,1,0:T(8,128)(2,1)} %bitcast.5.refs_0_, bf16[1,16,128,256]{3,2,1,0:T(8,128)(2,1)} %bitcast.6.refs_1_), custom_call_target="tpu_custom_call" | custom-call | bytes 4194304 | tf_op jit(solution)/shard_map/pick/pallas_call | solution.py:245
  111.9 6.2 %product.5 = (bf16[2,2,96,768]{3,2,1,0:T(8,128)(2,1)S(1)}, f32[2,2,96,768]{3,2,1,0:T(8,128)S(1)}) custom-call(s32[1]{0:T(128)} %get-tuple-element.66.refs_3_.more, bf16[128,4096]{1,0:T(8,128)(2,1)S(1)} %combine.4.refs_0_, bf16[640,4096]{1,0:T(8,128)(2,1)S(1)} %combine.5.refs_1_, bf16[13,128,256]{2,1,0:T(8,128)(2,1)S(1)} %bitcast.10, ...), custom_call_target="tpu_custom_call" | custom-call | flops 4831838208 | bytes 12582912 | tf_op jit(solution)/shard_map/product/pallas_call | solution.py:455
  118.1 7.9 %collective-permute-start.28 = (bf16[2,2,96,768]{3,2,1,0:T(8,128)(2,1)S(1)}, bf16[2,2,96,768]{3,2,1,0:T(8,128)(2,1)S(1)}, u32[]{:S(2)}, u32[]{:S(2)}) collective-permute-start(bf16[2,2,96,768]{3,2,1,0:T(8,128)(2,1)S(1)} %get-tuple-element.108), channel_id=1, source_target_pairs={{0,2},{1,3},{2,0},{3,1},{4,6},{5,7},{6,4},{7,5},{8,10},{9,11},{10,... | collective-permute-start | bytes 1769480 | tf_op jit(solution)/shard_map/ppermute | solution.py:26
  126.1 2.1 %pack.5 = (bf16[2,13,32,128]{3,2,1,0:T(8,128)(2,1)S(1)}, bf16[2,13,32,128]{3,2,1,0:T(8,128)(2,1)S(1)}, bf16[2,13,32,128]{3,2,1,0:T(8,128)(2,1)S(1)}, bf16[2,13,32,128]{3,2,1,0:T(8,128)(2,1)S(1)}) custom-call(s32[17]{0:T(128)S(1)} %get-tuple-element.72.refs_0_.order, s32[1]{0:T(128)} %bitcast.2.refs_1_.refs_0_, bf16[16,128,1024]{2,1,0:T(8,128)(2,1)S(1)} %bitcast.20), custom_call_target="tpu_custom_call" | custom-call | bytes 1703936 | tf_op jit(solution)/shard_map/pack/pallas_call | solution.py:174
  128.2 0.1 collective-permute-start.5
  128.3 3.2 %collective-permute-start.6 = (bf16[2,13,32,128]{3,2,1,0:T(8,128)(2,1)S(1)}, bf16[2,13,32,128]{3,2,1,0:T(8,128)(2,1)S(1)}, u32[]{:S(2)}, u32[]{:S(2)}) collective-permute-start(bf16[2,13,32,128]{3,2,1,0:T(8,128)(2,1)S(1)} %get-tuple-element.75), channel_id=1, source_target_pairs={{0,4},{1,5},{2,6},{3,7},{4,0},{5,1},{6,2},{7,3},{8,12},{9,13},{10,... | collective-permute-start | bytes 638984 | tf_op jit(solution)/shard_map/ppermute | solution.py:26
  131.4 17.3 %collective-permute-done.5.refs_5_ = bf16[2,13,32,128]{3,2,1,0:T(8,128)(2,1)S(1)} collective-permute-done((bf16[2,13,32,128]{3,2,1,0:T(8,128)(2,1)S(1)}, bf16[2,13,32,128]{3,2,1,0:T(8,128)(2,1)S(1)}, u32[]{:S(2)}, u32[]{:S(2)}) %collective-permute-start.5) | collective-permute-done | bytes 213024 | tf_op jit(solution)/shard_map/ppermute | solution.py:26
  148.7 2.6 %collective-permute-start.7 = (bf16[2,13,32,128]{3,2,1,0:T(8,128)(2,1)S(1)}, bf16[2,13,32,128]{3,2,1,0:T(8,128)(2,1)S(1)}, u32[]{:S(2)}, u32[]{:S(2)}) collective-permute-start(bf16[2,13,32,128]{3,2,1,0:T(8,128)(2,1)S(1)} %get-tuple-element.76), channel_id=1, source_target_pairs={{0,6},{1,7},{2,4},{3,5},{4,2},{5,3},{6,0},{7,1},{8,14},{9,15},{10,... | collective-permute-start | bytes 638984 | tf_op jit(solution)/shard_map/ppermute | solution.py:26
  151.4 5.9 %collective-permute-done.7.refs_7_ = bf16[2,13,32,128]{3,2,1,0:T(8,128)(2,1)S(1)} collective-permute-done((bf16[2,13,32,128]{3,2,1,0:T(8,128)(2,1)S(1)}, bf16[2,13,32,128]{3,2,1,0:T(8,128)(2,1)S(1)}, u32[]{:S(2)}, u32[]{:S(2)}) %collective-permute-start.7) | collective-permute-done | bytes 213024 | tf_op jit(solution)/shard_map/ppermute | solution.py:26
  157.3 2.3 %combine.3.refs_0_ = bf16[256,4096]{1,0:T(8,128)(2,1)S(1)} custom-call(s32[25]{0:T(128)S(1)} %copy-done.12, f32[25]{0:T(128)S(1)} %copy-done.13, s32[65]{0:T(128)S(1)} %copy-done.14, s32[1]{0:T(128)} %get-tuple-element.66.refs_3_.more, bf16[2,13,32,128]{3,2,1,0:T(8,128)(2,1)S(1)} %get-tuple-element.73.refs_4_, ...), custom_call_target="tpu_custom_call" | custom-call | flops 4194304 | bytes 3145728 | tf_op jit(solution)/shard_map/combine/pallas_call | solution.py:380
  159.7 2.5 %product.4 = (bf16[2,2,96,256]{3,2,1,0:T(8,128)(2,1)S(1)}, f32[2,2,96,256]{3,2,1,0:T(8,128)S(1)}) custom-call(s32[1]{0:T(128)} %get-tuple-element.66.refs_3_.more, bf16[128,4096]{1,0:T(8,128)(2,1)S(1)} %combine.4.refs_0_, bf16[640,4096]{1,0:T(8,128)(2,1)S(1)} %combine.5.refs_1_, bf16[13,128,256]{2,1,0:T(8,128)(2,1)S(1)} %collective-permute-done.14.refs_3_.refs_2_, ...), custom_call_target="tpu_custom_call" | custom-call | flops 1610612736 | bytes 8388608 | tf_op jit(solution)/shard_map/product/pallas_call | solution.py:455
  162.1 3.6 %collective-permute-start.26 = (bf16[2,2,96,256]{3,2,1,0:T(8,128)(2,1)S(1)}, bf16[2,2,96,256]{3,2,1,0:T(8,128)(2,1)S(1)}, u32[]{:S(2)}, u32[]{:S(2)}) collective-permute-start(bf16[2,2,96,256]{3,2,1,0:T(8,128)(2,1)S(1)} %get-tuple-element.104), channel_id=1, source_target_pairs={{0,2},{1,3},{2,0},{3,1},{4,6},{5,7},{6,4},{7,5},{8,10},{9,11},{10,... | collective-permute-start | bytes 589832 | tf_op jit(solution)/shard_map/ppermute | solution.py:26
  165.7 0.1 halve.3
  165.8 0.1 collective-permute-start.29
  165.9 3.9 %product.3 = (bf16[1,2,32,1024]{3,2,1,0:T(8,128)(2,1)S(1)}, bf16[1,2,32,1024]{3,2,1,0:T(8,128)(2,1)S(1)}, bf16[1,2,32,1024]{3,2,1,0:T(8,128)(2,1)S(1)}, f32[1,2,32,1024]{3,2,1,0:T(8,128)S(1)}) custom-call(s32[1]{0:T(128)} %get-tuple-element.66.refs_3_.more, bf16[256,4096]{1,0:T(8,128)(2,1)S(1)} %combine.3.refs_0_, bf16[13,128,256]{2,1,0:T(8,128)(2,1)S(1)} %bitcast.11, ...), custom_call_target="tpu_custom_call" | custom-call | flops 2147483648 | bytes 10485760 | tf_op jit(solution)/shard_map/product/pallas_call | solution.py:455
  169.8 2.4 %collective-permute-start.17 = (bf16[1,2,32,1024]{3,2,1,0:T(8,128)(2,1)S(1)}, bf16[1,2,32,1024]{3,2,1,0:T(8,128)(2,1)S(1)}, u32[]{:S(2)}, u32[]{:S(2)}) collective-permute-start(bf16[1,2,32,1024]{3,2,1,0:T(8,128)(2,1)S(1)} %get-tuple-element.88), channel_id=1, source_target_pairs={{0,6},{1,7},{2,4},{3,5},{4,2},{5,3},{6,0},{7,1},{8,14},{9,15},{10,... | collective-permute-start | bytes 393224 | tf_op jit(solution)/shard_map/ppermute | solution.py:26
  172.2 1.0 collective-permute-start.18
  173.2 1.0 collective-permute-start.19
  174.3 2.1 %collective-permute-start.27 = (bf16[1,2,96,256]{3,2,1,0:T(8,128)(2,1)S(1)}, bf16[1,2,96,256]{3,2,1,0:T(8,128)(2,1)S(1)}, u32[]{:S(2)}, u32[]{:S(2)}) collective-permute-start(bf16[1,2,96,256]{3,2,1,0:T(8,128)(2,1)S(1)} %get-tuple-element.106), channel_id=1, source_target_pairs={{0,4},{1,5},{2,6},{3,7},{4,0},{5,1},{6,2},{7,3},{8,12},{9,13},{10,... | collective-permute-start | bytes 294920 | tf_op jit(solution)/shard_map/ppermute | solution.py:26
  176.3 13.6 %collective-permute-done.29.refs_0_ = bf16[1,2,96,768]{3,2,1,0:T(8,128)(2,1)S(1)} collective-permute-done((bf16[1,2,96,768]{3,2,1,0:T(8,128)(2,1)S(1)}, bf16[1,2,96,768]{3,2,1,0:T(8,128)(2,1)S(1)}, u32[]{:S(2)}, u32[]{:S(2)}) %collective-permute-start.29) | collective-permute-done | bytes 294944 | tf_op jit(solution)/shard_map/ppermute | solution.py:26
  190.0 1.0 finish.3.refs_1_
  190.9 6.1 %collective-permute-done.27.refs_0_ = bf16[1,2,96,256]{3,2,1,0:T(8,128)(2,1)S(1)} collective-permute-done((bf16[1,2,96,256]{3,2,1,0:T(8,128)(2,1)S(1)}, bf16[1,2,96,256]{3,2,1,0:T(8,128)(2,1)S(1)}, u32[]{:S(2)}, u32[]{:S(2)}) %collective-permute-start.27) | collective-permute-done | bytes 98336 | tf_op jit(solution)/shard_map/ppermute | solution.py:26
  197.0 0.8 finish.4.refs_3_
  197.8 0.8 finish.5
  (56 shorter events, 0.3 us)
Async XLA Ops:
  2.0 13.7 %all-to-all-start = ((s32[8,1,13]{2,1,0:T(1,128)}), s32[8,1,13]{2,1,0:T(1,128)S(1)}, u32[]{:S(2)}, u32[]{:S(2)}) async-start(s32[8,1,13]{2,1,0:T(1,128)} %broadcast_in_dim.11), calls=%async_computation | async-start | bytes 8192 | tf_op jit(solution)/shard_map/all_to_all | solution.py:548
  15.7 0.6 copy-start.20
  18.1 7.2 %collective-permute-start.10 = (s32[8,13]{1,0:T(8,128)}, s32[8,13]{1,0:T(8,128)S(1)}, u32[]{:S(2)}, u32[]{:S(2)}) collective-permute-start(s32[8,13]{1,0:T(8,128)} %bitcast.22), channel_id=1, source_target_pairs={{0,8},{8,0},{16,24},{24,16},{1,9},{9,1},{17,25},{25,17},{2,10},{10... | collective-permute-start | bytes 1256 | tf_op jit(solution)/shard_map/ppermute | solution.py:26
  18.1 1.5 collective-permute-start.8
  20.9 3.7 %collective-permute-start.9 = (s32[1]{0:T(128)}, s32[1]{0:T(128)}, u32[]{:S(2)}, u32[]{:S(2)}) collective-permute-start(s32[1]{0:T(128)} %max.6), channel_id=1, source_target_pairs={{0,16},{8,24},{16,0},{24,8},{1,17},{9,25},{17,1},{25,9},{2,18},{10... | collective-permute-start | bytes 20 | tf_op jit(solution)/shard_map/ppermute | solution.py:26
  25.3 0.6 copy-start.21
  31.0 6.0 %copy-start.16 = (bf16[1,16,128,1024]{3,2,1,0:T(8,128)(2,1)S(1)}, bf16[1,16,128,1024]{3,2,1,0:T(8,128)(2,1)}, u32[]{:S(2)}) copy-start(bf16[1,16,128,1024]{3,2,1,0:T(8,128)(2,1)} %param.9) | copy-start | bytes 12582916
  31.1 80.8 %collective-permute-start.13 = (bf16[13,128,512]{2,1,0:T(8,128)(2,1)}, bf16[13,128,512]{2,1,0:T(8,128)(2,1)S(1)}, u32[]{:S(2)}, u32[]{:S(2)}) collective-permute-start(bf16[13,128,512]{2,1,0:T(8,128)(2,1)} %slab.6), channel_id=1, source_target_pairs={{0,8},{8,0},{16,24},{24,16},{1,9},{9,1},{17,25},{25,17},{2,10},{10... | collective-permute-start | bytes 5111816 | tf_op jit(solution)/shard_map/ppermute | solution.py:26
  31.1 80.7 %collective-permute-start.15 = (bf16[13,128,512]{2,1,0:T(8,128)(2,1)}, bf16[13,128,512]{2,1,0:T(8,128)(2,1)S(1)}, u32[]{:S(2)}, u32[]{:S(2)}) collective-permute-start(bf16[13,128,512]{2,1,0:T(8,128)(2,1)} %slab.6), channel_id=1, source_target_pairs={{0,9},{1,8},{2,11},{3,10},{4,13},{5,12},{6,15},{7,14},{8,1},{9,0},... | collective-permute-start | bytes 5111816 | tf_op jit(solution)/shard_map/ppermute | solution.py:26
  35.7 0.8 copy-start
  36.5 29.2 %collective-permute-start.23 = (bf16[2,13,80,128]{3,2,1,0:T(8,128)(2,1)S(1)}, bf16[2,13,80,128]{3,2,1,0:T(8,128)(2,1)S(1)}, u32[]{:S(2)}, u32[]{:S(2)}) collective-permute-start(bf16[2,13,80,128]{3,2,1,0:T(8,128)(2,1)S(1)} %get-tuple-element.100), channel_id=1, source_target_pairs={{0,2},{1,3},{2,0},{3,1},{4,6},{5,7},{6,4},{7,5},{8,10},{9,11},{10,... | collective-permute-start | bytes 1597448 | tf_op jit(solution)/shard_map/ppermute | solution.py:26
  38.4 17.8 %collective-permute-start.20 = (bf16[2,16,16,128]{3,2,1,0:T(8,128)(2,1)S(1)}, bf16[2,16,16,128]{3,2,1,0:T(8,128)(2,1)S(1)}, u32[]{:S(2)}, u32[]{:S(2)}) collective-permute-start(bf16[2,16,16,128]{3,2,1,0:T(8,128)(2,1)S(1)} %get-tuple-element.92), channel_id=1, source_target_pairs={{0,2},{1,3},{2,0},{3,1},{4,6},{5,7},{6,4},{7,5},{8,10},{9,11},{10,... | collective-permute-start | bytes 393224 | tf_op jit(solution)/shard_map/ppermute | solution.py:26
  39.9 17.5 %collective-permute-start.21 = (bf16[2,16,16,128]{3,2,1,0:T(8,128)(2,1)S(1)}, bf16[2,16,16,128]{3,2,1,0:T(8,128)(2,1)S(1)}, u32[]{:S(2)}, u32[]{:S(2)}) collective-permute-start(bf16[2,16,16,128]{3,2,1,0:T(8,128)(2,1)S(1)} %get-tuple-element.93), channel_id=1, source_target_pairs={{0,4},{1,5},{2,6},{3,7},{4,0},{5,1},{6,2},{7,3},{8,12},{9,13},{10,... | collective-permute-start | bytes 393224 | tf_op jit(solution)/shard_map/ppermute | solution.py:26
  56.2 0.7 copy-start.6
  56.9 8.2 %collective-permute-start.22 = (bf16[2,16,16,128]{3,2,1,0:T(8,128)(2,1)S(1)}, bf16[2,16,16,128]{3,2,1,0:T(8,128)(2,1)S(1)}, u32[]{:S(2)}, u32[]{:S(2)}) collective-permute-start(bf16[2,16,16,128]{3,2,1,0:T(8,128)(2,1)S(1)} %get-tuple-element.94), channel_id=1, source_target_pairs={{0,6},{1,7},{2,4},{3,5},{4,2},{5,3},{6,0},{7,1},{8,14},{9,15},{10,... | collective-permute-start | bytes 393224 | tf_op jit(solution)/shard_map/ppermute | solution.py:26
  57.5 0.7 copy-start.8
  58.1 28.3 %collective-permute-start.24 = (bf16[2,13,80,128]{3,2,1,0:T(8,128)(2,1)S(1)}, bf16[2,13,80,128]{3,2,1,0:T(8,128)(2,1)S(1)}, u32[]{:S(2)}, u32[]{:S(2)}) collective-permute-start(bf16[2,13,80,128]{3,2,1,0:T(8,128)(2,1)S(1)} %get-tuple-element.101), channel_id=1, source_target_pairs={{0,4},{1,5},{2,6},{3,7},{4,0},{5,1},{6,2},{7,3},{8,12},{9,13},{10,... | collective-permute-start | bytes 1597448 | tf_op jit(solution)/shard_map/ppermute | solution.py:26
  65.1 0.7 copy-start.10
  65.7 42.3 %collective-permute-start.11 = (bf16[16,128,256]{2,1,0:T(8,128)(2,1)}, bf16[16,128,256]{2,1,0:T(8,128)(2,1)}, u32[]{:S(2)}, u32[]{:S(2)}) collective-permute-start(bf16[16,128,256]{2,1,0:T(8,128)(2,1)} %slab.5), channel_id=1, source_target_pairs={{0,8},{8,0},{16,24},{24,16},{1,9},{9,1},{17,25},{25,17},{2,10},{10... | collective-permute-start | bytes 3145736 | tf_op jit(solution)/shard_map/ppermute | solution.py:26
  65.7 0.8 copy-start.2
  66.6 43.1 %collective-permute-start.12 = (bf16[16,128,256]{2,1,0:T(8,128)(2,1)}, bf16[16,128,256]{2,1,0:T(8,128)(2,1)}, u32[]{:S(2)}, u32[]{:S(2)}) collective-permute-start(bf16[16,128,256]{2,1,0:T(8,128)(2,1)} %slab.5), channel_id=1, source_target_pairs={{0,9},{1,8},{2,11},{3,10},{4,13},{5,12},{6,15},{7,14},{8,1},{9,0},... | collective-permute-start | bytes 3145736 | tf_op jit(solution)/shard_map/ppermute | solution.py:26
  86.4 0.8 copy-start.4
  87.3 16.1 %collective-permute-start.25 = (bf16[2,13,80,128]{3,2,1,0:T(8,128)(2,1)}, bf16[2,13,80,128]{3,2,1,0:T(8,128)(2,1)}, u32[]{:S(2)}, u32[]{:S(2)}) collective-permute-start(bf16[2,13,80,128]{3,2,1,0:T(8,128)(2,1)} %get-tuple-element.102), channel_id=1, source_target_pairs={{0,6},{1,7},{2,4},{3,5},{4,2},{5,3},{6,0},{7,1},{8,14},{9,15},{10,... | collective-permute-start | bytes 1597448 | tf_op jit(solution)/shard_map/ppermute | solution.py:26
  90.6 2.3 %copy-start.7 = (bf16[2,16,16,128]{3,2,1,0:T(8,128)(2,1)S(1)}, bf16[2,16,16,128]{3,2,1,0:T(8,128)(2,1)}, u32[]{:S(2)}) copy-start(bf16[2,16,16,128]{3,2,1,0:T(8,128)(2,1)} %copy-done.6) | copy-start | bytes 393220
  90.6 2.3 %copy-start.9 = (bf16[2,16,16,128]{3,2,1,0:T(8,128)(2,1)S(1)}, bf16[2,16,16,128]{3,2,1,0:T(8,128)(2,1)}, u32[]{:S(2)}) copy-start(bf16[2,16,16,128]{3,2,1,0:T(8,128)(2,1)} %copy-done.8) | copy-start | bytes 393220
  90.6 2.3 %copy-start.11 = (bf16[2,16,16,128]{3,2,1,0:T(8,128)(2,1)S(1)}, bf16[2,16,16,128]{3,2,1,0:T(8,128)(2,1)}, u32[]{:S(2)}) copy-start(bf16[2,16,16,128]{3,2,1,0:T(8,128)(2,1)} %copy-done.10) | copy-start | bytes 393220
  90.6 3.8 %copy-start.12 = (s32[25]{0:T(128)S(1)}, s32[25]{0:T(128)}, u32[]{:S(2)}) copy-start(s32[25]{0:T(128)} %get-tuple-element.69.refs_0_) | copy-start | bytes 304
  90.6 3.8 %copy-start.13 = (f32[25]{0:T(128)S(1)}, f32[25]{0:T(128)}, u32[]{:S(2)}) copy-start(f32[25]{0:T(128)} %get-tuple-element.70.refs_1_) | copy-start | bytes 304
  90.7 3.8 %copy-start.14 = (s32[65]{0:T(128)S(1)}, s32[65]{0:T(128)}, u32[]{:S(2)}) copy-start(s32[65]{0:T(128)} %get-tuple-element.71.refs_2_) | copy-start | bytes 784
  90.7 3.8 %copy-start.19 = (bf16[2,3,128,128]{3,2,1,0:T(8,128)(2,1)S(1)}, bf16[2,3,128,128]{3,2,1,0:T(8,128)(2,1)}, u32[]{:S(2)}) copy-start(bf16[2,3,128,128]{3,2,1,0:T(8,128)(2,1)} %get-tuple-element.78.refs_8_) | copy-start | bytes 589828
  92.9 10.5 %copy-start.1 = (bf16[2,13,80,128]{3,2,1,0:T(8,128)(2,1)S(1)}, bf16[2,13,80,128]{3,2,1,0:T(8,128)(2,1)}, u32[]{:S(2)}) copy-start(bf16[2,13,80,128]{3,2,1,0:T(8,128)(2,1)} %copy-done) | copy-start | bytes 1597444
  92.9 10.5 %copy-start.3 = (bf16[2,13,80,128]{3,2,1,0:T(8,128)(2,1)S(1)}, bf16[2,13,80,128]{3,2,1,0:T(8,128)(2,1)}, u32[]{:S(2)}) copy-start(bf16[2,13,80,128]{3,2,1,0:T(8,128)(2,1)} %copy-done.2) | copy-start | bytes 1597444
  92.9 10.5 %copy-start.5 = (bf16[2,13,80,128]{3,2,1,0:T(8,128)(2,1)S(1)}, bf16[2,13,80,128]{3,2,1,0:T(8,128)(2,1)}, u32[]{:S(2)}) copy-start(bf16[2,13,80,128]{3,2,1,0:T(8,128)(2,1)} %copy-done.4) | copy-start | bytes 1597444
  103.3 56.3 %collective-permute-start.14 = (bf16[13,128,256]{2,1,0:T(8,128)(2,1)S(1)}, bf16[13,128,256]{2,1,0:T(8,128)(2,1)S(1)}, u32[]{:S(2)}, u32[]{:S(2)}) collective-permute-start(bf16[13,128,256]{2,1,0:T(8,128)(2,1)S(1)} %slab.7), channel_id=1, source_target_pairs={{0,8},{8,0},{16,24},{24,16},{1,9},{9,1},{17,25},{25,17},{2,10},{10... | collective-permute-start | bytes 2555912 | tf_op jit(solution)/shard_map/ppermute | solution.py:26
  103.4 6.3 %copy-start.15 = (s32[17]{0:T(128)S(1)}, s32[17]{0:T(128)}, u32[]{:S(2)}) copy-start(s32[17]{0:T(128)} %get-tuple-element.82.order) | copy-start | bytes 208
  108.0 51.6 %collective-permute-start.16 = (bf16[13,128,256]{2,1,0:T(8,128)(2,1)S(1)}, bf16[13,128,256]{2,1,0:T(8,128)(2,1)S(1)}, u32[]{:S(2)}, u32[]{:S(2)}) collective-permute-start(bf16[13,128,256]{2,1,0:T(8,128)(2,1)S(1)} %slab.7), channel_id=1, source_target_pairs={{0,9},{1,8},{2,11},{3,10},{4,13},{5,12},{6,15},{7,14},{8,1},{9,0},... | collective-permute-start | bytes 2555912 | tf_op jit(solution)/shard_map/ppermute | solution.py:26
  111.9 14.2 %copy-start.17 = (bf16[1,16,128,1024]{3,2,1,0:T(8,128)(2,1)S(1)}, bf16[1,16,128,1024]{3,2,1,0:T(8,128)(2,1)}, u32[]{:S(2)}) copy-start(bf16[1,16,128,1024]{3,2,1,0:T(8,128)(2,1)} %param.9) | copy-start | bytes 12582916
  118.1 47.6 %collective-permute-start.28 = (bf16[2,2,96,768]{3,2,1,0:T(8,128)(2,1)S(1)}, bf16[2,2,96,768]{3,2,1,0:T(8,128)(2,1)S(1)}, u32[]{:S(2)}, u32[]{:S(2)}) collective-permute-start(bf16[2,2,96,768]{3,2,1,0:T(8,128)(2,1)S(1)} %get-tuple-element.108), channel_id=1, source_target_pairs={{0,2},{1,3},{2,0},{3,1},{4,6},{5,7},{6,4},{7,5},{8,10},{9,11},{10,... | collective-permute-start | bytes 1769480 | tf_op jit(solution)/shard_map/ppermute | solution.py:26
  128.2 20.6 %collective-permute-start.5 = (bf16[2,13,32,128]{3,2,1,0:T(8,128)(2,1)S(1)}, bf16[2,13,32,128]{3,2,1,0:T(8,128)(2,1)S(1)}, u32[]{:S(2)}, u32[]{:S(2)}) collective-permute-start(bf16[2,13,32,128]{3,2,1,0:T(8,128)(2,1)S(1)} %get-tuple-element.74), channel_id=1, source_target_pairs={{0,2},{1,3},{2,0},{3,1},{4,6},{5,7},{6,4},{7,5},{8,10},{9,11},{10,... | collective-permute-start | bytes 638984 | tf_op jit(solution)/shard_map/ppermute | solution.py:26
  128.3 23.1 %collective-permute-start.6 = (bf16[2,13,32,128]{3,2,1,0:T(8,128)(2,1)S(1)}, bf16[2,13,32,128]{3,2,1,0:T(8,128)(2,1)S(1)}, u32[]{:S(2)}, u32[]{:S(2)}) collective-permute-start(bf16[2,13,32,128]{3,2,1,0:T(8,128)(2,1)S(1)} %get-tuple-element.75), channel_id=1, source_target_pairs={{0,4},{1,5},{2,6},{3,7},{4,0},{5,1},{6,2},{7,3},{8,12},{9,13},{10,... | collective-permute-start | bytes 638984 | tf_op jit(solution)/shard_map/ppermute | solution.py:26
  148.7 8.6 %collective-permute-start.7 = (bf16[2,13,32,128]{3,2,1,0:T(8,128)(2,1)S(1)}, bf16[2,13,32,128]{3,2,1,0:T(8,128)(2,1)S(1)}, u32[]{:S(2)}, u32[]{:S(2)}) collective-permute-start(bf16[2,13,32,128]{3,2,1,0:T(8,128)(2,1)S(1)} %get-tuple-element.76), channel_id=1, source_target_pairs={{0,6},{1,7},{2,4},{3,5},{4,2},{5,3},{6,0},{7,1},{8,14},{9,15},{10,... | collective-permute-start | bytes 638984 | tf_op jit(solution)/shard_map/ppermute | solution.py:26
  162.1 12.1 %collective-permute-start.26 = (bf16[2,2,96,256]{3,2,1,0:T(8,128)(2,1)S(1)}, bf16[2,2,96,256]{3,2,1,0:T(8,128)(2,1)S(1)}, u32[]{:S(2)}, u32[]{:S(2)}) collective-permute-start(bf16[2,2,96,256]{3,2,1,0:T(8,128)(2,1)S(1)} %get-tuple-element.104), channel_id=1, source_target_pairs={{0,2},{1,3},{2,0},{3,1},{4,6},{5,7},{6,4},{7,5},{8,10},{9,11},{10,... | collective-permute-start | bytes 589832 | tf_op jit(solution)/shard_map/ppermute | solution.py:26
  165.8 24.2 %collective-permute-start.29 = (bf16[1,2,96,768]{3,2,1,0:T(8,128)(2,1)S(1)}, bf16[1,2,96,768]{3,2,1,0:T(8,128)(2,1)S(1)}, u32[]{:S(2)}, u32[]{:S(2)}) collective-permute-start(bf16[1,2,96,768]{3,2,1,0:T(8,128)(2,1)S(1)} %get-tuple-element.110), channel_id=1, source_target_pairs={{0,4},{1,5},{2,6},{3,7},{4,0},{5,1},{6,2},{7,3},{8,12},{9,13},{10,... | collective-permute-start | bytes 884744 | tf_op jit(solution)/shard_map/ppermute | solution.py:26
  169.8 28.0 %collective-permute-start.17 = (bf16[1,2,32,1024]{3,2,1,0:T(8,128)(2,1)S(1)}, bf16[1,2,32,1024]{3,2,1,0:T(8,128)(2,1)S(1)}, u32[]{:S(2)}, u32[]{:S(2)}) collective-permute-start(bf16[1,2,32,1024]{3,2,1,0:T(8,128)(2,1)S(1)} %get-tuple-element.88), channel_id=1, source_target_pairs={{0,6},{1,7},{2,4},{3,5},{4,2},{5,3},{6,0},{7,1},{8,14},{9,15},{10,... | collective-permute-start | bytes 393224 | tf_op jit(solution)/shard_map/ppermute | solution.py:26
  172.2 25.6 %collective-permute-start.18 = (bf16[1,2,32,1024]{3,2,1,0:T(8,128)(2,1)S(1)}, bf16[1,2,32,1024]{3,2,1,0:T(8,128)(2,1)S(1)}, u32[]{:S(2)}, u32[]{:S(2)}) collective-permute-start(bf16[1,2,32,1024]{3,2,1,0:T(8,128)(2,1)S(1)} %get-tuple-element.89), channel_id=1, source_target_pairs={{0,4},{1,5},{2,6},{3,7},{4,0},{5,1},{6,2},{7,3},{8,12},{9,13},{10,... | collective-permute-start | bytes 393224 | tf_op jit(solution)/shard_map/ppermute | solution.py:26
  173.2 24.6 %collective-permute-start.19 = (bf16[1,2,32,1024]{3,2,1,0:T(8,128)(2,1)S(1)}, bf16[1,2,32,1024]{3,2,1,0:T(8,128)(2,1)S(1)}, u32[]{:S(2)}, u32[]{:S(2)}) collective-permute-start(bf16[1,2,32,1024]{3,2,1,0:T(8,128)(2,1)S(1)} %get-tuple-element.90), channel_id=1, source_target_pairs={{0,2},{1,3},{2,0},{3,1},{4,6},{5,7},{6,4},{7,5},{8,10},{9,11},{10,... | collective-permute-start | bytes 393224 | tf_op jit(solution)/shard_map/ppermute | solution.py:26
  174.3 22.8 %collective-permute-start.27 = (bf16[1,2,96,256]{3,2,1,0:T(8,128)(2,1)S(1)}, bf16[1,2,96,256]{3,2,1,0:T(8,128)(2,1)S(1)}, u32[]{:S(2)}, u32[]{:S(2)}) collective-permute-start(bf16[1,2,96,256]{3,2,1,0:T(8,128)(2,1)S(1)} %get-tuple-element.106), channel_id=1, source_target_pairs={{0,4},{1,5},{2,6},{3,7},{4,0},{5,1},{6,2},{7,3},{8,12},{9,13},{10,... | collective-permute-start | bytes 294920 | tf_op jit(solution)/shard_map/ppermute | solution.py:26
